TPU v7x, 32 devices: a whole 2x2x4 slice. The times are simulated.
32 devices in a mesh: shard: 4 (over y, x), ctx: 4 (over z), tp: 2 (over core).
Axes of the slice: x: 2, y: 2, z: 4, core: 2. Of those that a mesh axis runs over, the one named last changes fastest.
Arguments:
- inputs: bfloat16 [4, 512, 1024], P('shard', 'ctx'), may hold values from -6 to 6
- cotangent: bfloat16 [4, 512, 1024], P('shard', 'ctx'), may hold values from -6 to 6
- mixer_matrix: float32 [1024, 4, 1024], P(('shard', 'ctx', 'tp')), may hold values from -0.1875 to 0.1875
- ffn_weight: float32 [4608, 3, 1024], P(('shard', 'ctx', 'tp')), may hold values from -0.1875 to 0.1875
- conv_weight: float32 [3, 1024], replicated, may hold values from -3.5 to 3.5
- norm_gains: float32 [2, 1024], replicated, may hold values from 0.5 to 1.5
- mixer_first: float32 [1024, 4, 1024], P(('shard', 'ctx', 'tp')), as said below
- mixer_second: float32 [1024, 4, 1024], P(('shard', 'ctx', 'tp')), as said below
- ffn_first: float32 [4608, 3, 1024], P(('shard', 'ctx', 'tp')), as said below
- ffn_second: float32 [4608, 3, 1024], P(('shard', 'ctx', 'tp')), as said below
- conv_first: float32 [3, 1024], replicated, as said below
- conv_second: float32 [3, 1024], replicated, as said below
- gain_first: float32 [2, 1024], replicated, as said below
- gain_second: float32 [2, 1024], replicated, as said below
Outputs:
- output: bfloat16 [4, 512, 1024], P('shard', 'ctx')
- input_grad: float32 [4, 512, 1024], P('shard', 'ctx')
- mixer_grad: float32 [1024, 4, 1024], P(('shard', 'ctx', 'tp'))
- ffn_grad: float32 [4608, 3, 1024], P(('shard', 'ctx', 'tp'))
- conv_grad: float32 [3, 1024], replicated
- gain_grad: float32 [2, 1024], replicated
- mixer_new: float32 [1024, 4, 1024], P(('shard', 'ctx', 'tp'))
- ffn_new: float32 [4608, 3, 1024], P(('shard', 'ctx', 'tp'))
- conv_new: float32 [3, 1024], replicated
- gain_new: float32 [2, 1024], replicated
- mixer_first_new: float32 [1024, 4, 1024], P(('shard', 'ctx', 'tp'))
- mixer_second_new: float32 [1024, 4, 1024], P(('shard', 'ctx', 'tp'))
- ffn_first_new: float32 [4608, 3, 1024], P(('shard', 'ctx', 'tp'))
- ffn_second_new: float32 [4608, 3, 1024], P(('shard', 'ctx', 'tp'))
- conv_first_new: float32 [3, 1024], replicated
- conv_second_new: float32 [3, 1024], replicated
- gain_first_new: float32 [2, 1024], replicated
- gain_second_new: float32 [2, 1024], replicated
Inputs may be any that keep to these rules, and one draw needn't show every extreme that they name: `mixer_first`: a running mean of earlier gradients. `mixer_second`: a running mean of squared earlier gradients. `ffn_first`: a running mean of earlier gradients. `ffn_second`: a running mean of squared earlier gradients. `conv_first`: a running mean of earlier gradients. `conv_second`: a running mean of squared earlier gradients. `gain_first`: a running mean of earlier gradients. `gain_second`: a running mean of squared earlier gradients.
All inputs are finite; a program needn't handle non-finite values.
Results may differ from a plain program's by a relative error of at most 0.009.
The roundings to bfloat16 on the way count: a program that leaves them out, or rounds other values in their place, can miss the bound.
Values may be sent and summed in bfloat16 or wider, within the bound.
No kernel may reach another device: no remote copies, remote signals or barrier semaphores. Data moves between devices by JAX's collectives and lax.ppermute only.
A program may use at most 192 MiB of HBM per device.

v0:
```python
import functools

import jax
import jax.numpy as jnp
from jax import lax
from jax.experimental import pallas as pl
from jax.experimental.pallas import tpu as pltpu
from jax.sharding import PartitionSpec as P


STEP = 10


norm_eps = 1e-05
beta_first = 0.9
beta_second = 0.999
adam_eps = 1e-08
matrix_rate = 0.02
small_rate = 0.25
decay_rate = 0.1

bf16 = jnp.bfloat16
f32 = jnp.float32


def norm_backward(grad_normed, normed, scale):
    return scale * (grad_normed - normed * jnp.mean(grad_normed * normed, axis=-1, keepdims=True))


def adam_update(weight, gradient, first, second, rate, decay):
    first_new = beta_first * first + (1.0 - beta_first) * gradient
    second_new = beta_second * second + (1.0 - beta_second) * gradient * gradient
    first_hat = first_new / (1.0 - beta_first**STEP)
    second_hat = second_new / (1.0 - beta_second**STEP)
    weight_new = weight - rate * (first_hat / (jnp.sqrt(second_hat) + adam_eps) + decay * weight)
    return (weight_new, first_new, second_new)


def partner_of(index, step, count):
    assert count & (count - 1) == 0
    return index ^ step


def swap_with(value, axis, step):
    count = lax.axis_size(axis)
    return lax.ppermute(
        value, axis, [(i, partner_of(i, step, count)) for i in range(count)]
    )


def send_up(value, axis, steps):
    count = lax.axis_size(axis)
    return lax.ppermute(value, axis, [(i, (i + steps) % count) for i in range(count)])


def tree_sum(values):
    while len(values) > 1:
        values = [a + b for a, b in zip(values[::2], values[1::2])]
    return values[0]


def sum_over(value, axis):
    count = lax.axis_size(axis)
    return tree_sum([value] + [swap_with(value, axis, k) for k in range(1, count)])


def spread_rows(own):
    count = lax.axis_size("ctx")
    mine = [own] + [send_up(own, "ctx", -k) for k in range(1, count)]
    return mine + [swap_with(piece, "tp", 1) for piece in mine]


def in_vmem(body, outs, *operands, scalars=None, scratch=(), flops=0):
    specs = [pl.BlockSpec(memory_space=pltpu.VMEM)] * len(operands)
    if scalars is not None:
        specs = [pl.BlockSpec(memory_space=pltpu.SMEM)] + specs
        operands = (scalars, *operands)
    shapes = [jax.ShapeDtypeStruct(shape, dtype) for shape, dtype in outs]
    moved = sum(x.size * x.dtype.itemsize for x in (*operands, *shapes))
    return pl.pallas_call(
        body,
        out_shape=shapes,
        in_specs=specs,
        out_specs=[pl.BlockSpec(memory_space=pltpu.VMEM)] * len(shapes),
        scratch_shapes=list(scratch),
        compiler_params=pltpu.CompilerParams(vmem_limit_bytes=48 << 20),
        cost_estimate=pl.CostEstimate(flops=flops, bytes_accessed=moved, transcendentals=0),
    )(*operands)


def by_rows(rows, weight):
    return lax.dot_general(rows, weight, (((1,), (1,)), ((), ())), preferred_element_type=f32)


def down_rows(left, right):
    return lax.dot_general(left, right, (((0,), (0,)), ((), ())), preferred_element_type=f32)


def block_start(piece, core, rows):
    return pl.multiple_of((2 * piece + core) * rows, rows)


def masked_roll(values, steps, length, zero_rows):
    rolled = pltpu.roll(values, steps % length, 0)
    row = lax.broadcasted_iota(jnp.int32, values.shape, 0)
    kept = row != zero_rows[0]
    for at in zero_rows[1:]:
        kept = kept & (row != at)
    return jnp.where(kept, rolled, 0.0)


def convolved(b_part, x_part, taps, length, first):
    product = b_part * x_part
    second = lax.rem(first + 1, length)
    one = masked_roll(product, 1, length, (first,))
    two = masked_roll(product, 2, length, (first, second))
    return product, one, two, taps[0:1] * two + taps[1:2] * one + taps[2:3] * product


def own_columns(groups, block, at_ref, shape):
    row = lax.broadcasted_iota(jnp.int32, shape, 0)
    ahead = lax.broadcasted_iota(jnp.int32, shape, 1) - row
    stride = shape[1] // groups
    found = jnp.zeros(shape, f32)
    for k in range(groups):
        base = jnp.bitwise_xor(at_ref[2], k) * stride + (at_ref[3] - k) * block
        inside = (row >= k * block) & (row < (k + 1) * block)
        found = jnp.where(inside & (ahead == base), 1.0, found)
    return found


def mixer_forward(count, groups, at_ref, *refs):
    pieces, parts = refs[: 2 * count], refs[2 * count : 2 * count + groups]
    gain_ref, conv_ref, h_ref, w_ref, p_ref, y_ref, taps_ref, keep_ref, send_ref = refs[
        2 * count + groups :
    ]
    rows, length = pieces[0].shape[0], h_ref.shape[0]
    block, channels = parts[0].shape[1], y_ref.shape[1]
    core, first = at_ref[0], at_ref[1]
    taps_ref[...] = lax.dot_general(
        conv_ref[...],
        own_columns(groups, block, at_ref, (channels, conv_ref.shape[1])),
        (((1,), (1,)), ((), ())),
        precision=lax.Precision.HIGHEST,
        preferred_element_type=f32,
    )
    for k in range(4):
        for s in range(groups):
            w_ref[k * channels + s * block : k * channels + (s + 1) * block, :] = parts[s][k]
    gain = gain_ref[...]
    for j in range(2 * count):
        x = pieces[j][...].astype(f32)
        scale = lax.rsqrt(jnp.mean(x * x, axis=-1, keepdims=True) + norm_eps)
        side = core if j < count else 1 - core
        h_ref[pl.ds(block_start(j % count, side, rows), rows), :] = (x * scale * gain).astype(bf16)
    p_ref[...] = by_rows(h_ref[...], w_ref[: 3 * channels, :])
    in_b, in_c = p_ref[:, :channels], p_ref[:, channels : 2 * channels]
    in_x = p_ref[:, 2 * channels :]
    mixed = convolved(in_b, in_x, taps_ref[...], length, first)[3]
    y_ref[...] = (in_c * mixed).astype(bf16)
    out_w = w_ref[3 * channels :, :]
    for side, out_ref in ((1 - core, send_ref), (core, keep_ref)):
        rows_of = [y_ref[pl.ds(block_start(k, side, rows), rows), :] for k in range(count)]
        part = jnp.dot(jnp.concatenate(rows_of, axis=0), out_w, preferred_element_type=f32)
        out_ref[...] = part.astype(out_ref.dtype)


def mixer_backward(count, groups, at_ref, *refs):
    pieces = refs[: 2 * count]
    h_ref, w_ref, p_ref, gain_ref, taps_ref, gain_two_ref = refs[2 * count : 2 * count + 6]
    dm_ref, dp_ref, small_ref, keep_ref, send_ref = refs[2 * count + 6 :]
    rows, length = pieces[0].shape[0], h_ref.shape[0]
    channels = taps_ref.shape[1]
    core, first = at_ref[0], at_ref[1]
    for j in range(2 * count):
        side = core if j < count else 1 - core
        dm_ref[pl.ds(block_start(j % count, side, rows), rows), :] = pieces[j][...]
    grad_gated = by_rows(dm_ref[...], w_ref[3 * channels :, :])
    in_b, in_c = p_ref[:, :channels], p_ref[:, channels : 2 * channels]
    in_x = p_ref[:, 2 * channels :]
    taps = taps_ref[...]
    product, one, two, mixed = convolved(in_b, in_x, taps, length, first)
    grad_mixed = grad_gated * in_c
    last = lax.rem(first + length - 1, length)
    before = lax.rem(first + length - 2, length)
    next_one = masked_roll(grad_mixed, -1, length, (last,))
    next_two = masked_roll(grad_mixed, -2, length, (last, before))
    grad_prod = taps[0:1] * next_two + taps[1:2] * next_one + taps[2:3] * grad_mixed
    dp_ref[:, :channels] = (grad_prod * in_x).astype(bf16)
    dp_ref[:, channels : 2 * channels] = (grad_gated * mixed).astype(bf16)
    dp_ref[:, 2 * channels :] = (grad_prod * in_b).astype(bf16)
    tap_sums = [
        jnp.sum(grad_mixed * shifted, axis=0, keepdims=True) for shifted in (two, one, product)
    ]
    small_ref[2:, :] = jnp.dot(
        jnp.concatenate(tap_sums, axis=0),
        own_columns(groups, channels // groups, at_ref, (channels, h_ref.shape[1])),
        precision=lax.Precision.HIGHEST,
        preferred_element_type=f32,
    )
    small_ref[1:2, :] = gain_two_ref[...]
    gain_sum = jnp.zeros(gain_ref.shape, f32)
    for side, out_ref in ((1 - core, send_ref), (core, keep_ref)):
        starts = [block_start(k, side, rows) for k in range(count)]
        grads = jnp.concatenate([dp_ref[pl.ds(at, rows), :] for at in starts], axis=0)
        part = jnp.dot(grads, w_ref[: 3 * channels, :], preferred_element_type=f32)
        out_ref[...] = part.astype(out_ref.dtype)
        normed = jnp.concatenate([h_ref[pl.ds(at, rows), :] for at in starts], axis=0)
        gain_sum = gain_sum + jnp.sum(part * normed.astype(f32), axis=0, keepdims=True)
    small_ref[0:1, :] = gain_sum / gain_ref[...]


def mixer_weight_grads(groups, dp_ref, h_ref, y_ref, dm_ref, *outs):
    block = outs[0].shape[1]
    channels = y_ref.shape[1]
    inner = down_rows(dp_ref[...], h_ref[...])
    outer = down_rows(y_ref[...], dm_ref[...])
    for s in range(groups):
        for k in range(3):
            at = k * channels + s * block
            outs[s][k] = inner[at : at + block].astype(outs[s].dtype)
        outs[s][3] = outer[s * block : (s + 1) * block].astype(outs[s].dtype)


def ffn_rows(count, groups, *refs):
    pieces, g_pieces = refs[: 2 * count], refs[2 * count : 4 * count]
    parts = refs[4 * count : 4 * count + groups]
    h_ref, g_ref, act_ref, gate_ref, up_ref, down_ref, keep_ref, send_ref, w_ref = refs[
        4 * count + groups :
    ]
    rows, block, hidden = pieces[0].shape[0], parts[0].shape[1], down_ref.shape[0]
    for j in range(2 * count):
        h_ref[j * rows : (j + 1) * rows, :] = pieces[j][...]
        g_ref[j * rows : (j + 1) * rows, :] = g_pieces[j][...]
    for s in range(groups):
        for k in range(2):
            at = k * hidden + s * block
            w_ref[at : at + block, :] = parts[s][k]
        down_ref[s * block : (s + 1) * block, :] = parts[s][2]
    side_rows = count * rows
    for at, out_ref in ((side_rows, send_ref), (0, keep_ref)):
        these = slice(at, at + side_rows)
        gate = by_rows(h_ref[these, :], w_ref[:hidden, :])
        up = by_rows(h_ref[these, :], w_ref[hidden:, :])
        sigmoid = jax.nn.sigmoid(gate)
        gate_act = gate * sigmoid
        act_ref[these, :] = (gate_act * up).astype(bf16)
        grad_act = by_rows(g_ref[these, :], down_ref[...])
        up_ref[these, :] = (grad_act * gate_act).astype(bf16)
        gate_ref[these, :] = (
            grad_act * up * sigmoid * (1.0 + gate * (1.0 - sigmoid))
        ).astype(bf16)
        part = jnp.dot(gate_ref[these, :], w_ref[:hidden, :], preferred_element_type=f32)
        part = part + jnp.dot(up_ref[these, :], w_ref[hidden:, :], preferred_element_type=f32)
        out_ref[...] = part.astype(out_ref.dtype)


def ffn_down(act_ref, down_ref, keep_ref, send_ref):
    half = keep_ref.shape[0]
    for at, out_ref in ((half, send_ref), (0, keep_ref)):
        part = jnp.dot(act_ref[at : at + half, :], down_ref[...], preferred_element_type=f32)
        out_ref[...] = part.astype(out_ref.dtype)


def ffn_weight_grads(groups, gate_ref, up_ref, act_ref, h_ref, g_ref, *outs):
    block = outs[0].shape[1]
    for k, (left, right) in enumerate(((gate_ref, h_ref), (up_ref, h_ref), (act_ref, g_ref))):
        term = down_rows(left[...], right[...])
        for s in range(groups):
            outs[s][k] = term[s * block : (s + 1) * block].astype(outs[s].dtype)


def mixer_adam(groups, *refs):
    own_ref, *parts = refs[:groups]
    weight, first, second, grad_out, weight_out, first_out, second_out = refs[groups:]
    for k in range(4):
        grad = own_ref[k]
        for part in parts:
            grad = grad + part[k].astype(f32)
        news = adam_update(
            weight[:, k, :], grad, first[:, k, :], second[:, k, :], matrix_rate, decay_rate
        )
        grad_out[:, k, :] = grad
        for out, new in zip((weight_out, first_out, second_out), news):
            out[:, k, :] = new


def pair_kernel(kept_ref, got_ref, *outs):
    rows = outs[0].shape[0]
    for k, out_ref in enumerate(outs):
        at = slice(k * rows, (k + 1) * rows)
        out_ref[...] = (kept_ref[at, :] + got_ref[at, :].astype(f32)).astype(out_ref.dtype)


def total_of(own_ref, got_refs):
    total = own_ref[...]
    for got in got_refs:
        total = total + got[...].astype(f32)
    return total


def second_norm(*refs):
    own_ref, *got = refs[:-5]
    x_ref, gain_ref, resid_ref, normed_ref, h_ref = refs[-5:]
    residual = x_ref[...].astype(f32) + total_of(own_ref, got)
    resid_ref[...] = residual
    normed = residual * lax.rsqrt(jnp.mean(residual * residual, axis=-1, keepdims=True) + norm_eps)
    normed_ref[...] = normed
    h_ref[...] = (normed * gain_ref[...]).astype(bf16)


def second_norm_backward(*refs):
    own_ref, *got = refs[:-7]
    resid_ref, normed_ref, g_ref, gain_ref, grad_ref, dm_ref, gain_part_ref = refs[-7:]
    grad_h = total_of(own_ref, got)
    normed, residual = normed_ref[...], resid_ref[...]
    scale = lax.rsqrt(jnp.mean(residual * residual, axis=-1, keepdims=True) + norm_eps)
    grad = g_ref[...].astype(f32) + norm_backward(grad_h * gain_ref[...], normed, scale)
    grad_ref[...] = grad
    dm_ref[...] = grad.astype(bf16)
    gain_part_ref[...] = jnp.sum(grad_h * normed, axis=0, keepdims=True)


def first_norm_backward(*refs):
    own_ref, *got = refs[:-4]
    x_ref, grad_ref, gain_ref, out_ref = refs[-4:]
    x = x_ref[...].astype(f32)
    scale = lax.rsqrt(jnp.mean(x * x, axis=-1, keepdims=True) + norm_eps)
    out_ref[...] = grad_ref[...] + norm_backward(
        total_of(own_ref, got) * gain_ref[...], x * scale, scale
    )


def output_kernel(*refs):
    own_ref, *got = refs[:-2]
    resid_ref, out_ref = refs[-2:]
    out_ref[...] = (resid_ref[...] + total_of(own_ref, got)).astype(out_ref.dtype)


def collect_rows(kept, sent):
    count = lax.axis_size("ctx")
    rows, width = kept.shape[0] // count, kept.shape[1]
    outs = [((rows, width), f32)] + [((rows, width), bf16)] * (count - 1)
    got = swap_with(sent, "tp", 1)
    pieces = in_vmem(pair_kernel, outs, kept, got)
    return [pieces[0]] + [send_up(pieces[k], "ctx", k) for k in range(1, count)]


def per_device(
    inputs,
    cotangent,
    mixer_matrix,
    ffn_weight,
    conv_weight,
    norm_gains,
    mixer_first,
    mixer_second,
    ffn_first,
    ffn_second,
    conv_first,
    conv_second,
    gain_first,
    gain_second,
):
    shard_count = lax.axis_size("shard")
    ctx_count = lax.axis_size("ctx")
    tp_count = lax.axis_size("tp")
    seq_count, tok_count, width = inputs.shape
    assert seq_count == 1 and tp_count == 2
    shard_at = lax.axis_index("shard")
    ctx_at = lax.axis_index("ctx")
    tp_at = lax.axis_index("tp")
    half = tok_count // tp_count
    seq_len = tok_count * ctx_count
    first_core = tp_at == 0

    def own_half(rows):
        return lax.dynamic_slice_in_dim(rows[0], tp_at * half, half, axis=0)

    def both_halves(mine):
        other = swap_with(mine, "tp", 1)
        return jnp.concatenate(
            [jnp.where(first_core, mine, other), jnp.where(first_core, other, mine)], axis=0
        )[None]

    x_half = own_half(inputs)
    x_pieces = spread_rows(x_half)
    mixer_own = mixer_matrix.transpose(1, 0, 2).astype(bf16)
    mixer_parts = [mixer_own] + [swap_with(mixer_own, "shard", k) for k in range(1, shard_count)]
    g_half = own_half(cotangent)
    g_pieces = spread_rows(g_half)
    ffn_own = ffn_weight.transpose(1, 0, 2).astype(bf16)
    ffn_parts = [ffn_own] + [swap_with(ffn_own, "shard", k) for k in range(1, shard_count)]

    block, ffn_block = mixer_own.shape[1], ffn_own.shape[1]
    channels, hidden = block * shard_count, ffn_block * shard_count
    first = (seq_len - ctx_at * tok_count) % seq_len
    scalars = jnp.stack([tp_at, first, shard_at, ctx_at * tp_count + tp_at]).astype(jnp.int32)
    gain_one, gain_two = norm_gains[0:1], norm_gains[1:2]
    mine_count = seq_len // 2
    half_shape, half_sent = ((half, width), f32), ((half, width), bf16)
    parted = [((mine_count, width), f32), ((mine_count, width), bf16)]

    h_one, mixer_w, projected, gated, taps, kept, sent = in_vmem(
        functools.partial(mixer_forward, ctx_count, shard_count),
        [
            ((seq_len, width), bf16),
            ((4 * channels, width), bf16),
            ((seq_len, 3 * channels), f32),
            ((seq_len, channels), bf16),
            ((3, channels), f32),
        ]
        + parted,
        *x_pieces,
        *mixer_parts,
        gain_one,
        conv_weight,
        scalars=scalars,
        flops=8 * seq_len * channels * width,
    )
    residual, normed_two, h_two_own = in_vmem(
        second_norm,
        [half_shape, half_shape, half_sent],
        *collect_rows(kept, sent),
        x_half,
        gain_two,
    )

    hidden_rows = ((seq_len, hidden), bf16)
    h_two, g_all, act, grad_gate, grad_up, down_w, kept, sent = in_vmem(
        functools.partial(ffn_rows, ctx_count, shard_count),
        [
            ((seq_len, width), bf16),
            ((seq_len, width), bf16),
            hidden_rows,
            hidden_rows,
            hidden_rows,
            ((hidden, width), bf16),
        ]
        + parted,
        *spread_rows(h_two_own),
        *g_pieces,
        *ffn_parts,
        scratch=[pltpu.VMEM((2 * hidden, width), bf16)],
        flops=10 * seq_len * hidden * width,
    )
    grad_resid, grad_mix_own, gain_two_part = in_vmem(
        second_norm_backward,
        [half_shape, half_sent, ((1, width), f32)],
        *collect_rows(kept, sent),
        residual,
        normed_two,
        g_half,
        gain_two,
    )
    kept, sent = in_vmem(ffn_down, parted, act, down_w, flops=2 * seq_len * hidden * width)
    ffn_pieces = collect_rows(kept, sent)
    ffn_terms = in_vmem(
        functools.partial(ffn_weight_grads, shard_count),
        [((3, ffn_block, width), f32)] + [((3, ffn_block, width), bf16)] * (shard_count - 1),
        grad_gate,
        grad_up,
        act,
        h_two,
        g_all,
        flops=6 * seq_len * hidden * width,
    )
    ffn_got = [swap_with(ffn_terms[k], "shard", k) for k in range(1, shard_count)]

    grad_mix_all, grad_triple, small, kept, sent = in_vmem(
        functools.partial(mixer_backward, ctx_count, shard_count),
        [
            ((seq_len, width), bf16),
            ((seq_len, 3 * channels), bf16),
            ((5, width), f32),
        ]
        + parted,
        *spread_rows(grad_mix_own),
        h_one,
        mixer_w,
        projected,
        gain_one,
        taps,
        gain_two_part,
        scalars=scalars,
        flops=8 * seq_len * channels * width,
    )
    in_pieces = collect_rows(kept, sent)
    mixer_terms = in_vmem(
        functools.partial(mixer_weight_grads, shard_count),
        [((4, block, width), f32)] + [((4, block, width), bf16)] * (shard_count - 1),
        grad_triple,
        h_one,
        gated,
        grad_mix_all,
        flops=8 * seq_len * channels * width,
    )
    mixer_got = [swap_with(mixer_terms[k], "shard", k) for k in range(1, shard_count)]
    small = sum_over(sum_over(small, "tp"), "shard")
    small = sum_over(small, "ctx")
    gain_grad, conv_grad = small[:2], small[2:]

    ffn_grad = ffn_terms[0]
    for got in ffn_got:
        ffn_grad = ffn_grad + got.astype(f32)
    ffn_grad = ffn_grad.transpose(1, 0, 2)
    ffn_new, ffn_first_new, ffn_second_new = adam_update(
        ffn_weight, ffn_grad, ffn_first, ffn_second, matrix_rate, decay_rate
    )
    out_own = in_vmem(output_kernel, [half_sent], *ffn_pieces, residual)[0]
    output = both_halves(out_own)
    input_grad = both_halves(
        in_vmem(first_norm_backward, [half_shape], *in_pieces, x_half, grad_resid, gain_one)[0],
    )
    mixer_grad, mixer_new, mixer_first_new, mixer_second_new = in_vmem(
        functools.partial(mixer_adam, shard_count),
        [(mixer_matrix.shape, f32)] * 4,
        mixer_terms[0],
        *mixer_got,
        mixer_matrix,
        mixer_first,
        mixer_second,
    )
    conv_new, conv_first_new, conv_second_new = adam_update(
        conv_weight, conv_grad, conv_first, conv_second, small_rate, 0.0
    )
    gain_new, gain_first_new, gain_second_new = adam_update(
        norm_gains, gain_grad, gain_first, gain_second, small_rate, 0.0
    )
    return (
        output,
        input_grad,
        mixer_grad,
        ffn_grad,
        conv_grad,
        gain_grad,
        mixer_new,
        ffn_new,
        conv_new,
        gain_new,
        mixer_first_new,
        mixer_second_new,
        ffn_first_new,
        ffn_second_new,
        conv_first_new,
        conv_second_new,
        gain_first_new,
        gain_second_new,
    )


def solution(mesh):
    tokens = P("shard", "ctx", None)
    rows = P(("shard", "ctx", "tp"), None, None)
    in_specs = (tokens, tokens, rows, rows, P(), P(), rows, rows, rows, rows, P(), P(), P(), P())
    out_specs = (
        (tokens, tokens, rows, rows, P(), P(), rows, rows, P(), P())
        + (rows, rows, rows, rows)
        + (P(), P(), P(), P())
    )

    return jax.shard_map(
        per_device, mesh=mesh, in_specs=in_specs, out_specs=out_specs, check_vma=False
    )
```

profile of v0, /device:TPU:0, one launch (start us, length us, event | category | flops | bytes accessed | tf_op | source)
XLA Modules:
  0.0 202.1 jit_solution(11728515427654528525)
XLA Ops:
  1.6 3.1 %collective-permute-start.2 = (bf16[64,1024]{1,0:T(8,128)(2,1)S(1)}, bf16[64,1024]{1,0:T(8,128)(2,1)S(1)}, u32[]{:S(2)}, u32[]{:S(2)}) collective-permute-start(bf16[64,1024]{1,0:T(8,128)(2,1)S(1)} %dynamic-slice_bitcast_fusion.1.refs_0_.refs_4_), channel_id=1, source_target_pairs={{0,2},{2,4},{4,6},{6,0},{1,3},{3,5},{5,7},{7,1},{8,10},{10,12},{12... | collective-permute-start | bytes 393224 | tf_op jit(solution)/shard_map/ppermute | solution.py:53
  4.7 2.6 %collective-permute-start.1 = (bf16[64,1024]{1,0:T(8,128)(2,1)S(1)}, bf16[64,1024]{1,0:T(8,128)(2,1)S(1)}, u32[]{:S(2)}, u32[]{:S(2)}) collective-permute-start(bf16[64,1024]{1,0:T(8,128)(2,1)S(1)} %dynamic-slice_bitcast_fusion.1.refs_0_.refs_4_), channel_id=1, source_target_pairs={{0,4},{2,6},{4,0},{6,2},{1,5},{3,7},{5,1},{7,3},{8,12},{10,14},{12... | collective-permute-start | bytes 393224 | tf_op jit(solution)/shard_map/ppermute | solution.py:53
  8.7 2.2 %collective-permute-done.2.refs_3_ = bf16[64,1024]{1,0:T(8,128)(2,1)S(1)} collective-permute-done((bf16[64,1024]{1,0:T(8,128)(2,1)S(1)}, bf16[64,1024]{1,0:T(8,128)(2,1)S(1)}, u32[]{:S(2)}, u32[]{:S(2)}) %collective-permute-start.2) | collective-permute-done | bytes 131104 | tf_op jit(solution)/shard_map/ppermute | solution.py:53
  12.2 2.5 %collective-permute-start.9 = (bf16[4,32,1024]{2,1,0:T(8,128)(2,1)S(1)}, bf16[4,32,1024]{2,1,0:T(8,128)(2,1)S(1)}, u32[]{:S(2)}, u32[]{:S(2)}) collective-permute-start(bf16[4,32,1024]{2,1,0:T(8,128)(2,1)S(1)} %bitcast.20), channel_id=1, source_target_pairs={{0,24},{8,16},{16,8},{24,0},{1,25},{9,17},{17,9},{25,1},{2,26},{10... | collective-permute-start | bytes 786440 | tf_op jit(solution)/shard_map/ppermute | solution.py:46
  16.0 1.5 collective-permute-start.7
  22.4 5.1 %collective-permute-done.8.refs_10_ = bf16[4,32,1024]{2,1,0:T(8,128)(2,1)S(1)} collective-permute-done((bf16[4,32,1024]{2,1,0:T(8,128)(2,1)S(1)}, bf16[4,32,1024]{2,1,0:T(8,128)(2,1)S(1)}, u32[]{:S(2)}, u32[]{:S(2)}) %collective-permute-start.8) | collective-permute-done | bytes 262176 | tf_op jit(solution)/shard_map/ppermute | solution.py:46
  33.7 3.9 %shard_map.277 = (bf16[512,1024]{1,0:T(8,128)(2,1)S(1)}, bf16[512,1024]{1,0:T(8,128)(2,1)S(1)}, f32[512,384]{1,0:T(8,128)S(1)}, bf16[512,128]{1,0:T(8,128)(2,1)S...) custom-call(s32[4]{0:T(128)S(1)} %pad_add_fusion.at_ref, ...), custom_call_target="tpu_custom_call" | custom-call | flops 536870912 | bytes 6702608 | tf_op jit(solution)/shard_map/pallas_call | solution.py:80
  39.3 2.4 %collective-permute-start.30 = (bf16[3,144,1024]{2,1,0:T(8,128)(2,1)S(1)}, bf16[3,144,1024]{2,1,0:T(8,128)(2,1)S(1)}, u32[]{:S(2)}, u32[]{:S(2)}) collective-permute-start(bf16[3,144,1024]{2,1,0:T(8,128)(2,1)S(1)} %convert_bitcast_fusion.refs_16_), channel_id=1, source_target_pairs={{0,24},{8,16},{16,8},{24,0},{1,25},{9,17},{17,9},{25,1},{2,26},{10... | collective-permute-start | bytes 2654216 | tf_op jit(solution)/shard_map/ppermute | solution.py:46
  42.4 4.6 %collective-permute-start.23 = (bf16[64,1024]{1,0:T(8,128)(2,1)S(1)}, bf16[64,1024]{1,0:T(8,128)(2,1)S(1)}, u32[]{:S(2)}, u32[]{:S(2)}) collective-permute-start(bf16[64,1024]{1,0:T(8,128)(2,1)S(1)} %dynamic-slice_bitcast_fusion.refs_8_.refs_6_), channel_id=1, source_target_pairs={{0,2},{2,4},{4,6},{6,0},{1,3},{3,5},{5,7},{7,1},{8,10},{10,12},{12... | collective-permute-start | bytes 393224 | tf_op jit(solution)/shard_map/ppermute | solution.py:53
  47.7 2.7 %collective-permute-done.23.refs_11_ = bf16[64,1024]{1,0:T(8,128)(2,1)S(1)} collective-permute-done((bf16[64,1024]{1,0:T(8,128)(2,1)S(1)}, bf16[64,1024]{1,0:T(8,128)(2,1)S(1)}, u32[]{:S(2)}, u32[]{:S(2)}) %collective-permute-start.23) | collective-permute-done | bytes 131104 | tf_op jit(solution)/shard_map/ppermute | solution.py:53
  50.4 4.5 %collective-permute-start.22 = (bf16[64,1024]{1,0:T(8,128)(2,1)S(1)}, bf16[64,1024]{1,0:T(8,128)(2,1)S(1)}, u32[]{:S(2)}, u32[]{:S(2)}) collective-permute-start(bf16[64,1024]{1,0:T(8,128)(2,1)S(1)} %dynamic-slice_bitcast_fusion.refs_8_.refs_6_), channel_id=1, source_target_pairs={{0,4},{2,6},{4,0},{6,2},{1,5},{3,7},{5,1},{7,3},{8,12},{10,14},{12... | collective-permute-start | bytes 393224 | tf_op jit(solution)/shard_map/ppermute | solution.py:53
  55.5 5.8 %collective-permute-done.22.refs_10_ = bf16[64,1024]{1,0:T(8,128)(2,1)S(1)} collective-permute-done((bf16[64,1024]{1,0:T(8,128)(2,1)S(1)}, bf16[64,1024]{1,0:T(8,128)(2,1)S(1)}, u32[]{:S(2)}, u32[]{:S(2)}) %collective-permute-start.22) | collective-permute-done | bytes 131104 | tf_op jit(solution)/shard_map/ppermute | solution.py:53
  62.2 2.2 %collective-permute-start.11 = (bf16[64,1024]{1,0:T(8,128)(2,1)S(1)}, bf16[64,1024]{1,0:T(8,128)(2,1)S(1)}, u32[]{:S(2)}, u32[]{:S(2)}) collective-permute-start(bf16[64,1024]{1,0:T(8,128)(2,1)S(1)} %get-tuple-element.77), channel_id=1, source_target_pairs={{0,2},{2,4},{4,6},{6,0},{1,3},{3,5},{5,7},{7,1},{8,10},{10,12},{12... | collective-permute-start | bytes 393224 | tf_op jit(solution)/shard_map/ppermute | solution.py:53
  64.4 2.6 %collective-permute-start.12 = (bf16[64,1024]{1,0:T(8,128)(2,1)S(1)}, bf16[64,1024]{1,0:T(8,128)(2,1)S(1)}, u32[]{:S(2)}, u32[]{:S(2)}) collective-permute-start(bf16[64,1024]{1,0:T(8,128)(2,1)S(1)} %get-tuple-element.78), channel_id=1, source_target_pairs={{0,4},{2,6},{4,0},{6,2},{1,5},{3,7},{5,1},{7,3},{8,12},{10,14},{12... | collective-permute-start | bytes 393224 | tf_op jit(solution)/shard_map/ppermute | solution.py:53
  67.0 3.9 %collective-permute-done.11.refs_1_ = bf16[64,1024]{1,0:T(8,128)(2,1)S(1)} collective-permute-done((bf16[64,1024]{1,0:T(8,128)(2,1)S(1)}, bf16[64,1024]{1,0:T(8,128)(2,1)S(1)}, u32[]{:S(2)}, u32[]{:S(2)}) %collective-permute-start.11) | collective-permute-done | bytes 131104 | tf_op jit(solution)/shard_map/ppermute | solution.py:53
  70.9 1.8 collective-permute-start.13
  72.7 3.7 %collective-permute-done.12.refs_2_ = bf16[64,1024]{1,0:T(8,128)(2,1)S(1)} collective-permute-done((bf16[64,1024]{1,0:T(8,128)(2,1)S(1)}, bf16[64,1024]{1,0:T(8,128)(2,1)S(1)}, u32[]{:S(2)}, u32[]{:S(2)}) %collective-permute-start.12) | collective-permute-done | bytes 131104 | tf_op jit(solution)/shard_map/ppermute | solution.py:53
  76.4 2.3 %collective-permute-done.13.refs_3_ = bf16[64,1024]{1,0:T(8,128)(2,1)S(1)} collective-permute-done((bf16[64,1024]{1,0:T(8,128)(2,1)S(1)}, bf16[64,1024]{1,0:T(8,128)(2,1)S(1)}, u32[]{:S(2)}, u32[]{:S(2)}) %collective-permute-start.13) | collective-permute-done | bytes 131104 | tf_op jit(solution)/shard_map/ppermute | solution.py:53
  80.1 1.7 collective-permute-start.15
  81.8 1.6 collective-permute-start.14
  83.4 3.9 %collective-permute-done.16.refs_3_ = bf16[64,1024]{1,0:T(8,128)(2,1)S(1)} collective-permute-done((bf16[64,1024]{1,0:T(8,128)(2,1)S(1)}, bf16[64,1024]{1,0:T(8,128)(2,1)S(1)}, u32[]{:S(2)}, u32[]{:S(2)}) %collective-permute-start.16) | collective-permute-done | bytes 131104 | tf_op jit(solution)/shard_map/ppermute | solution.py:53
  87.3 5.1 %collective-permute-done.15.refs_2_ = bf16[64,1024]{1,0:T(8,128)(2,1)S(1)} collective-permute-done((bf16[64,1024]{1,0:T(8,128)(2,1)S(1)}, bf16[64,1024]{1,0:T(8,128)(2,1)S(1)}, u32[]{:S(2)}, u32[]{:S(2)}) %collective-permute-start.15) | collective-permute-done | bytes 131104 | tf_op jit(solution)/shard_map/ppermute | solution.py:53
  94.0 8.4 %shard_map.280 = (bf16[512,1024]{1,0:T(8,128)(2,1)}, bf16[512,1024]{1,0:T(8,128)(2,1)}, bf16[512,576]{1,0:T(8,128)(2,1)S(1)}, bf16[512,576]{1,0:T(8,128)(2,1)S(1...) custom-call(bf16[64,1024]{1,0:T(8,128)(2,1)S(1)} %get-tuple-element., ...), custom_call_target="tpu_custom_call" | custom-call | flops 3019898880 | bytes 12255232 | tf_op jit(solution)/shard_map/pallas_call | solution.py:80
  106.7 3.0 %collective-permute-start.32 = (bf16[64,1024]{1,0:T(8,128)(2,1)S(1)}, bf16[64,1024]{1,0:T(8,128)(2,1)S(1)}, u32[]{:S(2)}, u32[]{:S(2)}) collective-permute-start(bf16[64,1024]{1,0:T(8,128)(2,1)S(1)} %get-tuple-element.86), channel_id=1, source_target_pairs={{0,2},{2,4},{4,6},{6,0},{1,3},{3,5},{5,7},{7,1},{8,10},{10,12},{12... | collective-permute-start | bytes 393224 | tf_op jit(solution)/shard_map/ppermute | solution.py:53
  109.8 2.3 %collective-permute-start.34 = (bf16[64,1024]{1,0:T(8,128)(2,1)S(1)}, bf16[64,1024]{1,0:T(8,128)(2,1)S(1)}, u32[]{:S(2)}, u32[]{:S(2)}) collective-permute-start(bf16[64,1024]{1,0:T(8,128)(2,1)S(1)} %get-tuple-element.88), channel_id=1, source_target_pairs={{0,6},{2,0},{4,2},{6,4},{1,7},{3,1},{5,3},{7,5},{8,14},{10,8},{12,... | collective-permute-start | bytes 393224 | tf_op jit(solution)/shard_map/ppermute | solution.py:53
  112.3 2.5 %collective-permute-start.38 = (bf16[64,1024]{1,0:T(8,128)(2,1)S(1)}, bf16[64,1024]{1,0:T(8,128)(2,1)S(1)}, u32[]{:S(2)}, u32[]{:S(2)}) collective-permute-start(bf16[64,1024]{1,0:T(8,128)(2,1)S(1)} %get-tuple-element.94), channel_id=1, source_target_pairs={{0,4},{2,6},{4,0},{6,2},{1,5},{3,7},{5,1},{7,3},{8,12},{10,14},{12... | collective-permute-start | bytes 393224 | tf_op jit(solution)/shard_map/ppermute | solution.py:53
  116.1 5.2 %shard_map.291 = (f32[3,144,1024]{2,1,0:T(8,128)}, bf16[3,144,1024]{2,1,0:T(8,128)(2,1)}, bf16[3,144,1024]{2,1,0:T(8,128)(2,1)}, bf16[3,144,1024]{2,1,0:T(8,128)(2,1)}) custom-call(bf16[512,576]{1,0:T(8,128)(2,1)S(1)} %get-tuple-element.118.gate_ref, bf16[512,576]{1,0:T(8,128)(2,1)S(1)} %get-tuple-element.119.up_ref, ...), custom_call_target="tpu_custom_call" | custom-call | flops 1811939328 | bytes 8290304 | tf_op jit(solution)/shard_map/pallas_call | solution.py:80
  125.0 6.3 %collective-permute-done.38.refs_2_ = bf16[64,1024]{1,0:T(8,128)(2,1)S(1)} collective-permute-done((bf16[64,1024]{1,0:T(8,128)(2,1)S(1)}, bf16[64,1024]{1,0:T(8,128)(2,1)S(1)}, u32[]{:S(2)}, u32[]{:S(2)}) %collective-permute-start.38) | collective-permute-done | bytes 131104 | tf_op jit(solution)/shard_map/ppermute | solution.py:53
  132.6 2.3 %collective-permute-start.42 = (bf16[64,1024]{1,0:T(8,128)(2,1)S(1)}, bf16[64,1024]{1,0:T(8,128)(2,1)S(1)}, u32[]{:S(2)}, u32[]{:S(2)}) collective-permute-start(bf16[64,1024]{1,0:T(8,128)(2,1)S(1)} %get-tuple-element.97.refs_0_), channel_id=1, source_target_pairs={{0,2},{2,4},{4,6},{6,0},{1,3},{3,5},{5,7},{7,1},{8,10},{10,12},{12... | collective-permute-start | bytes 393224 | tf_op jit(solution)/shard_map/ppermute | solution.py:53
  135.0 2.5 %collective-permute-start.41 = (bf16[64,1024]{1,0:T(8,128)(2,1)S(1)}, bf16[64,1024]{1,0:T(8,128)(2,1)S(1)}, u32[]{:S(2)}, u32[]{:S(2)}) collective-permute-start(bf16[64,1024]{1,0:T(8,128)(2,1)S(1)} %get-tuple-element.97.refs_0_), channel_id=1, source_target_pairs={{0,4},{2,6},{4,0},{6,2},{1,5},{3,7},{5,1},{7,3},{8,12},{10,14},{12... | collective-permute-start | bytes 393224 | tf_op jit(solution)/shard_map/ppermute | solution.py:53
  137.4 3.9 %collective-permute-done.42.refs_3_ = bf16[64,1024]{1,0:T(8,128)(2,1)S(1)} collective-permute-done((bf16[64,1024]{1,0:T(8,128)(2,1)S(1)}, bf16[64,1024]{1,0:T(8,128)(2,1)S(1)}, u32[]{:S(2)}, u32[]{:S(2)}) %collective-permute-start.42) | collective-permute-done | bytes 131104 | tf_op jit(solution)/shard_map/ppermute | solution.py:53
  141.3 1.9 collective-permute-start.40
  143.3 3.2 %collective-permute-done.41.refs_2_ = bf16[64,1024]{1,0:T(8,128)(2,1)S(1)} collective-permute-done((bf16[64,1024]{1,0:T(8,128)(2,1)S(1)}, bf16[64,1024]{1,0:T(8,128)(2,1)S(1)}, u32[]{:S(2)}, u32[]{:S(2)}) %collective-permute-start.41) | collective-permute-done | bytes 131104 | tf_op jit(solution)/shard_map/ppermute | solution.py:53
  146.5 1.9 collective-permute-done.40.refs_1_
  150.6 3.6 %shard_map.286 = (bf16[512,1024]{1,0:T(8,128)(2,1)S(1)}, bf16[512,384]{1,0:T(8,128)(2,1)S(1)}, f32[5,1024]{1,0:T(8,128)S(1)}, f32[256,1024]{1,0:T(8,128)S(1)}, bf16[256,1024]{1,0:T(8,128)(2,1)S(1)}) custom-call(s32[4]{0:T(128)S(1)} %pad_add_fusion.at_ref, bf16[64,1024]{1,0:T(8,128)(2,1)S(1)} %get-tuple-element.97.refs_0_, ...), custom_call_target="tpu_custom_call" | custom-call | flops 536870912 | bytes 6977040 | tf_op jit(solution)/shard_map/pallas_call | solution.py:80
  155.5 1.5 collective-permute-start.61
  157.6 6.4 %collective-permute-start.59 = (f32[5,1024]{1,0:T(8,128)S(1)}, f32[5,1024]{1,0:T(8,128)S(1)}, u32[]{:S(2)}, u32[]{:S(2)}) collective-permute-start(f32[5,1024]{1,0:T(8,128)S(1)} %add.92), channel_id=1, source_target_pairs={{0,8},{8,0},{16,24},{24,16},{1,9},{9,1},{17,25},{25,17},{2,10},{10... | collective-permute-start | bytes 61448 | tf_op jit(solution)/shard_map/ppermute | solution.py:46
  164.0 6.8 %multiply_subtract_fusion = (f32[144,3,1024]{2,0,1:T(8,128)}, f32[144,3,1024]{2,0,1:T(8,128)}, f32[144,3,1024]{2,0,1:T(8,128)}, f32[144,3,1024]{2,0,1:T(8,128)}) fusion(f32[144,3,1024]{2,0,1:T(8,128)S(1)} %copy-done.26, f32[144,3,1024]{2,0,1:T(8,128)S(1)} %copy-done.27, f32[144,3,1024]{2,0,1:T(8,128)} %param.23, ...), kind=kLoop, calls=%fused_computation.2 | loop fusion | flops 9289728 | bytes 16809984 | tf_op jit(solution)/shard_map/sub | solution.py:35
  170.9 3.4 %collective-permute-start.64 = (f32[5,1024]{1,0:T(8,128)S(1)}, f32[5,1024]{1,0:T(8,128)S(1)}, u32[]{:S(2)}, u32[]{:S(2)}) collective-permute-start(f32[5,1024]{1,0:T(8,128)S(1)} %add_add_fusion.1), channel_id=1, source_target_pairs={{0,6},{2,4},{4,2},{6,0},{1,7},{3,5},{5,3},{7,1},{8,14},{10,12},{12... | collective-permute-start | bytes 61448 | tf_op jit(solution)/shard_map/ppermute | solution.py:46
  174.3 5.7 %collective-permute-start.63 = (f32[5,1024]{1,0:T(8,128)S(1)}, f32[5,1024]{1,0:T(8,128)S(1)}, u32[]{:S(2)}, u32[]{:S(2)}) collective-permute-start(f32[5,1024]{1,0:T(8,128)S(1)} %add_add_fusion.1), channel_id=1, source_target_pairs={{0,4},{2,6},{4,0},{6,2},{1,5},{3,7},{5,1},{7,3},{8,12},{10,14},{12... | collective-permute-start | bytes 61448 | tf_op jit(solution)/shard_map/ppermute | solution.py:46
  180.8 1.5 collective-permute-start.52
  182.3 1.5 collective-permute-start.53
  183.8 2.1 %collective-permute-start.48 = (bf16[64,1024]{1,0:T(8,128)(2,1)S(1)}, bf16[64,1024]{1,0:T(8,128)(2,1)S(1)}, u32[]{:S(2)}, u32[]{:S(2)}) collective-permute-start(bf16[64,1024]{1,0:T(8,128)(2,1)S(1)} %get-tuple-element.106), channel_id=1, source_target_pairs={{0,2},{2,4},{4,6},{6,0},{1,3},{3,5},{5,7},{7,1},{8,10},{10,12},{12... | collective-permute-start | bytes 393224 | tf_op jit(solution)/shard_map/ppermute | solution.py:53
  185.9 2.4 %collective-permute-start.50 = (bf16[64,1024]{1,0:T(8,128)(2,1)S(1)}, bf16[64,1024]{1,0:T(8,128)(2,1)S(1)}, u32[]{:S(2)}, u32[]{:S(2)}) collective-permute-start(bf16[64,1024]{1,0:T(8,128)(2,1)S(1)} %get-tuple-element.108), channel_id=1, source_target_pairs={{0,6},{2,0},{4,2},{6,4},{1,7},{3,1},{5,3},{7,5},{8,14},{10,8},{12,... | collective-permute-start | bytes 393224 | tf_op jit(solution)/shard_map/ppermute | solution.py:53
  188.4 3.2 %collective-permute-done.48.refs_1_ = bf16[64,1024]{1,0:T(8,128)(2,1)S(1)} collective-permute-done((bf16[64,1024]{1,0:T(8,128)(2,1)S(1)}, bf16[64,1024]{1,0:T(8,128)(2,1)S(1)}, u32[]{:S(2)}, u32[]{:S(2)}) %collective-permute-start.48) | collective-permute-done | bytes 131104 | tf_op jit(solution)/shard_map/ppermute | solution.py:53
  192.2 3.3 %collective-permute-done.49.refs_2_ = bf16[64,1024]{1,0:T(8,128)(2,1)S(1)} collective-permute-done((bf16[64,1024]{1,0:T(8,128)(2,1)S(1)}, bf16[64,1024]{1,0:T(8,128)(2,1)S(1)}, u32[]{:S(2)}, u32[]{:S(2)}) %collective-permute-start.49) | collective-permute-done | bytes 131104 | tf_op jit(solution)/shard_map/ppermute | solution.py:53
  197.1 1.7 collective-permute-done.54.refs_3_
  198.8 2.3 %shard_map.290 = (f32[32,4,1024]{2,1,0:T(4,128)}, f32[32,4,1024]{2,1,0:T(4,128)}, f32[32,4,1024]{2,1,0:T(4,128)}, f32[32,4,1024]{2,1,0:T(4,128)}) custom-call(f32[4,32,1024]{2,1,0:T(8,128)S(1)} %get-tuple-element.113.refs_0_, bf16[4,32,1024]{2,1,0:T(8,128)(2,1)S(1)} %collective-permute-done.52.refs_1_, ...), custom_call_target="tpu_custom_call" | custom-call | bytes 4980736 | tf_op jit(solution)/shard_map/pallas_call | solution.py:80
  (189 shorter events, 42.6 us)
Async XLA Ops:
  1.6 9.2 %collective-permute-start.2 = (bf16[64,1024]{1,0:T(8,128)(2,1)S(1)}, bf16[64,1024]{1,0:T(8,128)(2,1)S(1)}, u32[]{:S(2)}, u32[]{:S(2)}) collective-permute-start(bf16[64,1024]{1,0:T(8,128)(2,1)S(1)} %dynamic-slice_bitcast_fusion.1.refs_0_.refs_4_), channel_id=1, source_target_pairs={{0,2},{2,4},{4,6},{6,0},{1,3},{3,5},{5,7},{7,1},{8,10},{10,12},{12... | collective-permute-start | bytes 393224 | tf_op jit(solution)/shard_map/ppermute | solution.py:53
  4.7 10.0 %collective-permute-start.3 = (bf16[64,1024]{1,0:T(8,128)(2,1)S(1)}, bf16[64,1024]{1,0:T(8,128)(2,1)S(1)}, u32[]{:S(2)}, u32[]{:S(2)}) collective-permute-start(bf16[64,1024]{1,0:T(8,128)(2,1)S(1)} %dynamic-slice_bitcast_fusion.1.refs_0_.refs_4_), channel_id=1, source_target_pairs={{0,1},{1,0},{2,3},{3,2},{4,5},{5,4},{6,7},{7,6},{8,9},{9,8},{10,11... | collective-permute-start | bytes 393224 | tf_op jit(solution)/shard_map/ppermute | solution.py:46
  4.7 11.2 %collective-permute-start.1 = (bf16[64,1024]{1,0:T(8,128)(2,1)S(1)}, bf16[64,1024]{1,0:T(8,128)(2,1)S(1)}, u32[]{:S(2)}, u32[]{:S(2)}) collective-permute-start(bf16[64,1024]{1,0:T(8,128)(2,1)S(1)} %dynamic-slice_bitcast_fusion.1.refs_0_.refs_4_), channel_id=1, source_target_pairs={{0,4},{2,6},{4,0},{6,2},{1,5},{3,7},{5,1},{7,3},{8,12},{10,14},{12... | collective-permute-start | bytes 393224 | tf_op jit(solution)/shard_map/ppermute | solution.py:53
  7.3 10.1 %collective-permute-start = (bf16[64,1024]{1,0:T(8,128)(2,1)S(1)}, bf16[64,1024]{1,0:T(8,128)(2,1)S(1)}, u32[]{:S(2)}, u32[]{:S(2)}) collective-permute-start(bf16[64,1024]{1,0:T(8,128)(2,1)S(1)} %dynamic-slice_bitcast_fusion.1.refs_0_.refs_4_), channel_id=1, source_target_pairs={{0,6},{2,0},{4,2},{6,4},{1,7},{3,1},{5,3},{7,5},{8,14},{10,8},{12,... | collective-permute-start | bytes 393224 | tf_op jit(solution)/shard_map/ppermute | solution.py:53
  10.9 7.3 %collective-permute-start.6 = (bf16[64,1024]{1,0:T(8,128)(2,1)S(1)}, bf16[64,1024]{1,0:T(8,128)(2,1)S(1)}, u32[]{:S(2)}, u32[]{:S(2)}) collective-permute-start(bf16[64,1024]{1,0:T(8,128)(2,1)S(1)} %collective-permute-done.2.refs_3_), channel_id=1, source_target_pairs={{0,1},{1,0},{2,3},{3,2},{4,5},{5,4},{6,7},{7,6},{8,9},{9,8},{10,11... | collective-permute-start | bytes 393224 | tf_op jit(solution)/shard_map/ppermute | solution.py:46
  12.2 10.2 %collective-permute-start.9 = (bf16[4,32,1024]{2,1,0:T(8,128)(2,1)S(1)}, bf16[4,32,1024]{2,1,0:T(8,128)(2,1)S(1)}, u32[]{:S(2)}, u32[]{:S(2)}) collective-permute-start(bf16[4,32,1024]{2,1,0:T(8,128)(2,1)S(1)} %bitcast.20), channel_id=1, source_target_pairs={{0,24},{8,16},{16,8},{24,0},{1,25},{9,17},{17,9},{25,1},{2,26},{10... | collective-permute-start | bytes 786440 | tf_op jit(solution)/shard_map/ppermute | solution.py:46
  15.4 12.1 %collective-permute-start.8 = (bf16[4,32,1024]{2,1,0:T(8,128)(2,1)S(1)}, bf16[4,32,1024]{2,1,0:T(8,128)(2,1)S(1)}, u32[]{:S(2)}, u32[]{:S(2)}) collective-permute-start(bf16[4,32,1024]{2,1,0:T(8,128)(2,1)S(1)} %bitcast.21), channel_id=1, source_target_pairs={{0,16},{8,24},{16,0},{24,8},{1,17},{9,25},{17,1},{25,9},{2,18},{10... | collective-permute-start | bytes 786440 | tf_op jit(solution)/shard_map/ppermute | solution.py:46
  16.0 11.6 %collective-permute-start.7 = (bf16[4,32,1024]{2,1,0:T(8,128)(2,1)S(1)}, bf16[4,32,1024]{2,1,0:T(8,128)(2,1)S(1)}, u32[]{:S(2)}, u32[]{:S(2)}) collective-permute-start(bf16[4,32,1024]{2,1,0:T(8,128)(2,1)S(1)} %bitcast.22), channel_id=1, source_target_pairs={{0,8},{8,0},{16,24},{24,16},{1,9},{9,1},{17,25},{25,17},{2,10},{10... | collective-permute-start | bytes 786440 | tf_op jit(solution)/shard_map/ppermute | solution.py:46
  39.2 15.8 %collective-permute-start.10 = (bf16[256,1024]{1,0:T(8,128)(2,1)S(1)}, bf16[256,1024]{1,0:T(8,128)(2,1)S(1)}, u32[]{:S(2)}, u32[]{:S(2)}) collective-permute-start(bf16[256,1024]{1,0:T(8,128)(2,1)S(1)} %get-tuple-element.75), channel_id=1, source_target_pairs={{0,1},{1,0},{2,3},{3,2},{4,5},{5,4},{6,7},{7,6},{8,9},{9,8},{10,11... | collective-permute-start | bytes 1572872 | tf_op jit(solution)/shard_map/ppermute | solution.py:46
  39.3 42.5 %collective-permute-start.30 = (bf16[3,144,1024]{2,1,0:T(8,128)(2,1)S(1)}, bf16[3,144,1024]{2,1,0:T(8,128)(2,1)S(1)}, u32[]{:S(2)}, u32[]{:S(2)}) collective-permute-start(bf16[3,144,1024]{2,1,0:T(8,128)(2,1)S(1)} %convert_bitcast_fusion.refs_16_), channel_id=1, source_target_pairs={{0,24},{8,16},{16,8},{24,0},{1,25},{9,17},{17,9},{25,1},{2,26},{10... | collective-permute-start | bytes 2654216 | tf_op jit(solution)/shard_map/ppermute | solution.py:46
  41.7 41.7 %collective-permute-start.29 = (bf16[3,144,1024]{2,1,0:T(8,128)(2,1)S(1)}, bf16[3,144,1024]{2,1,0:T(8,128)(2,1)S(1)}, u32[]{:S(2)}, u32[]{:S(2)}) collective-permute-start(bf16[3,144,1024]{2,1,0:T(8,128)(2,1)S(1)} %convert_bitcast_fusion.refs_16_), channel_id=1, source_target_pairs={{0,16},{8,24},{16,0},{24,8},{1,17},{9,25},{17,1},{25,9},{2,18},{10... | collective-permute-start | bytes 2654216 | tf_op jit(solution)/shard_map/ppermute | solution.py:46
  42.4 8.0 %collective-permute-start.23 = (bf16[64,1024]{1,0:T(8,128)(2,1)S(1)}, bf16[64,1024]{1,0:T(8,128)(2,1)S(1)}, u32[]{:S(2)}, u32[]{:S(2)}) collective-permute-start(bf16[64,1024]{1,0:T(8,128)(2,1)S(1)} %dynamic-slice_bitcast_fusion.refs_8_.refs_6_), channel_id=1, source_target_pairs={{0,2},{2,4},{4,6},{6,0},{1,3},{3,5},{5,7},{7,1},{8,10},{10,12},{12... | collective-permute-start | bytes 393224 | tf_op jit(solution)/shard_map/ppermute | solution.py:53
  47.0 45.9 %collective-permute-start.28 = (bf16[3,144,1024]{2,1,0:T(8,128)(2,1)S(1)}, bf16[3,144,1024]{2,1,0:T(8,128)(2,1)S(1)}, u32[]{:S(2)}, u32[]{:S(2)}) collective-permute-start(bf16[3,144,1024]{2,1,0:T(8,128)(2,1)S(1)} %convert_bitcast_fusion.refs_16_), channel_id=1, source_target_pairs={{0,8},{8,0},{16,24},{24,16},{1,9},{9,1},{17,25},{25,17},{2,10},{10... | collective-permute-start | bytes 2654216 | tf_op jit(solution)/shard_map/ppermute | solution.py:46
  50.4 10.9 %collective-permute-start.22 = (bf16[64,1024]{1,0:T(8,128)(2,1)S(1)}, bf16[64,1024]{1,0:T(8,128)(2,1)S(1)}, u32[]{:S(2)}, u32[]{:S(2)}) collective-permute-start(bf16[64,1024]{1,0:T(8,128)(2,1)S(1)} %dynamic-slice_bitcast_fusion.refs_8_.refs_6_), channel_id=1, source_target_pairs={{0,4},{2,6},{4,0},{6,2},{1,5},{3,7},{5,1},{7,3},{8,12},{10,14},{12... | collective-permute-start | bytes 393224 | tf_op jit(solution)/shard_map/ppermute | solution.py:53
  55.0 7.3 %collective-permute-start.21 = (bf16[64,1024]{1,0:T(8,128)(2,1)S(1)}, bf16[64,1024]{1,0:T(8,128)(2,1)S(1)}, u32[]{:S(2)}, u32[]{:S(2)}) collective-permute-start(bf16[64,1024]{1,0:T(8,128)(2,1)S(1)} %dynamic-slice_bitcast_fusion.refs_8_.refs_6_), channel_id=1, source_target_pairs={{0,6},{2,0},{4,2},{6,4},{1,7},{3,1},{5,3},{7,5},{8,14},{10,8},{12,... | collective-permute-start | bytes 393224 | tf_op jit(solution)/shard_map/ppermute | solution.py:53
  62.2 8.7 %collective-permute-start.11 = (bf16[64,1024]{1,0:T(8,128)(2,1)S(1)}, bf16[64,1024]{1,0:T(8,128)(2,1)S(1)}, u32[]{:S(2)}, u32[]{:S(2)}) collective-permute-start(bf16[64,1024]{1,0:T(8,128)(2,1)S(1)} %get-tuple-element.77), channel_id=1, source_target_pairs={{0,2},{2,4},{4,6},{6,0},{1,3},{3,5},{5,7},{7,1},{8,10},{10,12},{12... | collective-permute-start | bytes 393224 | tf_op jit(solution)/shard_map/ppermute | solution.py:53
  64.4 11.9 %collective-permute-start.12 = (bf16[64,1024]{1,0:T(8,128)(2,1)S(1)}, bf16[64,1024]{1,0:T(8,128)(2,1)S(1)}, u32[]{:S(2)}, u32[]{:S(2)}) collective-permute-start(bf16[64,1024]{1,0:T(8,128)(2,1)S(1)} %get-tuple-element.78), channel_id=1, source_target_pairs={{0,4},{2,6},{4,0},{6,2},{1,5},{3,7},{5,1},{7,3},{8,12},{10,14},{12... | collective-permute-start | bytes 393224 | tf_op jit(solution)/shard_map/ppermute | solution.py:53
  70.9 7.8 %collective-permute-start.13 = (bf16[64,1024]{1,0:T(8,128)(2,1)S(1)}, bf16[64,1024]{1,0:T(8,128)(2,1)S(1)}, u32[]{:S(2)}, u32[]{:S(2)}) collective-permute-start(bf16[64,1024]{1,0:T(8,128)(2,1)S(1)} %get-tuple-element.79), channel_id=1, source_target_pairs={{0,6},{2,0},{4,2},{6,4},{1,7},{3,1},{5,3},{7,5},{8,14},{10,8},{12,... | collective-permute-start | bytes 393224 | tf_op jit(solution)/shard_map/ppermute | solution.py:53
  78.9 8.4 %collective-permute-start.16 = (bf16[64,1024]{1,0:T(8,128)(2,1)S(1)}, bf16[64,1024]{1,0:T(8,128)(2,1)S(1)}, u32[]{:S(2)}, u32[]{:S(2)}) collective-permute-start(bf16[64,1024]{1,0:T(8,128)(2,1)S(1)} %get-tuple-element.80.refs_0_), channel_id=1, source_target_pairs={{0,2},{2,4},{4,6},{6,0},{1,3},{3,5},{5,7},{7,1},{8,10},{10,12},{12... | collective-permute-start | bytes 393224 | tf_op jit(solution)/shard_map/ppermute | solution.py:53
  80.1 12.4 %collective-permute-start.15 = (bf16[64,1024]{1,0:T(8,128)(2,1)S(1)}, bf16[64,1024]{1,0:T(8,128)(2,1)S(1)}, u32[]{:S(2)}, u32[]{:S(2)}) collective-permute-start(bf16[64,1024]{1,0:T(8,128)(2,1)S(1)} %get-tuple-element.80.refs_0_), channel_id=1, source_target_pairs={{0,4},{2,6},{4,0},{6,2},{1,5},{3,7},{5,1},{7,3},{8,12},{10,14},{12... | collective-permute-start | bytes 393224 | tf_op jit(solution)/shard_map/ppermute | solution.py:53
  81.8 10.6 %collective-permute-start.14 = (bf16[64,1024]{1,0:T(8,128)(2,1)S(1)}, bf16[64,1024]{1,0:T(8,128)(2,1)S(1)}, u32[]{:S(2)}, u32[]{:S(2)}) collective-permute-start(bf16[64,1024]{1,0:T(8,128)(2,1)S(1)} %get-tuple-element.80.refs_0_), channel_id=1, source_target_pairs={{0,6},{2,0},{4,2},{6,4},{1,7},{3,1},{5,3},{7,5},{8,14},{10,8},{12,... | collective-permute-start | bytes 393224 | tf_op jit(solution)/shard_map/ppermute | solution.py:53
  83.4 9.6 %collective-permute-start.17 = (bf16[64,1024]{1,0:T(8,128)(2,1)S(1)}, bf16[64,1024]{1,0:T(8,128)(2,1)S(1)}, u32[]{:S(2)}, u32[]{:S(2)}) collective-permute-start(bf16[64,1024]{1,0:T(8,128)(2,1)S(1)} %get-tuple-element.80.refs_0_), channel_id=1, source_target_pairs={{0,1},{1,0},{2,3},{3,2},{4,5},{5,4},{6,7},{7,6},{8,9},{9,8},{10,11... | collective-permute-start | bytes 393224 | tf_op jit(solution)/shard_map/ppermute | solution.py:46
  105.0 7.1 %collective-permute-start.36 = (bf16[256,1024]{1,0:T(8,128)(2,1)S(1)}, bf16[256,1024]{1,0:T(8,128)(2,1)S(1)}, u32[]{:S(2)}, u32[]{:S(2)}) collective-permute-start(bf16[256,1024]{1,0:T(8,128)(2,1)S(1)} %get-tuple-element.91), channel_id=1, source_target_pairs={{0,1},{1,0},{2,3},{3,2},{4,5},{5,4},{6,7},{7,6},{8,9},{9,8},{10,11... | collective-permute-start | bytes 1572872 | tf_op jit(solution)/shard_map/ppermute | solution.py:46
  106.7 8.3 %collective-permute-start.32 = (bf16[64,1024]{1,0:T(8,128)(2,1)S(1)}, bf16[64,1024]{1,0:T(8,128)(2,1)S(1)}, u32[]{:S(2)}, u32[]{:S(2)}) collective-permute-start(bf16[64,1024]{1,0:T(8,128)(2,1)S(1)} %get-tuple-element.86), channel_id=1, source_target_pairs={{0,2},{2,4},{4,6},{6,0},{1,3},{3,5},{5,7},{7,1},{8,10},{10,12},{12... | collective-permute-start | bytes 393224 | tf_op jit(solution)/shard_map/ppermute | solution.py:53
  109.7 11.7 %collective-permute-start.33 = (bf16[64,1024]{1,0:T(8,128)(2,1)S(1)}, bf16[64,1024]{1,0:T(8,128)(2,1)S(1)}, u32[]{:S(2)}, u32[]{:S(2)}) collective-permute-start(bf16[64,1024]{1,0:T(8,128)(2,1)S(1)} %get-tuple-element.87), channel_id=1, source_target_pairs={{0,4},{2,6},{4,0},{6,2},{1,5},{3,7},{5,1},{7,3},{8,12},{10,14},{12... | collective-permute-start | bytes 393224 | tf_op jit(solution)/shard_map/ppermute | solution.py:53
  109.8 12.1 %collective-permute-start.34 = (bf16[64,1024]{1,0:T(8,128)(2,1)S(1)}, bf16[64,1024]{1,0:T(8,128)(2,1)S(1)}, u32[]{:S(2)}, u32[]{:S(2)}) collective-permute-start(bf16[64,1024]{1,0:T(8,128)(2,1)S(1)} %get-tuple-element.88), channel_id=1, source_target_pairs={{0,6},{2,0},{4,2},{6,4},{1,7},{3,1},{5,3},{7,5},{8,14},{10,8},{12,... | collective-permute-start | bytes 393224 | tf_op jit(solution)/shard_map/ppermute | solution.py:53
  112.2 11.3 %collective-permute-start.37 = (bf16[64,1024]{1,0:T(8,128)(2,1)S(1)}, bf16[64,1024]{1,0:T(8,128)(2,1)S(1)}, u32[]{:S(2)}, u32[]{:S(2)}) collective-permute-start(bf16[64,1024]{1,0:T(8,128)(2,1)S(1)} %get-tuple-element.93), channel_id=1, source_target_pairs={{0,2},{2,4},{4,6},{6,0},{1,3},{3,5},{5,7},{7,1},{8,10},{10,12},{12... | collective-permute-start | bytes 393224 | tf_op jit(solution)/shard_map/ppermute | solution.py:53
  112.3 19.0 %collective-permute-start.38 = (bf16[64,1024]{1,0:T(8,128)(2,1)S(1)}, bf16[64,1024]{1,0:T(8,128)(2,1)S(1)}, u32[]{:S(2)}, u32[]{:S(2)}) collective-permute-start(bf16[64,1024]{1,0:T(8,128)(2,1)S(1)} %get-tuple-element.94), channel_id=1, source_target_pairs={{0,4},{2,6},{4,0},{6,2},{1,5},{3,7},{5,1},{7,3},{8,12},{10,14},{12... | collective-permute-start | bytes 393224 | tf_op jit(solution)/shard_map/ppermute | solution.py:53
  115.0 16.3 %collective-permute-start.39 = (bf16[64,1024]{1,0:T(8,128)(2,1)S(1)}, bf16[64,1024]{1,0:T(8,128)(2,1)S(1)}, u32[]{:S(2)}, u32[]{:S(2)}) collective-permute-start(bf16[64,1024]{1,0:T(8,128)(2,1)S(1)} %get-tuple-element.95), channel_id=1, source_target_pairs={{0,6},{2,0},{4,2},{6,4},{1,7},{3,1},{5,3},{7,5},{8,14},{10,8},{12,... | collective-permute-start | bytes 393224 | tf_op jit(solution)/shard_map/ppermute | solution.py:53
  121.4 35.6 %collective-permute-start.55 = (bf16[3,144,1024]{2,1,0:T(8,128)(2,1)}, bf16[3,144,1024]{2,1,0:T(8,128)(2,1)}, u32[]{:S(2)}, u32[]{:S(2)}) collective-permute-start(bf16[3,144,1024]{2,1,0:T(8,128)(2,1)} %get-tuple-element.123), channel_id=1, source_target_pairs={{0,8},{8,0},{16,24},{24,16},{1,9},{9,1},{17,25},{25,17},{2,10},{10... | collective-permute-start | bytes 2654216 | tf_op jit(solution)/shard_map/ppermute | solution.py:46
  122.0 35.6 %collective-permute-start.56 = (bf16[3,144,1024]{2,1,0:T(8,128)(2,1)}, bf16[3,144,1024]{2,1,0:T(8,128)(2,1)}, u32[]{:S(2)}, u32[]{:S(2)}) collective-permute-start(bf16[3,144,1024]{2,1,0:T(8,128)(2,1)} %get-tuple-element.124), channel_id=1, source_target_pairs={{0,16},{8,24},{16,0},{24,8},{1,17},{9,25},{17,1},{25,9},{2,18},{10... | collective-permute-start | bytes 2654216 | tf_op jit(solution)/shard_map/ppermute | solution.py:46
  123.5 40.5 %collective-permute-start.57 = (bf16[3,144,1024]{2,1,0:T(8,128)(2,1)}, bf16[3,144,1024]{2,1,0:T(8,128)(2,1)}, u32[]{:S(2)}, u32[]{:S(2)}) collective-permute-start(bf16[3,144,1024]{2,1,0:T(8,128)(2,1)} %get-tuple-element.125), channel_id=1, source_target_pairs={{0,24},{8,16},{16,8},{24,0},{1,25},{9,17},{17,9},{25,1},{2,26},{10... | collective-permute-start | bytes 2654216 | tf_op jit(solution)/shard_map/ppermute | solution.py:46
  132.6 8.7 %collective-permute-start.42 = (bf16[64,1024]{1,0:T(8,128)(2,1)S(1)}, bf16[64,1024]{1,0:T(8,128)(2,1)S(1)}, u32[]{:S(2)}, u32[]{:S(2)}) collective-permute-start(bf16[64,1024]{1,0:T(8,128)(2,1)S(1)} %get-tuple-element.97.refs_0_), channel_id=1, source_target_pairs={{0,2},{2,4},{4,6},{6,0},{1,3},{3,5},{5,7},{7,1},{8,10},{10,12},{12... | collective-permute-start | bytes 393224 | tf_op jit(solution)/shard_map/ppermute | solution.py:53
  135.0 11.5 %collective-permute-start.41 = (bf16[64,1024]{1,0:T(8,128)(2,1)S(1)}, bf16[64,1024]{1,0:T(8,128)(2,1)S(1)}, u32[]{:S(2)}, u32[]{:S(2)}) collective-permute-start(bf16[64,1024]{1,0:T(8,128)(2,1)S(1)} %get-tuple-element.97.refs_0_), channel_id=1, source_target_pairs={{0,4},{2,6},{4,0},{6,2},{1,5},{3,7},{5,1},{7,3},{8,12},{10,14},{12... | collective-permute-start | bytes 393224 | tf_op jit(solution)/shard_map/ppermute | solution.py:53
  141.3 7.1 %collective-permute-start.40 = (bf16[64,1024]{1,0:T(8,128)(2,1)S(1)}, bf16[64,1024]{1,0:T(8,128)(2,1)S(1)}, u32[]{:S(2)}, u32[]{:S(2)}) collective-permute-start(bf16[64,1024]{1,0:T(8,128)(2,1)S(1)} %get-tuple-element.97.refs_0_), channel_id=1, source_target_pairs={{0,6},{2,0},{4,2},{6,4},{1,7},{3,1},{5,3},{7,5},{8,14},{10,8},{12,... | collective-permute-start | bytes 393224 | tf_op jit(solution)/shard_map/ppermute | solution.py:53
  155.3 27.0 %collective-permute-start.47 = (bf16[256,1024]{1,0:T(8,128)(2,1)S(1)}, bf16[256,1024]{1,0:T(8,128)(2,1)S(1)}, u32[]{:S(2)}, u32[]{:S(2)}) collective-permute-start(bf16[256,1024]{1,0:T(8,128)(2,1)S(1)} %get-tuple-element.104), channel_id=1, source_target_pairs={{0,1},{1,0},{2,3},{3,2},{4,5},{5,4},{6,7},{7,6},{8,9},{9,8},{10,11... | collective-permute-start | bytes 1572872 | tf_op jit(solution)/shard_map/ppermute | solution.py:46
  155.5 15.4 %collective-permute-start.61 = (f32[5,1024]{1,0:T(8,128)S(1)}, f32[5,1024]{1,0:T(8,128)S(1)}, u32[]{:S(2)}, u32[]{:S(2)}) collective-permute-start(f32[5,1024]{1,0:T(8,128)S(1)} %add.92), channel_id=1, source_target_pairs={{0,24},{8,16},{16,8},{24,0},{1,25},{9,17},{17,9},{25,1},{2,26},{10... | collective-permute-start | bytes 61448 | tf_op jit(solution)/shard_map/ppermute | solution.py:46
  157.0 13.9 %collective-permute-start.60 = (f32[5,1024]{1,0:T(8,128)S(1)}, f32[5,1024]{1,0:T(8,128)S(1)}, u32[]{:S(2)}, u32[]{:S(2)}) collective-permute-start(f32[5,1024]{1,0:T(8,128)S(1)} %add.92), channel_id=1, source_target_pairs={{0,16},{8,24},{16,0},{24,8},{1,17},{9,25},{17,1},{25,9},{2,18},{10... | collective-permute-start | bytes 61448 | tf_op jit(solution)/shard_map/ppermute | solution.py:46
  157.6 13.2 %collective-permute-start.59 = (f32[5,1024]{1,0:T(8,128)S(1)}, f32[5,1024]{1,0:T(8,128)S(1)}, u32[]{:S(2)}, u32[]{:S(2)}) collective-permute-start(f32[5,1024]{1,0:T(8,128)S(1)} %add.92), channel_id=1, source_target_pairs={{0,8},{8,0},{16,24},{24,16},{1,9},{9,1},{17,25},{25,17},{2,10},{10... | collective-permute-start | bytes 61448 | tf_op jit(solution)/shard_map/ppermute | solution.py:46
  170.9 13.0 %collective-permute-start.64 = (f32[5,1024]{1,0:T(8,128)S(1)}, f32[5,1024]{1,0:T(8,128)S(1)}, u32[]{:S(2)}, u32[]{:S(2)}) collective-permute-start(f32[5,1024]{1,0:T(8,128)S(1)} %add_add_fusion.1), channel_id=1, source_target_pairs={{0,6},{2,4},{4,2},{6,0},{1,7},{3,5},{5,3},{7,1},{8,14},{10,12},{12... | collective-permute-start | bytes 61448 | tf_op jit(solution)/shard_map/ppermute | solution.py:46
  174.3 11.7 %collective-permute-start.63 = (f32[5,1024]{1,0:T(8,128)S(1)}, f32[5,1024]{1,0:T(8,128)S(1)}, u32[]{:S(2)}, u32[]{:S(2)}) collective-permute-start(f32[5,1024]{1,0:T(8,128)S(1)} %add_add_fusion.1), channel_id=1, source_target_pairs={{0,4},{2,6},{4,0},{6,2},{1,5},{3,7},{5,1},{7,3},{8,12},{10,14},{12... | collective-permute-start | bytes 61448 | tf_op jit(solution)/shard_map/ppermute | solution.py:46
  180.0 6.0 %collective-permute-start.62 = (f32[5,1024]{1,0:T(8,128)S(1)}, f32[5,1024]{1,0:T(8,128)S(1)}, u32[]{:S(2)}, u32[]{:S(2)}) collective-permute-start(f32[5,1024]{1,0:T(8,128)S(1)} %add_add_fusion.1), channel_id=1, source_target_pairs={{0,2},{2,0},{4,6},{6,4},{1,3},{3,1},{5,7},{7,5},{8,10},{10,8},{12,... | collective-permute-start | bytes 61448 | tf_op jit(solution)/shard_map/ppermute | solution.py:46
  180.8 16.3 %collective-permute-start.52 = (bf16[4,32,1024]{2,1,0:T(8,128)(2,1)S(1)}, bf16[4,32,1024]{2,1,0:T(8,128)(2,1)S(1)}, u32[]{:S(2)}, u32[]{:S(2)}) collective-permute-start(bf16[4,32,1024]{2,1,0:T(8,128)(2,1)S(1)} %get-tuple-element.114), channel_id=1, source_target_pairs={{0,8},{8,0},{16,24},{24,16},{1,9},{9,1},{17,25},{25,17},{2,10},{10... | collective-permute-start | bytes 786440 | tf_op jit(solution)/shard_map/ppermute | solution.py:46
  182.3 14.8 %collective-permute-start.53 = (bf16[4,32,1024]{2,1,0:T(8,128)(2,1)S(1)}, bf16[4,32,1024]{2,1,0:T(8,128)(2,1)S(1)}, u32[]{:S(2)}, u32[]{:S(2)}) collective-permute-start(bf16[4,32,1024]{2,1,0:T(8,128)(2,1)S(1)} %get-tuple-element.115), channel_id=1, source_target_pairs={{0,16},{8,24},{16,0},{24,8},{1,17},{9,25},{17,1},{25,9},{2,18},{10... | collective-permute-start | bytes 786440 | tf_op jit(solution)/shard_map/ppermute | solution.py:46
  183.8 7.7 %collective-permute-start.48 = (bf16[64,1024]{1,0:T(8,128)(2,1)S(1)}, bf16[64,1024]{1,0:T(8,128)(2,1)S(1)}, u32[]{:S(2)}, u32[]{:S(2)}) collective-permute-start(bf16[64,1024]{1,0:T(8,128)(2,1)S(1)} %get-tuple-element.106), channel_id=1, source_target_pairs={{0,2},{2,4},{4,6},{6,0},{1,3},{3,5},{5,7},{7,1},{8,10},{10,12},{12... | collective-permute-start | bytes 393224 | tf_op jit(solution)/shard_map/ppermute | solution.py:53
  185.9 9.5 %collective-permute-start.49 = (bf16[64,1024]{1,0:T(8,128)(2,1)S(1)}, bf16[64,1024]{1,0:T(8,128)(2,1)S(1)}, u32[]{:S(2)}, u32[]{:S(2)}) collective-permute-start(bf16[64,1024]{1,0:T(8,128)(2,1)S(1)} %get-tuple-element.107), channel_id=1, source_target_pairs={{0,4},{2,6},{4,0},{6,2},{1,5},{3,7},{5,1},{7,3},{8,12},{10,14},{12... | collective-permute-start | bytes 393224 | tf_op jit(solution)/shard_map/ppermute | solution.py:53
  185.9 9.5 %collective-permute-start.50 = (bf16[64,1024]{1,0:T(8,128)(2,1)S(1)}, bf16[64,1024]{1,0:T(8,128)(2,1)S(1)}, u32[]{:S(2)}, u32[]{:S(2)}) collective-permute-start(bf16[64,1024]{1,0:T(8,128)(2,1)S(1)} %get-tuple-element.108), channel_id=1, source_target_pairs={{0,6},{2,0},{4,2},{6,4},{1,7},{3,1},{5,3},{7,5},{8,14},{10,8},{12,... | collective-permute-start | bytes 393224 | tf_op jit(solution)/shard_map/ppermute | solution.py:53
  191.5 7.3 %collective-permute-start.54 = (bf16[4,32,1024]{2,1,0:T(8,128)(2,1)S(1)}, bf16[4,32,1024]{2,1,0:T(8,128)(2,1)S(1)}, u32[]{:S(2)}, u32[]{:S(2)}) collective-permute-start(bf16[4,32,1024]{2,1,0:T(8,128)(2,1)S(1)} %get-tuple-element.116), channel_id=1, source_target_pairs={{0,24},{8,16},{16,8},{24,0},{1,25},{9,17},{17,9},{25,1},{2,26},{10... | collective-permute-start | bytes 786440 | tf_op jit(solution)/shard_map/ppermute | solution.py:46
  (55 other events, 315.0 us)
where the time goes:
time: 203 us; the launch traced here: 202 us
  starting transfers between devices  84.2 us (41%)
  waiting for transfers between devices  63.1 us (31%)
  Pallas kernels  26.1 us (13%)
  local copies, waits for them, and re-layouts  16.7 us (8%)
  other arithmetic  10.9 us (5%)
    ppermute x24, waiting for transfers between devices, send_up(): lax.ppermute(value, axis, [(i, (i + steps) % count) for i in range(count)])  52.7 us
    ppermute x24, starting transfers between devices, send_up(): lax.ppermute(value, axis, [(i, (i + steps) % count) for i in range(count)])  47.9 us
    ppermute x41, starting transfers between devices, swap_with(): lax.ppermute(value, axis, [(i, partner_of(i, step, count)) for i in range...  36.2 us
    pallas_call x15, Pallas kernels, in_vmem(): pl.pallas_call(body, out_shape=shapes, in_specs=specs, out_specs=[pl.Bloc...  26.1 us
    unnamed x77, local copies, waits for them, and re-layouts  15.9 us
    ppermute x41, waiting for transfers between devices, swap_with(): lax.ppermute(value, axis, [(i, partner_of(i, step, count)) for i in range...  10.4 us
    sub x3, other arithmetic, adam_update(): weight - rate * (first_hat / (jnp.sqrt(second_hat) + adam_eps) + decay *...  8.09 us
  transfers between devices with their start and end apart: 65, of which 28 were waited for; matrix products, arithmetic and copies ran while one was open for 6% of the time, Pallas kernels for 6%

commit v1 on v0

v1 whole, which is shorter than its diff:
```python
import functools

import jax
import jax.numpy as jnp
from jax import lax
from jax.experimental import pallas as pl
from jax.experimental.pallas import tpu as pltpu
from jax.sharding import PartitionSpec as P


STEP = 10


norm_eps = 1e-05
beta_first = 0.9
beta_second = 0.999
adam_eps = 1e-08
matrix_rate = 0.02
small_rate = 0.25
decay_rate = 0.1
small_rows = 8

bf16 = jnp.bfloat16
f32 = jnp.float32


def norm_backward(grad_normed, normed, scale):
    return scale * (grad_normed - normed * jnp.mean(grad_normed * normed, axis=-1, keepdims=True))


def adam_update(weight, gradient, first, second, rate, decay):
    first_new = beta_first * first + (1.0 - beta_first) * gradient
    second_new = beta_second * second + (1.0 - beta_second) * gradient * gradient
    first_hat = first_new / (1.0 - beta_first**STEP)
    second_hat = second_new / (1.0 - beta_second**STEP)
    weight_new = weight - rate * (first_hat / (jnp.sqrt(second_hat) + adam_eps) + decay * weight)
    return (weight_new, first_new, second_new)


def partner_of(index, step, count):
    assert count & (count - 1) == 0
    return index ^ step


def swap_with(value, axis, step):
    count = lax.axis_size(axis)
    return lax.ppermute(
        value, axis, [(i, partner_of(i, step, count)) for i in range(count)]
    )


def tree_sum(values):
    while len(values) > 1:
        values = [a + b for a, b in zip(values[::2], values[1::2])]
    return values[0]


def across_shard(halves):
    count = lax.axis_size("shard")
    pieces = [list(halves)]
    for k in range(1, count):
        low, high = k & -k, 1 << (k.bit_length() - 1)
        pieces.append(
            [swap_with(pieces[k ^ via][j], "shard", via) for j, via in enumerate((low, high))]
        )
    return pieces


def spread_rows(own):
    count = lax.axis_size("ctx")
    mine = [own]
    for k in range(1, count):
        if k == 1 or k % 2 == 0:
            mine.append(swap_with(own, "ctx", k))
        else:
            mine.append(swap_with(mine[k - 1], "ctx", 1))
    return mine + [swap_with(piece, "tp", 1) for piece in mine]


def in_vmem(body, outs, *operands, scratch=(), flops=0, mib=16):
    shapes = [jax.ShapeDtypeStruct(shape, dtype) for shape, dtype in outs]
    moved = sum(x.size * x.dtype.itemsize for x in (*operands, *shapes))
    return pl.pallas_call(
        body,
        out_shape=shapes,
        in_specs=[pl.BlockSpec(memory_space=pltpu.VMEM)] * len(operands),
        out_specs=[pl.BlockSpec(memory_space=pltpu.VMEM)] * len(shapes),
        scratch_shapes=list(scratch),
        compiler_params=pltpu.CompilerParams(vmem_limit_bytes=mib << 20),
        cost_estimate=pl.CostEstimate(flops=flops, bytes_accessed=moved, transcendentals=0),
    )(*operands)


def by_rows(rows, weight):
    return lax.dot_general(rows, weight, (((1,), (1,)), ((), ())), preferred_element_type=f32)


def down_rows(left, right):
    return lax.dot_general(left, right, (((0,), (0,)), ((), ())), preferred_element_type=f32)


def block_start(step, core, rows):
    return pl.multiple_of((2 * jnp.bitwise_xor(lax.axis_index("ctx"), step) + core) * rows, rows)


def delayed(values, steps):
    length = values.shape[0]
    rolled = pltpu.roll(values, steps % length, 0)
    row = lax.broadcasted_iota(jnp.int32, values.shape, 0)
    kept = row >= steps if steps > 0 else row < length + steps
    return jnp.where(kept, rolled, 0.0)


def convolved(b_part, x_part, taps):
    product = b_part * x_part
    one, two = delayed(product, 1), delayed(product, 2)
    return product, one, two, taps[0:1] * two + taps[1:2] * one + taps[2:3] * product


def own_columns(groups, block, shape):
    row = lax.broadcasted_iota(jnp.int32, shape, 0)
    ahead = lax.broadcasted_iota(jnp.int32, shape, 1) - row
    stride = shape[1] // groups
    found = jnp.zeros(shape, f32)
    group_at = lax.axis_index("shard")
    within = lax.axis_index("ctx") * lax.axis_size("tp") + lax.axis_index("tp")
    for k in range(groups):
        base = jnp.bitwise_xor(group_at, k) * stride + (within - k) * block
        inside = (row >= k * block) & (row < (k + 1) * block)
        found = jnp.where(inside & (ahead == base), 1.0, found)
    return found


def mixer_forward(count, groups, *refs):
    pieces, parts = refs[: 2 * count], refs[2 * count : 2 * count + groups]
    gain_ref, conv_ref, h_ref, w_ref, p_ref, y_ref, taps_ref, keep_ref, send_ref = refs[
        2 * count + groups :
    ]
    rows = pieces[0].shape[0]
    block, channels = parts[0].shape[1], y_ref.shape[1]
    core = lax.axis_index("tp")
    taps_ref[...] = lax.dot_general(
        conv_ref[...],
        own_columns(groups, block, (channels, conv_ref.shape[1])),
        (((1,), (1,)), ((), ())),
        precision=lax.Precision.HIGHEST,
        preferred_element_type=f32,
    )
    for k in range(4):
        for s in range(groups):
            w_ref[k * channels + s * block : k * channels + (s + 1) * block, :] = parts[s][k]
    gain = gain_ref[0:1, :]
    for j in range(2 * count):
        x = pieces[j][...].astype(f32)
        scale = lax.rsqrt(jnp.mean(x * x, axis=-1, keepdims=True) + norm_eps)
        side = core if j < count else 1 - core
        h_ref[pl.ds(block_start(j % count, side, rows), rows), :] = (x * scale * gain).astype(bf16)
    p_ref[...] = by_rows(h_ref[...], w_ref[: 3 * channels, :])
    in_b, in_c = p_ref[:, :channels], p_ref[:, channels : 2 * channels]
    in_x = p_ref[:, 2 * channels :]
    mixed = convolved(in_b, in_x, taps_ref[...])[3]
    y_ref[...] = (in_c * mixed).astype(bf16)
    out_w = w_ref[3 * channels :, :]
    for side, out_ref in ((1 - core, send_ref), (core, keep_ref)):
        starts = [block_start(k, side, rows) for k in range(count)]
        rows_of = [y_ref[pl.ds(at, rows), :] for at in starts]
        part = jnp.dot(jnp.concatenate(rows_of, axis=0), out_w, preferred_element_type=f32)
        out_ref[...] = part.astype(out_ref.dtype)


def halves_of(values):
    coarse = values.astype(bf16)
    return coarse, (values - coarse.astype(f32)).astype(bf16)


def whole_of(ref, at):
    rows = small_rows
    return ref[at : at + rows, :].astype(f32) + ref[at + rows : at + 2 * rows, :].astype(f32)


def mixer_backward(count, groups, *refs):
    pieces = refs[: 2 * count]
    h_ref, w_ref, p_ref, gain_ref, taps_ref, gain_two_ref = refs[2 * count : 2 * count + 6]
    dm_ref, dp_ref, keep_ref, send_ref, small_ref = refs[2 * count + 6 :]
    rows, side_rows = pieces[0].shape[0], count * pieces[0].shape[0]
    channels = taps_ref.shape[1]
    core = lax.axis_index("tp")
    for j in range(2 * count):
        side = core if j < count else 1 - core
        dm_ref[pl.ds(block_start(j % count, side, rows), rows), :] = pieces[j][...]
    grad_gated = by_rows(dm_ref[...], w_ref[3 * channels :, :])
    in_b, in_c = p_ref[:, :channels], p_ref[:, channels : 2 * channels]
    in_x = p_ref[:, 2 * channels :]
    taps = taps_ref[...]
    product, one, two, mixed = convolved(in_b, in_x, taps)
    grad_mixed = grad_gated * in_c
    next_one, next_two = delayed(grad_mixed, -1), delayed(grad_mixed, -2)
    grad_prod = taps[0:1] * next_two + taps[1:2] * next_one + taps[2:3] * grad_mixed
    dp_ref[:, :channels] = (grad_prod * in_x).astype(bf16)
    dp_ref[:, channels : 2 * channels] = (grad_gated * mixed).astype(bf16)
    dp_ref[:, 2 * channels :] = (grad_prod * in_b).astype(bf16)
    tap_sums = [
        jnp.sum(grad_mixed * shifted, axis=0, keepdims=True) for shifted in (two, one, product)
    ]
    small_ref[...] = jnp.zeros(small_ref.shape, f32)
    small_ref[2:5, :] = jnp.dot(
        jnp.concatenate(tap_sums, axis=0),
        own_columns(groups, channels // groups, (channels, h_ref.shape[1])),
        precision=lax.Precision.HIGHEST,
        preferred_element_type=f32,
    )
    small_ref[1:2, :] = gain_two_ref[...]
    gain_sum = jnp.zeros((1, gain_ref.shape[1]), f32)
    for side, out_ref in ((1 - core, send_ref), (core, keep_ref)):
        starts = [block_start(k, side, rows) for k in range(count)]
        grads = jnp.concatenate([dp_ref[pl.ds(at, rows), :] for at in starts], axis=0)
        part = jnp.dot(grads, w_ref[: 3 * channels, :], preferred_element_type=f32)
        out_ref[:side_rows, :] = part.astype(out_ref.dtype)
        normed = jnp.concatenate([h_ref[pl.ds(at, rows), :] for at in starts], axis=0)
        gain_sum = gain_sum + jnp.sum(part * normed.astype(f32), axis=0, keepdims=True)
    small_ref[0:1, :] = gain_sum / gain_ref[0:1, :]
    coarse, fine = halves_of(small_ref[...])
    send_ref[side_rows:, :] = jnp.concatenate([coarse, fine], axis=0)
    keep_ref[side_rows:, :] = coarse.astype(f32) + fine.astype(f32)


def mixer_weight_grads(groups, dp_ref, h_ref, y_ref, dm_ref, *outs):
    block = outs[0].shape[1]
    channels = y_ref.shape[1]
    inner = down_rows(dp_ref[...], h_ref[...])
    outer = down_rows(y_ref[...], dm_ref[...])
    for s in range(groups):
        for k in range(3):
            at = k * channels + s * block
            outs[s][k] = inner[at : at + block].astype(outs[s].dtype)
        outs[s][3] = outer[s * block : (s + 1) * block].astype(outs[s].dtype)


def ffn_gather(count, *refs):
    *pieces, g_ref, w_ref, down_ref = refs
    g_pieces, parts = pieces[: 2 * count], pieces[2 * count :]
    rows, hidden = g_pieces[0].shape[0], down_ref.shape[0]
    for j in range(2 * count):
        g_ref[j * rows : (j + 1) * rows, :] = g_pieces[j][...]
    block, columns = parts[0].shape[1:]
    for j, part in enumerate(parts):
        at, side = (j // 2) * block, slice((j % 2) * columns, (j % 2 + 1) * columns)
        w_ref[at : at + block, side] = part[0]
        w_ref[hidden + at : hidden + at + block, side] = part[1]
        down_ref[at : at + block, side] = part[2]


def ffn_rows(count, *refs):
    pieces = refs[: 2 * count]
    g_ref, w_ref, down_ref, h_ref, act_ref, gate_ref, up_ref, keep_ref, send_ref = refs[2 * count :]
    rows, hidden = pieces[0].shape[0], down_ref.shape[0]
    for j in range(2 * count):
        h_ref[j * rows : (j + 1) * rows, :] = pieces[j][...]
    side_rows = count * rows
    for at, out_ref in ((side_rows, send_ref), (0, keep_ref)):
        these = slice(at, at + side_rows)
        gate = by_rows(h_ref[these, :], w_ref[:hidden, :])
        up = by_rows(h_ref[these, :], w_ref[hidden:, :])
        sigmoid = jax.nn.sigmoid(gate)
        gate_act = gate * sigmoid
        act_ref[these, :] = (gate_act * up).astype(bf16)
        grad_act = by_rows(g_ref[these, :], down_ref[...])
        up_ref[these, :] = (grad_act * gate_act).astype(bf16)
        gate_ref[these, :] = (
            grad_act * up * sigmoid * (1.0 + gate * (1.0 - sigmoid))
        ).astype(bf16)
        part = jnp.dot(gate_ref[these, :], w_ref[:hidden, :], preferred_element_type=f32)
        part = part + jnp.dot(up_ref[these, :], w_ref[hidden:, :], preferred_element_type=f32)
        out_ref[...] = part.astype(out_ref.dtype)


def ffn_down(act_ref, down_ref, keep_ref, send_ref):
    half = keep_ref.shape[0]
    for at, out_ref in ((half, send_ref), (0, keep_ref)):
        part = jnp.dot(act_ref[at : at + half, :], down_ref[...], preferred_element_type=f32)
        out_ref[...] = part.astype(out_ref.dtype)


def ffn_weight_grads(groups, gate_ref, up_ref, act_ref, h_ref, g_ref, *outs):
    block = outs[0].shape[1]
    for k, (left, right) in enumerate(((gate_ref, h_ref), (up_ref, h_ref), (act_ref, g_ref))):
        term = down_rows(left[...], right[...])
        for s in range(groups):
            outs[s][k] = term[s * block : (s + 1) * block].astype(outs[s].dtype)


def ffn_adam(groups, *refs):
    own_ref, *parts = refs[:groups]
    weight, first, second, grad_out, *outs = refs[groups:]
    for k in range(3):
        grad = own_ref[k]
        for part in parts:
            grad = grad + part[k].astype(f32)
        grad_out[k] = grad
        news = adam_update(weight[k], grad, first[k], second[k], matrix_rate, decay_rate)
        for out, new in zip(outs, news):
            out[k] = new


def mixer_adam(groups, *refs):
    own_ref, *parts = refs[:groups]
    weight, first, second, grad_out, weight_out, first_out, second_out = refs[groups:]
    for k in range(4):
        grad = own_ref[k]
        for part in parts:
            grad = grad + part[k].astype(f32)
        news = adam_update(
            weight[:, k, :], grad, first[:, k, :], second[:, k, :], matrix_rate, decay_rate
        )
        grad_out[:, k, :] = grad
        for out, new in zip((weight_out, first_out, second_out), news):
            out[:, k, :] = new


def pair_kernel(kept_ref, got_ref, *outs):
    rows = outs[0].shape[0]
    for k, out_ref in enumerate(outs):
        at = slice(k * rows, (k + 1) * rows)
        out_ref[...] = (kept_ref[at, :] + got_ref[at, :].astype(f32)).astype(out_ref.dtype)


def pair_with_small(kept_ref, got_ref, *outs):
    rows = outs[0].shape[0] - small_rows
    count = len(outs)
    small = kept_ref[count * rows :, :] + whole_of(got_ref, count * rows)
    coarse, fine = halves_of(small)
    for k, out_ref in enumerate(outs):
        at = slice(k * rows, (k + 1) * rows)
        pair = kept_ref[at, :] + got_ref[at, :].astype(f32)
        out_ref[:rows, :] = pair.astype(out_ref.dtype)
        if k == 0:
            out_ref[rows:, :] = coarse.astype(f32) + fine.astype(f32)
        else:
            out_ref[rows:, :] = jnp.concatenate([coarse, fine], axis=0)


def total_of(own_ref, got_refs, rows=None):
    total = own_ref[:rows, :]
    for got in got_refs:
        total = total + got[:rows, :].astype(f32)
    return total


def own_rows(rows_ref, out_ref):
    count = out_ref.shape[0]
    start = pl.multiple_of(lax.axis_index("tp") * count, count)
    out_ref[...] = rows_ref[0, pl.ds(start, count), :]


def join_rows(mine_ref, other_ref, out_ref):
    count, core = mine_ref.shape[0], lax.axis_index("tp")
    out_ref[0, pl.ds(pl.multiple_of(core * count, count), count), :] = mine_ref[...]
    out_ref[0, pl.ds(pl.multiple_of((1 - core) * count, count), count), :] = other_ref[...]


def prepare_ffn(weight_ref, *outs):
    columns = outs[0].shape[2]
    for j, out_ref in enumerate(outs):
        out_ref[...] = weight_ref[:, :, j * columns : (j + 1) * columns].astype(bf16)


def prepare_mixer(weight_ref, out_ref):
    for k in range(4):
        out_ref[k] = weight_ref[:, k, :].astype(bf16)


def second_norm(*refs):
    own_ref, *got = refs[:-5]
    x_ref, gain_ref, resid_ref, normed_ref, h_ref = refs[-5:]
    residual = x_ref[...].astype(f32) + total_of(own_ref, got)
    resid_ref[...] = residual
    normed = residual * lax.rsqrt(jnp.mean(residual * residual, axis=-1, keepdims=True) + norm_eps)
    normed_ref[...] = normed
    h_ref[...] = (normed * gain_ref[1:2, :]).astype(bf16)


def second_norm_backward(*refs):
    own_ref, *got = refs[:-7]
    resid_ref, normed_ref, g_ref, gain_ref, grad_ref, dm_ref, gain_part_ref = refs[-7:]
    grad_h = total_of(own_ref, got)
    normed, residual = normed_ref[...], resid_ref[...]
    scale = lax.rsqrt(jnp.mean(residual * residual, axis=-1, keepdims=True) + norm_eps)
    grad = g_ref[...].astype(f32) + norm_backward(grad_h * gain_ref[1:2, :], normed, scale)
    grad_ref[...] = grad
    dm_ref[...] = grad.astype(bf16)
    gain_part_ref[...] = jnp.sum(grad_h * normed, axis=0, keepdims=True)


def first_norm_backward(*refs):
    own_ref, *got = refs[:-5]
    x_ref, grad_ref, gain_ref, out_ref, small_ref = refs[-5:]
    rows = x_ref.shape[0]
    x = x_ref[...].astype(f32)
    scale = lax.rsqrt(jnp.mean(x * x, axis=-1, keepdims=True) + norm_eps)
    out_ref[...] = grad_ref[...] + norm_backward(
        total_of(own_ref, got, rows) * gain_ref[0:1, :], x * scale, scale
    )
    small_ref[...] = tree_sum([own_ref[rows:, :]] + [whole_of(ref, rows) for ref in got])


def small_adam(groups, *refs):
    pieces, operands, outs = refs[:groups], refs[groups : groups + 6], refs[groups + 6 :]
    total = tree_sum([piece[...] for piece in pieces])
    for which, grad in enumerate((total[0:2], total[2:5])):
        weight, first, second = (ref[...] for ref in operands[3 * which : 3 * which + 3])
        news = adam_update(weight, grad, first, second, small_rate, 0.0)
        for out, value in zip(outs[4 * which : 4 * which + 4], (grad, *news)):
            out[...] = value


def output_kernel(*refs):
    own_ref, *got = refs[:-2]
    resid_ref, out_ref = refs[-2:]
    out_ref[...] = (resid_ref[...] + total_of(own_ref, got)).astype(out_ref.dtype)


def collect_rows(kept, sent, small=False):
    count = lax.axis_size("ctx")
    width = kept.shape[1]
    rows = (kept.shape[0] - small_rows * small) // count
    outs = [((rows + small_rows * small, width), f32)]
    outs += [((rows + 2 * small_rows * small, width), bf16)] * (count - 1)
    got = swap_with(sent, "tp", 1)
    pieces = in_vmem(pair_with_small if small else pair_kernel, outs, kept, got)
    return [pieces[0]] + [swap_with(pieces[k], "ctx", k) for k in range(1, count)]


def per_device(
    inputs,
    cotangent,
    mixer_matrix,
    ffn_weight,
    conv_weight,
    norm_gains,
    mixer_first,
    mixer_second,
    ffn_first,
    ffn_second,
    conv_first,
    conv_second,
    gain_first,
    gain_second,
):
    shard_count = lax.axis_size("shard")
    ctx_count = lax.axis_size("ctx")
    tp_count = lax.axis_size("tp")
    seq_count, tok_count, width = inputs.shape
    assert seq_count == 1 and tp_count == 2
    half = tok_count // tp_count
    seq_len = tok_count * ctx_count

    half_shape, half_sent = ((half, width), f32), ((half, width), bf16)

    def both_halves(mine):
        other = swap_with(mine, "tp", 1)
        whole = ((1, tok_count, width), mine.dtype)
        return in_vmem(join_rows, [whole], mine, other)[0]

    x_half = in_vmem(own_rows, [half_sent], inputs)[0]
    x_pieces = spread_rows(x_half)
    block = mixer_matrix.shape[0]
    mixer_own = in_vmem(prepare_mixer, [((4, block, width), bf16)], mixer_matrix)[0]
    mixer_parts = [mixer_own] + [swap_with(mixer_own, "shard", k) for k in range(1, shard_count)]
    ffn_block = ffn_weight.shape[0]
    ffn_own = in_vmem(
        prepare_ffn, [((3, ffn_block, width // 2), bf16)] * 2, ffn_weight.transpose(1, 0, 2)
    )
    ffn_halves = across_shard(ffn_own)
    ffn_parts = [half for halves in ffn_halves for half in halves]
    g_half = in_vmem(own_rows, [half_sent], cotangent)[0]
    g_pieces = spread_rows(g_half)

    channels, hidden = block * shard_count, ffn_block * shard_count
    mine_count = seq_len // 2
    parted = [((mine_count, width), f32), ((mine_count, width), bf16)]

    h_one, mixer_w, projected, gated, taps, kept, sent = in_vmem(
        functools.partial(mixer_forward, ctx_count, shard_count),
        [
            ((seq_len, width), bf16),
            ((4 * channels, width), bf16),
            ((seq_len, 3 * channels), f32),
            ((seq_len, channels), bf16),
            ((3, channels), f32),
        ]
        + parted,
        *x_pieces,
        *mixer_parts,
        norm_gains,
        conv_weight,
        flops=8 * seq_len * channels * width,
    )
    residual, normed_two, h_two_own = in_vmem(
        second_norm,
        [half_shape, half_shape, half_sent],
        *collect_rows(kept, sent),
        x_half,
        norm_gains,
    )

    hidden_rows = ((seq_len, hidden), bf16)
    g_all, gate_up_w, down_w = in_vmem(
        functools.partial(ffn_gather, ctx_count),
        [
            ((seq_len, width), bf16),
            ((2 * hidden, width), bf16),
            ((hidden, width), bf16),
        ],
        *g_pieces,
        *ffn_parts,
    )
    h_two, act, grad_gate, grad_up, kept, sent = in_vmem(
        functools.partial(ffn_rows, ctx_count),
        [((seq_len, width), bf16), hidden_rows, hidden_rows, hidden_rows] + parted,
        *spread_rows(h_two_own),
        g_all,
        gate_up_w,
        down_w,
        flops=10 * seq_len * hidden * width,
    )
    grad_resid, grad_mix_own, gain_two_part = in_vmem(
        second_norm_backward,
        [half_shape, half_sent, ((1, width), f32)],
        *collect_rows(kept, sent),
        residual,
        normed_two,
        g_half,
        norm_gains,
    )
    kept, sent = in_vmem(ffn_down, parted, act, down_w, flops=2 * seq_len * hidden * width)
    ffn_pieces = collect_rows(kept, sent)
    ffn_terms = in_vmem(
        functools.partial(ffn_weight_grads, shard_count),
        [((3, ffn_block, width), f32)] + [((3, ffn_block, width), bf16)] * (shard_count - 1),
        grad_gate,
        grad_up,
        act,
        h_two,
        g_all,
        flops=6 * seq_len * hidden * width,
    )
    ffn_got = [swap_with(ffn_terms[k], "shard", k) for k in range(1, shard_count)]

    grad_mix_all, grad_triple, kept, sent = in_vmem(
        functools.partial(mixer_backward, ctx_count, shard_count),
        [
            ((seq_len, width), bf16),
            ((seq_len, 3 * channels), bf16),
            ((mine_count + small_rows, width), f32),
            ((mine_count + 2 * small_rows, width), bf16),
        ],
        *spread_rows(grad_mix_own),
        h_one,
        mixer_w,
        projected,
        norm_gains,
        taps,
        gain_two_part,
        scratch=[pltpu.VMEM((small_rows, width), f32)],
        flops=8 * seq_len * channels * width,
    )
    in_pieces = collect_rows(kept, sent, small=True)
    mixer_terms = in_vmem(
        functools.partial(mixer_weight_grads, shard_count),
        [((4, block, width), f32)] + [((4, block, width), bf16)] * (shard_count - 1),
        grad_triple,
        h_one,
        gated,
        grad_mix_all,
        flops=8 * seq_len * channels * width,
    )
    mixer_got = [swap_with(mixer_terms[k], "shard", k) for k in range(1, shard_count)]
    ffn_news = in_vmem(
        functools.partial(ffn_adam, shard_count),
        [((3, ffn_block, width), f32)] * 4,
        ffn_terms[0],
        *ffn_got,
        *(value.transpose(1, 0, 2) for value in (ffn_weight, ffn_first, ffn_second)),
    )
    ffn_grad, ffn_new, ffn_first_new, ffn_second_new = (
        value.transpose(1, 0, 2) for value in ffn_news
    )
    out_own = in_vmem(output_kernel, [half_sent], *ffn_pieces, residual)[0]
    output = both_halves(out_own)
    input_grad, small = in_vmem(
        first_norm_backward,
        [half_shape, ((small_rows, width), f32)],
        *in_pieces,
        x_half,
        grad_resid,
        norm_gains,
    )
    input_grad = both_halves(input_grad)
    (
        gain_grad,
        gain_new,
        gain_first_new,
        gain_second_new,
        conv_grad,
        conv_new,
        conv_first_new,
        conv_second_new,
    ) = in_vmem(
        functools.partial(small_adam, shard_count),
        [(norm_gains.shape, f32)] * 4 + [(conv_weight.shape, f32)] * 4,
        small,
        *(swap_with(small, "shard", k) for k in range(1, shard_count)),
        norm_gains,
        gain_first,
        gain_second,
        conv_weight,
        conv_first,
        conv_second,
    )
    mixer_grad, mixer_new, mixer_first_new, mixer_second_new = in_vmem(
        functools.partial(mixer_adam, shard_count),
        [(mixer_matrix.shape, f32)] * 4,
        mixer_terms[0],
        *mixer_got,
        mixer_matrix,
        mixer_first,
        mixer_second,
    )
    return (
        output,
        input_grad,
        mixer_grad,
        ffn_grad,
        conv_grad,
        gain_grad,
        mixer_new,
        ffn_new,
        conv_new,
        gain_new,
        mixer_first_new,
        mixer_second_new,
        ffn_first_new,
        ffn_second_new,
        conv_first_new,
        conv_second_new,
        gain_first_new,
        gain_second_new,
    )


def solution(mesh):
    tokens = P("shard", "ctx", None)
    rows = P(("shard", "ctx", "tp"), None, None)
    in_specs = (tokens, tokens, rows, rows, P(), P(), rows, rows, rows, rows, P(), P(), P(), P())
    out_specs = (
        (tokens, tokens, rows, rows, P(), P(), rows, rows, P(), P())
        + (rows, rows, rows, rows)
        + (P(), P(), P(), P())
    )

    return jax.shard_map(
        per_device, mesh=mesh, in_specs=in_specs, out_specs=out_specs, check_vma=False
    )
```

time: 203 us -> 176 us (0.87)
  starting transfers between devices: 84.2 us -> 60.3 us
  waiting for transfers between devices: 63.1 us -> 85.9 us
  local copies, waits for them, and re-layouts: 16.7 us -> 3.59 us
  other arithmetic: 10.9 us -> 0 us
    ppermute x41 -> x64, waiting for transfers between devices: 10.4 us -> 85.9 us  [swap_with(): lax.ppermute(value, axis, [(i, partner_of(i, step, count)) for i in range...]
    ppermute x24 -> x0, waiting for transfers between devices: 52.7 us -> none  [send_up(): lax.ppermute(value, axis, [(i, (i + steps) % count) for i in range(count)])]
    ppermute x24 -> x0, starting transfers between devices: 47.9 us -> none  [send_up(): lax.ppermute(value, axis, [(i, (i + steps) % count) for i in range(count)])]
    ppermute x41 -> x64, starting transfers between devices: 36.2 us -> 60.3 us  [swap_with(): lax.ppermute(value, axis, [(i, partner_of(i, step, count)) for i in range...]
    unnamed x77 -> x34, local copies, waits for them, and re-layouts: 15.9 us -> 3.59 us
    sub x3 -> x0, other arithmetic: 8.09 us -> none  [adam_update(): weight - rate * (first_hat / (jnp.sqrt(second_hat) + adam_eps) + decay *...]
    pallas_call x15 -> x24, Pallas kernels: 26.1 us -> 24.8 us  [in_vmem(): pl.pallas_call(body, out_shape=shapes, in_specs=[pl.BlockSpec(memory_spac...]
  transfers between devices with their start and end apart: 65 -> 64, of which waited for: 28 -> 25; matrix products, arithmetic and copies ran while one was open for 6% -> 0% of each run, Pallas kernels for 6% -> 9%
where the time goes in v1:
time: 176 us
  waiting for transfers between devices  85.9 us (49%)
  starting transfers between devices  60.3 us (34%)
  Pallas kernels  24.8 us (14%)
  local copies, waits for them, and re-layouts  3.59 us (2%)
    ppermute x64, waiting for transfers between devices, swap_with(): lax.ppermute(value, axis, [(i, partner_of(i, step, count)) for i in range...  85.9 us
    ppermute x64, starting transfers between devices, swap_with(): lax.ppermute(value, axis, [(i, partner_of(i, step, count)) for i in range...  60.3 us
    pallas_call x24, Pallas kernels, in_vmem(): pl.pallas_call(body, out_shape=shapes, in_specs=[pl.BlockSpec(memory_spac...  24.8 us
    unnamed x34, local copies, waits for them, and re-layouts  3.59 us
  transfers between devices with their start and end apart: 64, of which 25 were waited for; matrix products, arithmetic and copies ran while one was open for 0% of the time, Pallas kernels for 9%

profile of v1, /device:TPU:0, one launch (start us, length us, event | category | flops | bytes accessed | tf_op | source)
XLA Modules:
  0.0 175.7 jit_solution(3812069836752176185)
XLA Ops:
  0.7 1.1 copy-done.9
  1.8 4.1 %collective-permute-start.1 = (bf16[64,1024]{1,0:T(8,128)(2,1)S(1)}, bf16[64,1024]{1,0:T(8,128)(2,1)S(1)}, u32[]{:S(2)}, u32[]{:S(2)}) collective-permute-start(bf16[64,1024]{1,0:T(8,128)(2,1)S(1)} %shard_map.277.refs_0_.refs_4_), channel_id=1, source_target_pairs={{0,4},{2,6},{4,0},{6,2},{1,5},{3,7},{5,1},{7,3},{8,12},{10,14},{12... | collective-permute-start | bytes 393224 | tf_op jit(solution)/shard_map/ppermute | solution.py:47
  5.9 1.6 collective-permute-start
  9.0 1.6 collective-permute-start.7
  10.6 1.5 collective-permute-start.8
  12.9 2.4 %collective-permute-start.9 = (bf16[4,32,1024]{2,1,0:T(8,128)(2,1)S(1)}, bf16[4,32,1024]{2,1,0:T(8,128)(2,1)S(1)}, u32[]{:S(2)}, u32[]{:S(2)}) collective-permute-start(bf16[4,32,1024]{2,1,0:T(8,128)(2,1)S(1)} %shard_map.278.refs_8_), channel_id=1, source_target_pairs={{0,24},{8,16},{16,8},{24,0},{1,25},{9,17},{17,9},{25,1},{2,26},{10... | collective-permute-start | bytes 786440 | tf_op jit(solution)/shard_map/ppermute | solution.py:47
  15.4 2.1 %collective-permute-done.2.refs_3_ = bf16[64,1024]{1,0:T(8,128)(2,1)S(1)} collective-permute-done((bf16[64,1024]{1,0:T(8,128)(2,1)S(1)}, bf16[64,1024]{1,0:T(8,128)(2,1)S(1)}, u32[]{:S(2)}, u32[]{:S(2)}) %collective-permute-start.2) | collective-permute-done | bytes 131104 | tf_op jit(solution)/shard_map/ppermute | solution.py:47
  18.8 5.8 %collective-permute-done.8.refs_10_ = bf16[4,32,1024]{2,1,0:T(8,128)(2,1)S(1)} collective-permute-done((bf16[4,32,1024]{2,1,0:T(8,128)(2,1)S(1)}, bf16[4,32,1024]{2,1,0:T(8,128)(2,1)S(1)}, u32[]{:S(2)}, u32[]{:S(2)}) %collective-permute-start.8) | collective-permute-done | bytes 262176 | tf_op jit(solution)/shard_map/ppermute | solution.py:47
  26.1 2.3 %shard_map.279 = (bf16[512,1024]{1,0:T(8,128)(2,1)S(1)}, bf16[512,1024]{1,0:T(8,128)(2,1)S(1)}, f32[512,384]{1,0:T(8,128)S(1)}, bf16[512,128]{1,0:T(8,128)(2,1)S...) custom-call(bf16[64,1024]{1,0:T(8,128)(2,1)S(1)} %shard_map.277.refs_0_.refs_4_, ...), custom_call_target="tpu_custom_call" | custom-call | flops 536870912 | bytes 6706688 | tf_op jit(solution)/shard_map/pallas_call | solution.py:83
  29.1 1.3 collective-permute-start.29
  31.2 1.3 collective-permute-start.22
  32.5 1.9 %collective-permute-done.21.refs_1_ = bf16[64,1024]{1,0:T(8,128)(2,1)S(1)} collective-permute-done((bf16[64,1024]{1,0:T(8,128)(2,1)S(1)}, bf16[64,1024]{1,0:T(8,128)(2,1)S(1)}, u32[]{:S(2)}, u32[]{:S(2)}) %collective-permute-start.21) | collective-permute-done | bytes 131104 | tf_op jit(solution)/shard_map/ppermute | solution.py:47
  34.5 5.5 %collective-permute-done.22.refs_2_ = bf16[64,1024]{1,0:T(8,128)(2,1)S(1)} collective-permute-done((bf16[64,1024]{1,0:T(8,128)(2,1)S(1)}, bf16[64,1024]{1,0:T(8,128)(2,1)S(1)}, u32[]{:S(2)}, u32[]{:S(2)}) %collective-permute-start.22) | collective-permute-done | bytes 131104 | tf_op jit(solution)/shard_map/ppermute | solution.py:47
  40.7 4.3 %collective-permute-done.23.refs_3_ = bf16[64,1024]{1,0:T(8,128)(2,1)S(1)} collective-permute-done((bf16[64,1024]{1,0:T(8,128)(2,1)S(1)}, bf16[64,1024]{1,0:T(8,128)(2,1)S(1)}, u32[]{:S(2)}, u32[]{:S(2)}) %collective-permute-start.23) | collective-permute-done | bytes 131104 | tf_op jit(solution)/shard_map/ppermute | solution.py:47
  45.0 1.5 collective-permute-start.28
  46.5 2.1 %collective-permute-start.12 = (bf16[64,1024]{1,0:T(8,128)(2,1)S(1)}, bf16[64,1024]{1,0:T(8,128)(2,1)S(1)}, u32[]{:S(2)}, u32[]{:S(2)}) collective-permute-start(bf16[64,1024]{1,0:T(8,128)(2,1)S(1)} %get-tuple-element.94), channel_id=1, source_target_pairs={{0,4},{2,6},{4,0},{6,2},{1,5},{3,7},{5,1},{7,3},{8,12},{10,14},{12... | collective-permute-start | bytes 393224 | tf_op jit(solution)/shard_map/ppermute | solution.py:47
  49.0 2.4 %collective-permute-start.13 = (bf16[64,1024]{1,0:T(8,128)(2,1)S(1)}, bf16[64,1024]{1,0:T(8,128)(2,1)S(1)}, u32[]{:S(2)}, u32[]{:S(2)}) collective-permute-start(bf16[64,1024]{1,0:T(8,128)(2,1)S(1)} %get-tuple-element.95), channel_id=1, source_target_pairs={{0,6},{2,4},{4,2},{6,0},{1,7},{3,5},{5,3},{7,1},{8,14},{10,12},{12... | collective-permute-start | bytes 393224 | tf_op jit(solution)/shard_map/ppermute | solution.py:47
  51.4 1.7 collective-permute-start.32
  53.1 4.9 %collective-permute-done.12.refs_2_ = bf16[64,1024]{1,0:T(8,128)(2,1)S(1)} collective-permute-done((bf16[64,1024]{1,0:T(8,128)(2,1)S(1)}, bf16[64,1024]{1,0:T(8,128)(2,1)S(1)}, u32[]{:S(2)}, u32[]{:S(2)}) %collective-permute-start.12) | collective-permute-done | bytes 131104 | tf_op jit(solution)/shard_map/ppermute | solution.py:47
  59.3 2.1 %collective-permute-start.15 = (bf16[64,1024]{1,0:T(8,128)(2,1)S(1)}, bf16[64,1024]{1,0:T(8,128)(2,1)S(1)}, u32[]{:S(2)}, u32[]{:S(2)}) collective-permute-start(bf16[64,1024]{1,0:T(8,128)(2,1)S(1)} %get-tuple-element.96.refs_0_), channel_id=1, source_target_pairs={{0,4},{2,6},{4,0},{6,2},{1,5},{3,7},{5,1},{7,3},{8,12},{10,14},{12... | collective-permute-start | bytes 393224 | tf_op jit(solution)/shard_map/ppermute | solution.py:47
  62.2 6.2 %collective-permute-done.15.refs_2_ = bf16[64,1024]{1,0:T(8,128)(2,1)S(1)} collective-permute-done((bf16[64,1024]{1,0:T(8,128)(2,1)S(1)}, bf16[64,1024]{1,0:T(8,128)(2,1)S(1)}, u32[]{:S(2)}, u32[]{:S(2)}) %collective-permute-start.15) | collective-permute-done | bytes 131104 | tf_op jit(solution)/shard_map/ppermute | solution.py:47
  69.0 4.8 %collective-permute-done.16.refs_3_ = bf16[64,1024]{1,0:T(8,128)(2,1)S(1)} collective-permute-done((bf16[64,1024]{1,0:T(8,128)(2,1)S(1)}, bf16[64,1024]{1,0:T(8,128)(2,1)S(1)}, u32[]{:S(2)}, u32[]{:S(2)}) %collective-permute-start.16) | collective-permute-done | bytes 131104 | tf_op jit(solution)/shard_map/ppermute | solution.py:47
  75.1 5.2 %shard_map.285 = (bf16[512,1024]{1,0:T(8,128)(2,1)S(1)}, bf16[512,576]{1,0:T(8,128)(2,1)S(1)}, bf16[512,576]{1,0:T(8,128)(2,1)S(1)}, bf16[512,576]{1,0:T(8,128)(...) custom-call(bf16[64,1024]{1,0:T(8,128)(2,1)S(1)} %get-tuple-element.96.refs_0_, ...), custom_call_target="tpu_custom_call" | custom-call | flops 3019898880 | bytes 10027008 | tf_op jit(solution)/shard_map/pallas_call | solution.py:83
  80.5 1.8 %collective-permute-done.39.got_ref = bf16[256,1024]{1,0:T(8,128)(2,1)S(1)} collective-permute-done((bf16[256,1024]{1,0:T(8,128)(2,1)S(1)}, bf16[256,1024]{1,0:T(8,128)(2,1)S(1)}, u32[]{:S(2)}, u32[]{:S(2)}) %collective-permute-start.39) | collective-permute-done | bytes 524320 | tf_op jit(solution)/shard_map/ppermute | solution.py:47
  82.7 2.4 %collective-permute-start.41 = (bf16[64,1024]{1,0:T(8,128)(2,1)S(1)}, bf16[64,1024]{1,0:T(8,128)(2,1)S(1)}, u32[]{:S(2)}, u32[]{:S(2)}) collective-permute-start(bf16[64,1024]{1,0:T(8,128)(2,1)S(1)} %get-tuple-element.114), channel_id=1, source_target_pairs={{0,4},{2,6},{4,0},{6,2},{1,5},{3,7},{5,1},{7,3},{8,12},{10,14},{12... | collective-permute-start | bytes 393224 | tf_op jit(solution)/shard_map/ppermute | solution.py:47
  85.1 1.7 collective-permute-start.42
  86.8 3.2 %collective-permute-done.40.refs_1_ = bf16[64,1024]{1,0:T(8,128)(2,1)S(1)} collective-permute-done((bf16[64,1024]{1,0:T(8,128)(2,1)S(1)}, bf16[64,1024]{1,0:T(8,128)(2,1)S(1)}, u32[]{:S(2)}, u32[]{:S(2)}) %collective-permute-start.40) | collective-permute-done | bytes 131104 | tf_op jit(solution)/shard_map/ppermute | solution.py:47
  90.0 5.6 %collective-permute-done.41.refs_2_ = bf16[64,1024]{1,0:T(8,128)(2,1)S(1)} collective-permute-done((bf16[64,1024]{1,0:T(8,128)(2,1)S(1)}, bf16[64,1024]{1,0:T(8,128)(2,1)S(1)}, u32[]{:S(2)}, u32[]{:S(2)}) %collective-permute-start.41) | collective-permute-done | bytes 131104 | tf_op jit(solution)/shard_map/ppermute | solution.py:47
  95.8 3.1 %collective-permute-start.44 = (bf16[64,1024]{1,0:T(8,128)(2,1)S(1)}, bf16[64,1024]{1,0:T(8,128)(2,1)S(1)}, u32[]{:S(2)}, u32[]{:S(2)}) collective-permute-start(bf16[64,1024]{1,0:T(8,128)(2,1)S(1)} %get-tuple-element.117.refs_0_), channel_id=1, source_target_pairs={{0,4},{2,6},{4,0},{6,2},{1,5},{3,7},{5,1},{7,3},{8,12},{10,14},{12... | collective-permute-start | bytes 393224 | tf_op jit(solution)/shard_map/ppermute | solution.py:47
  100.5 4.2 %collective-permute-done.44.refs_2_ = bf16[64,1024]{1,0:T(8,128)(2,1)S(1)} collective-permute-done((bf16[64,1024]{1,0:T(8,128)(2,1)S(1)}, bf16[64,1024]{1,0:T(8,128)(2,1)S(1)}, u32[]{:S(2)}, u32[]{:S(2)}) %collective-permute-start.44) | collective-permute-done | bytes 131104 | tf_op jit(solution)/shard_map/ppermute | solution.py:47
  104.7 2.2 %shard_map.298 = (f32[3,144,1024]{2,1,0:T(8,128)S(1)}, bf16[3,144,1024]{2,1,0:T(8,128)(2,1)S(1)}, bf16[3,144,1024]{2,1,0:T(8,128)(2,1)S(1)}, bf16[3,144,1024]{2,1,0:T(8,128)(2,1)S(1)}) custom-call(bf16[512,576]{1,0:T(8,128)(2,1)S(1)} %get-tuple-element.139.gate_ref, bf16[512,576]{1,0:T(8,128)(2,1)S(1)} %get-tuple-element.140.up_ref, ...), custom_call_target="tpu_custom_call" | custom-call | flops 1811939328 | bytes 8290304 | tf_op jit(solution)/shard_map/pallas_call | solution.py:83
  106.9 1.8 %collective-permute-start.58 = (bf16[3,144,1024]{2,1,0:T(8,128)(2,1)S(1)}, bf16[3,144,1024]{2,1,0:T(8,128)(2,1)S(1)}, u32[]{:S(2)}, u32[]{:S(2)}) collective-permute-start(bf16[3,144,1024]{2,1,0:T(8,128)(2,1)S(1)} %get-tuple-element.143), channel_id=1, source_target_pairs={{0,8},{8,0},{16,24},{24,16},{1,9},{9,1},{17,25},{25,17},{2,10},{10... | collective-permute-start | bytes 2654216 | tf_op jit(solution)/shard_map/ppermute | solution.py:47
  111.0 2.1 %shard_map.292 = (bf16[512,1024]{1,0:T(8,128)(2,1)S(1)}, bf16[512,384]{1,0:T(8,128)(2,1)S(1)}, f32[264,1024]{1,0:T(8,128)S(1)}, bf16[272,1024]{1,0:T(8,128)(2,1)S(1)}) custom-call(bf16[64,1024]{1,0:T(8,128)(2,1)S(1)} %get-tuple-element.117.refs_0_, bf16[64,1024]{1,0:T(8,128)(2,1)S(1)} %collective-permute-done.43.refs_1_, ...), custom_call_target="tpu_custom_call" | custom-call | flops 536870912 | bytes 7026176 | tf_op jit(solution)/shard_map/pallas_call | solution.py:83
  113.5 1.8 %collective-permute-start.35 = (bf16[64,1024]{1,0:T(8,128)(2,1)S(1)}, bf16[64,1024]{1,0:T(8,128)(2,1)S(1)}, u32[]{:S(2)}, u32[]{:S(2)}) collective-permute-start(bf16[64,1024]{1,0:T(8,128)(2,1)S(1)} %get-tuple-element.106), channel_id=1, source_target_pairs={{0,2},{2,0},{4,6},{6,4},{1,3},{3,1},{5,7},{7,5},{8,10},{10,8},{12,... | collective-permute-start | bytes 393224 | tf_op jit(solution)/shard_map/ppermute | solution.py:47
  116.2 3.3 %collective-permute-done.35.refs_1_ = bf16[64,1024]{1,0:T(8,128)(2,1)S(1)} collective-permute-done((bf16[64,1024]{1,0:T(8,128)(2,1)S(1)}, bf16[64,1024]{1,0:T(8,128)(2,1)S(1)}, u32[]{:S(2)}, u32[]{:S(2)}) %collective-permute-start.35) | collective-permute-done | bytes 131104 | tf_op jit(solution)/shard_map/ppermute | solution.py:47
  119.5 2.4 %collective-permute-start.36 = (bf16[64,1024]{1,0:T(8,128)(2,1)S(1)}, bf16[64,1024]{1,0:T(8,128)(2,1)S(1)}, u32[]{:S(2)}, u32[]{:S(2)}) collective-permute-start(bf16[64,1024]{1,0:T(8,128)(2,1)S(1)} %get-tuple-element.107), channel_id=1, source_target_pairs={{0,4},{2,6},{4,0},{6,2},{1,5},{3,7},{5,1},{7,3},{8,12},{10,14},{12... | collective-permute-start | bytes 393224 | tf_op jit(solution)/shard_map/ppermute | solution.py:47
  121.9 6.3 %collective-permute-done.36.refs_2_ = bf16[64,1024]{1,0:T(8,128)(2,1)S(1)} collective-permute-done((bf16[64,1024]{1,0:T(8,128)(2,1)S(1)}, bf16[64,1024]{1,0:T(8,128)(2,1)S(1)}, u32[]{:S(2)}, u32[]{:S(2)}) %collective-permute-start.36) | collective-permute-done | bytes 131104 | tf_op jit(solution)/shard_map/ppermute | solution.py:47
  128.2 2.6 %collective-permute-start.37 = (bf16[64,1024]{1,0:T(8,128)(2,1)S(1)}, bf16[64,1024]{1,0:T(8,128)(2,1)S(1)}, u32[]{:S(2)}, u32[]{:S(2)}) collective-permute-start(bf16[64,1024]{1,0:T(8,128)(2,1)S(1)} %get-tuple-element.108), channel_id=1, source_target_pairs={{0,6},{2,4},{4,2},{6,0},{1,7},{3,5},{5,3},{7,1},{8,14},{10,12},{12... | collective-permute-start | bytes 393224 | tf_op jit(solution)/shard_map/ppermute | solution.py:47
  130.8 4.3 %collective-permute-done.37.refs_3_ = bf16[64,1024]{1,0:T(8,128)(2,1)S(1)} collective-permute-done((bf16[64,1024]{1,0:T(8,128)(2,1)S(1)}, bf16[64,1024]{1,0:T(8,128)(2,1)S(1)}, u32[]{:S(2)}, u32[]{:S(2)}) %collective-permute-start.37) | collective-permute-done | bytes 131104 | tf_op jit(solution)/shard_map/ppermute | solution.py:47
  136.5 1.9 %collective-permute-start.52 = (bf16[80,1024]{1,0:T(8,128)(2,1)S(1)}, bf16[80,1024]{1,0:T(8,128)(2,1)S(1)}, u32[]{:S(2)}, u32[]{:S(2)}) collective-permute-start(bf16[80,1024]{1,0:T(8,128)(2,1)S(1)} %get-tuple-element.127), channel_id=1, source_target_pairs={{0,4},{2,6},{4,0},{6,2},{1,5},{3,7},{5,1},{7,3},{8,12},{10,14},{12... | collective-permute-start | bytes 491528 | tf_op jit(solution)/shard_map/ppermute | solution.py:47
  138.5 1.3 collective-permute-start.53
  140.5 4.1 %collective-permute-done.51.refs_1_ = bf16[80,1024]{1,0:T(8,128)(2,1)S(1)} collective-permute-done((bf16[80,1024]{1,0:T(8,128)(2,1)S(1)}, bf16[80,1024]{1,0:T(8,128)(2,1)S(1)}, u32[]{:S(2)}, u32[]{:S(2)}) %collective-permute-start.51) | collective-permute-done | bytes 163872 | tf_op jit(solution)/shard_map/ppermute | solution.py:47
  145.5 6.1 %collective-permute-done.52.refs_2_ = bf16[80,1024]{1,0:T(8,128)(2,1)S(1)} collective-permute-done((bf16[80,1024]{1,0:T(8,128)(2,1)S(1)}, bf16[80,1024]{1,0:T(8,128)(2,1)S(1)}, u32[]{:S(2)}, u32[]{:S(2)}) %collective-permute-start.52) | collective-permute-done | bytes 163872 | tf_op jit(solution)/shard_map/ppermute | solution.py:47
  152.6 2.0 %collective-permute-start.57 = (bf16[4,32,1024]{2,1,0:T(8,128)(2,1)S(1)}, bf16[4,32,1024]{2,1,0:T(8,128)(2,1)S(1)}, u32[]{:S(2)}, u32[]{:S(2)}) collective-permute-start(bf16[4,32,1024]{2,1,0:T(8,128)(2,1)S(1)} %get-tuple-element.137), channel_id=1, source_target_pairs={{0,24},{8,16},{16,8},{24,0},{1,25},{9,17},{17,9},{25,1},{2,26},{10... | collective-permute-start | bytes 786440 | tf_op jit(solution)/shard_map/ppermute | solution.py:47
  156.5 7.8 %collective-permute-done.56.refs_2_ = bf16[4,32,1024]{2,1,0:T(8,128)(2,1)S(1)} collective-permute-done((bf16[4,32,1024]{2,1,0:T(8,128)(2,1)S(1)}, bf16[4,32,1024]{2,1,0:T(8,128)(2,1)S(1)}, u32[]{:S(2)}, u32[]{:S(2)}) %collective-permute-start.56) | collective-permute-done | bytes 262176 | tf_op jit(solution)/shard_map/ppermute | solution.py:47
  164.2 2.1 %collective-permute-start.63 = (f32[8,1024]{1,0:T(8,128)S(1)}, f32[8,1024]{1,0:T(8,128)S(1)}, u32[]{:S(2)}, u32[]{:S(2)}) collective-permute-start(f32[8,1024]{1,0:T(8,128)S(1)} %get-tuple-element.147.refs_0_), channel_id=1, source_target_pairs={{0,24},{8,16},{16,8},{24,0},{1,25},{9,17},{17,9},{25,1},{2,26},{10... | collective-permute-start | bytes 98312 | tf_op jit(solution)/shard_map/ppermute | solution.py:47
  167.1 4.6 %shard_map.299 = (f32[3,144,1024]{2,1,0:T(8,128)}, f32[3,144,1024]{2,1,0:T(8,128)}, f32[3,144,1024]{2,1,0:T(8,128)}, f32[3,144,1024]{2,1,0:T(8,128)}) custom-call(f32[3,144,1024]{2,1,0:T(8,128)S(1)} %get-tuple-element.142.refs_0_, bf16[3,144,1024]{2,1,0:T(8,128)(2,1)S(1)} %collective-permute-done.58.refs_1_, ...), custom_call_target="tpu_custom_call" | custom-call | bytes 16809984 | tf_op jit(solution)/shard_map/pallas_call | solution.py:83
  171.7 2.3 %shard_map.297 = (f32[32,4,1024]{2,1,0:T(4,128)}, f32[32,4,1024]{2,1,0:T(4,128)}, f32[32,4,1024]{2,1,0:T(4,128)}, f32[32,4,1024]{2,1,0:T(4,128)}) custom-call(f32[4,32,1024]{2,1,0:T(8,128)S(1)} %get-tuple-element.134.refs_0_, bf16[4,32,1024]{2,1,0:T(8,128)(2,1)S(1)} %collective-permute-done.55.refs_1_, ...), custom_call_target="tpu_custom_call" | custom-call | bytes 4980736 | tf_op jit(solution)/shard_map/pallas_call | solution.py:83
  (138 shorter events, 26.2 us)
Async XLA Ops:
  1.8 10.5 %collective-permute-start.1 = (bf16[64,1024]{1,0:T(8,128)(2,1)S(1)}, bf16[64,1024]{1,0:T(8,128)(2,1)S(1)}, u32[]{:S(2)}, u32[]{:S(2)}) collective-permute-start(bf16[64,1024]{1,0:T(8,128)(2,1)S(1)} %shard_map.277.refs_0_.refs_4_), channel_id=1, source_target_pairs={{0,4},{2,6},{4,0},{6,2},{1,5},{3,7},{5,1},{7,3},{8,12},{10,14},{12... | collective-permute-start | bytes 393224 | tf_op jit(solution)/shard_map/ppermute | solution.py:47
  5.9 7.0 %collective-permute-start = (bf16[64,1024]{1,0:T(8,128)(2,1)S(1)}, bf16[64,1024]{1,0:T(8,128)(2,1)S(1)}, u32[]{:S(2)}, u32[]{:S(2)}) collective-permute-start(bf16[64,1024]{1,0:T(8,128)(2,1)S(1)} %shard_map.277.refs_0_.refs_4_), channel_id=1, source_target_pairs={{0,2},{2,0},{4,6},{6,4},{1,3},{3,1},{5,7},{7,5},{8,10},{10,8},{12,... | collective-permute-start | bytes 393224 | tf_op jit(solution)/shard_map/ppermute | solution.py:47
  7.5 7.9 %collective-permute-start.3 = (bf16[64,1024]{1,0:T(8,128)(2,1)S(1)}, bf16[64,1024]{1,0:T(8,128)(2,1)S(1)}, u32[]{:S(2)}, u32[]{:S(2)}) collective-permute-start(bf16[64,1024]{1,0:T(8,128)(2,1)S(1)} %shard_map.277.refs_0_.refs_4_), channel_id=1, source_target_pairs={{0,1},{1,0},{2,3},{3,2},{4,5},{5,4},{6,7},{7,6},{8,9},{9,8},{10,11... | collective-permute-start | bytes 393224 | tf_op jit(solution)/shard_map/ppermute | solution.py:47
  9.0 9.8 %collective-permute-start.7 = (bf16[4,32,1024]{2,1,0:T(8,128)(2,1)S(1)}, bf16[4,32,1024]{2,1,0:T(8,128)(2,1)S(1)}, u32[]{:S(2)}, u32[]{:S(2)}) collective-permute-start(bf16[4,32,1024]{2,1,0:T(8,128)(2,1)S(1)} %shard_map.278.refs_8_), channel_id=1, source_target_pairs={{0,8},{8,0},{16,24},{24,16},{1,9},{9,1},{17,25},{25,17},{2,10},{10... | collective-permute-start | bytes 786440 | tf_op jit(solution)/shard_map/ppermute | solution.py:47
  10.6 14.1 %collective-permute-start.8 = (bf16[4,32,1024]{2,1,0:T(8,128)(2,1)S(1)}, bf16[4,32,1024]{2,1,0:T(8,128)(2,1)S(1)}, u32[]{:S(2)}, u32[]{:S(2)}) collective-permute-start(bf16[4,32,1024]{2,1,0:T(8,128)(2,1)S(1)} %shard_map.278.refs_8_), channel_id=1, source_target_pairs={{0,16},{8,24},{16,0},{24,8},{1,17},{9,25},{17,1},{25,9},{2,18},{10... | collective-permute-start | bytes 786440 | tf_op jit(solution)/shard_map/ppermute | solution.py:47
  12.9 11.7 %collective-permute-start.9 = (bf16[4,32,1024]{2,1,0:T(8,128)(2,1)S(1)}, bf16[4,32,1024]{2,1,0:T(8,128)(2,1)S(1)}, u32[]{:S(2)}, u32[]{:S(2)}) collective-permute-start(bf16[4,32,1024]{2,1,0:T(8,128)(2,1)S(1)} %shard_map.278.refs_8_), channel_id=1, source_target_pairs={{0,24},{8,16},{16,8},{24,0},{1,25},{9,17},{17,9},{25,1},{2,26},{10... | collective-permute-start | bytes 786440 | tf_op jit(solution)/shard_map/ppermute | solution.py:47
  17.5 7.2 %collective-permute-start.6 = (bf16[64,1024]{1,0:T(8,128)(2,1)S(1)}, bf16[64,1024]{1,0:T(8,128)(2,1)S(1)}, u32[]{:S(2)}, u32[]{:S(2)}) collective-permute-start(bf16[64,1024]{1,0:T(8,128)(2,1)S(1)} %collective-permute-done.2.refs_3_), channel_id=1, source_target_pairs={{0,1},{1,0},{2,3},{3,2},{4,5},{5,4},{6,7},{7,6},{8,9},{9,8},{10,11... | collective-permute-start | bytes 393224 | tf_op jit(solution)/shard_map/ppermute | solution.py:47
  28.4 11.7 %collective-permute-start.10 = (bf16[256,1024]{1,0:T(8,128)(2,1)S(1)}, bf16[256,1024]{1,0:T(8,128)(2,1)S(1)}, u32[]{:S(2)}, u32[]{:S(2)}) collective-permute-start(bf16[256,1024]{1,0:T(8,128)(2,1)S(1)} %get-tuple-element.91), channel_id=1, source_target_pairs={{0,1},{1,0},{2,3},{3,2},{4,5},{5,4},{6,7},{7,6},{8,9},{9,8},{10,11... | collective-permute-start | bytes 1572872 | tf_op jit(solution)/shard_map/ppermute | solution.py:47
  28.5 6.0 %collective-permute-start.21 = (bf16[64,1024]{1,0:T(8,128)(2,1)S(1)}, bf16[64,1024]{1,0:T(8,128)(2,1)S(1)}, u32[]{:S(2)}, u32[]{:S(2)}) collective-permute-start(bf16[64,1024]{1,0:T(8,128)(2,1)S(1)} %shard_map.282.refs_0_.refs_6_), channel_id=1, source_target_pairs={{0,2},{2,0},{4,6},{6,4},{1,3},{3,1},{5,7},{7,5},{8,10},{10,8},{12,... | collective-permute-start | bytes 393224 | tf_op jit(solution)/shard_map/ppermute | solution.py:47
  29.1 19.4 %collective-permute-start.29 = (bf16[3,144,512]{2,1,0:T(8,128)(2,1)S(1)}, bf16[3,144,512]{2,1,0:T(8,128)(2,1)S(1)}, u32[]{:S(2)}, u32[]{:S(2)}) collective-permute-start(bf16[3,144,512]{2,1,0:T(8,128)(2,1)S(1)} %get-tuple-element.98.refs_9_), channel_id=1, source_target_pairs={{0,8},{8,0},{16,24},{24,16},{1,9},{9,1},{17,25},{25,17},{2,10},{10... | collective-permute-start | bytes 1327112 | tf_op jit(solution)/shard_map/ppermute | solution.py:47
  30.4 18.6 %collective-permute-start.30 = (bf16[3,144,512]{2,1,0:T(8,128)(2,1)S(1)}, bf16[3,144,512]{2,1,0:T(8,128)(2,1)S(1)}, u32[]{:S(2)}, u32[]{:S(2)}) collective-permute-start(bf16[3,144,512]{2,1,0:T(8,128)(2,1)S(1)} %get-tuple-element.97.refs_8_), channel_id=1, source_target_pairs={{0,16},{8,24},{16,0},{24,8},{1,17},{9,25},{17,1},{25,9},{2,18},{10... | collective-permute-start | bytes 1327112 | tf_op jit(solution)/shard_map/ppermute | solution.py:47
  31.2 8.8 %collective-permute-start.22 = (bf16[64,1024]{1,0:T(8,128)(2,1)S(1)}, bf16[64,1024]{1,0:T(8,128)(2,1)S(1)}, u32[]{:S(2)}, u32[]{:S(2)}) collective-permute-start(bf16[64,1024]{1,0:T(8,128)(2,1)S(1)} %shard_map.282.refs_0_.refs_6_), channel_id=1, source_target_pairs={{0,4},{2,6},{4,0},{6,2},{1,5},{3,7},{5,1},{7,3},{8,12},{10,14},{12... | collective-permute-start | bytes 393224 | tf_op jit(solution)/shard_map/ppermute | solution.py:47
  40.0 6.4 %collective-permute-start.26 = (bf16[64,1024]{1,0:T(8,128)(2,1)S(1)}, bf16[64,1024]{1,0:T(8,128)(2,1)S(1)}, u32[]{:S(2)}, u32[]{:S(2)}) collective-permute-start(bf16[64,1024]{1,0:T(8,128)(2,1)S(1)} %collective-permute-done.22.refs_2_), channel_id=1, source_target_pairs={{0,1},{1,0},{2,3},{3,2},{4,5},{5,4},{6,7},{7,6},{8,9},{9,8},{10,11... | collective-permute-start | bytes 393224 | tf_op jit(solution)/shard_map/ppermute | solution.py:47
  45.0 6.4 %collective-permute-start.11 = (bf16[64,1024]{1,0:T(8,128)(2,1)S(1)}, bf16[64,1024]{1,0:T(8,128)(2,1)S(1)}, u32[]{:S(2)}, u32[]{:S(2)}) collective-permute-start(bf16[64,1024]{1,0:T(8,128)(2,1)S(1)} %get-tuple-element.93), channel_id=1, source_target_pairs={{0,2},{2,0},{4,6},{6,4},{1,3},{3,1},{5,7},{7,5},{8,10},{10,8},{12,... | collective-permute-start | bytes 393224 | tf_op jit(solution)/shard_map/ppermute | solution.py:47
  45.0 16.4 %collective-permute-start.28 = (bf16[3,144,512]{2,1,0:T(8,128)(2,1)S(1)}, bf16[3,144,512]{2,1,0:T(8,128)(2,1)S(1)}, u32[]{:S(2)}, u32[]{:S(2)}) collective-permute-start(bf16[3,144,512]{2,1,0:T(8,128)(2,1)S(1)} %get-tuple-element.97.refs_8_), channel_id=1, source_target_pairs={{0,8},{8,0},{16,24},{24,16},{1,9},{9,1},{17,25},{25,17},{2,10},{10... | collective-permute-start | bytes 1327112 | tf_op jit(solution)/shard_map/ppermute | solution.py:47
  46.5 11.5 %collective-permute-start.12 = (bf16[64,1024]{1,0:T(8,128)(2,1)S(1)}, bf16[64,1024]{1,0:T(8,128)(2,1)S(1)}, u32[]{:S(2)}, u32[]{:S(2)}) collective-permute-start(bf16[64,1024]{1,0:T(8,128)(2,1)S(1)} %get-tuple-element.94), channel_id=1, source_target_pairs={{0,4},{2,6},{4,0},{6,2},{1,5},{3,7},{5,1},{7,3},{8,12},{10,14},{12... | collective-permute-start | bytes 393224 | tf_op jit(solution)/shard_map/ppermute | solution.py:47
  48.5 19.8 %collective-permute-start.31 = (bf16[3,144,512]{2,1,0:T(8,128)(2,1)S(1)}, bf16[3,144,512]{2,1,0:T(8,128)(2,1)S(1)}, u32[]{:S(2)}, u32[]{:S(2)}) collective-permute-start(bf16[3,144,512]{2,1,0:T(8,128)(2,1)S(1)} %get-tuple-element.98.refs_9_), channel_id=1, source_target_pairs={{0,16},{8,24},{16,0},{24,8},{1,17},{9,25},{17,1},{25,9},{2,18},{10... | collective-permute-start | bytes 1327112 | tf_op jit(solution)/shard_map/ppermute | solution.py:47
  49.0 8.9 %collective-permute-start.13 = (bf16[64,1024]{1,0:T(8,128)(2,1)S(1)}, bf16[64,1024]{1,0:T(8,128)(2,1)S(1)}, u32[]{:S(2)}, u32[]{:S(2)}) collective-permute-start(bf16[64,1024]{1,0:T(8,128)(2,1)S(1)} %get-tuple-element.95), channel_id=1, source_target_pairs={{0,6},{2,4},{4,2},{6,0},{1,7},{3,5},{5,3},{7,1},{8,14},{10,12},{12... | collective-permute-start | bytes 393224 | tf_op jit(solution)/shard_map/ppermute | solution.py:47
  51.4 17.0 %collective-permute-start.32 = (bf16[3,144,512]{2,1,0:T(8,128)(2,1)S(1)}, bf16[3,144,512]{2,1,0:T(8,128)(2,1)S(1)}, u32[]{:S(2)}, u32[]{:S(2)}) collective-permute-start(bf16[3,144,512]{2,1,0:T(8,128)(2,1)S(1)} %collective-permute-done.30.refs_12_), channel_id=1, source_target_pairs={{0,8},{8,0},{16,24},{24,16},{1,9},{9,1},{17,25},{25,17},{2,10},{10... | collective-permute-start | bytes 1327112 | tf_op jit(solution)/shard_map/ppermute | solution.py:47
  58.0 15.8 %collective-permute-start.33 = (bf16[3,144,512]{2,1,0:T(8,128)(2,1)S(1)}, bf16[3,144,512]{2,1,0:T(8,128)(2,1)S(1)}, u32[]{:S(2)}, u32[]{:S(2)}) collective-permute-start(bf16[3,144,512]{2,1,0:T(8,128)(2,1)S(1)} %collective-permute-done.29.refs_11_), channel_id=1, source_target_pairs={{0,16},{8,24},{16,0},{24,8},{1,17},{9,25},{17,1},{25,9},{2,18},{10... | collective-permute-start | bytes 1327112 | tf_op jit(solution)/shard_map/ppermute | solution.py:47
  59.3 9.0 %collective-permute-start.15 = (bf16[64,1024]{1,0:T(8,128)(2,1)S(1)}, bf16[64,1024]{1,0:T(8,128)(2,1)S(1)}, u32[]{:S(2)}, u32[]{:S(2)}) collective-permute-start(bf16[64,1024]{1,0:T(8,128)(2,1)S(1)} %get-tuple-element.96.refs_0_), channel_id=1, source_target_pairs={{0,4},{2,6},{4,0},{6,2},{1,5},{3,7},{5,1},{7,3},{8,12},{10,14},{12... | collective-permute-start | bytes 393224 | tf_op jit(solution)/shard_map/ppermute | solution.py:47
  61.4 7.5 %collective-permute-start.14 = (bf16[64,1024]{1,0:T(8,128)(2,1)S(1)}, bf16[64,1024]{1,0:T(8,128)(2,1)S(1)}, u32[]{:S(2)}, u32[]{:S(2)}) collective-permute-start(bf16[64,1024]{1,0:T(8,128)(2,1)S(1)} %get-tuple-element.96.refs_0_), channel_id=1, source_target_pairs={{0,2},{2,0},{4,6},{6,4},{1,3},{3,1},{5,7},{7,5},{8,10},{10,8},{12,... | collective-permute-start | bytes 393224 | tf_op jit(solution)/shard_map/ppermute | solution.py:47
  68.4 5.7 %collective-permute-start.17 = (bf16[64,1024]{1,0:T(8,128)(2,1)S(1)}, bf16[64,1024]{1,0:T(8,128)(2,1)S(1)}, u32[]{:S(2)}, u32[]{:S(2)}) collective-permute-start(bf16[64,1024]{1,0:T(8,128)(2,1)S(1)} %get-tuple-element.96.refs_0_), channel_id=1, source_target_pairs={{0,1},{1,0},{2,3},{3,2},{4,5},{5,4},{6,7},{7,6},{8,9},{9,8},{10,11... | collective-permute-start | bytes 393224 | tf_op jit(solution)/shard_map/ppermute | solution.py:47
  68.4 5.7 %collective-permute-start.19 = (bf16[64,1024]{1,0:T(8,128)(2,1)S(1)}, bf16[64,1024]{1,0:T(8,128)(2,1)S(1)}, u32[]{:S(2)}, u32[]{:S(2)}) collective-permute-start(bf16[64,1024]{1,0:T(8,128)(2,1)S(1)} %collective-permute-done.15.refs_2_), channel_id=1, source_target_pairs={{0,1},{1,0},{2,3},{3,2},{4,5},{5,4},{6,7},{7,6},{8,9},{9,8},{10,11... | collective-permute-start | bytes 393224 | tf_op jit(solution)/shard_map/ppermute | solution.py:47
  82.4 7.6 %collective-permute-start.40 = (bf16[64,1024]{1,0:T(8,128)(2,1)S(1)}, bf16[64,1024]{1,0:T(8,128)(2,1)S(1)}, u32[]{:S(2)}, u32[]{:S(2)}) collective-permute-start(bf16[64,1024]{1,0:T(8,128)(2,1)S(1)} %get-tuple-element.113), channel_id=1, source_target_pairs={{0,2},{2,0},{4,6},{6,4},{1,3},{3,1},{5,7},{7,5},{8,10},{10,8},{12,... | collective-permute-start | bytes 393224 | tf_op jit(solution)/shard_map/ppermute | solution.py:47
  82.7 12.9 %collective-permute-start.41 = (bf16[64,1024]{1,0:T(8,128)(2,1)S(1)}, bf16[64,1024]{1,0:T(8,128)(2,1)S(1)}, u32[]{:S(2)}, u32[]{:S(2)}) collective-permute-start(bf16[64,1024]{1,0:T(8,128)(2,1)S(1)} %get-tuple-element.114), channel_id=1, source_target_pairs={{0,4},{2,6},{4,0},{6,2},{1,5},{3,7},{5,1},{7,3},{8,12},{10,14},{12... | collective-permute-start | bytes 393224 | tf_op jit(solution)/shard_map/ppermute | solution.py:47
  85.1 10.5 %collective-permute-start.42 = (bf16[64,1024]{1,0:T(8,128)(2,1)S(1)}, bf16[64,1024]{1,0:T(8,128)(2,1)S(1)}, u32[]{:S(2)}, u32[]{:S(2)}) collective-permute-start(bf16[64,1024]{1,0:T(8,128)(2,1)S(1)} %get-tuple-element.115), channel_id=1, source_target_pairs={{0,6},{2,4},{4,2},{6,0},{1,7},{3,5},{5,3},{7,1},{8,14},{10,12},{12... | collective-permute-start | bytes 393224 | tf_op jit(solution)/shard_map/ppermute | solution.py:47
  95.8 8.8 %collective-permute-start.44 = (bf16[64,1024]{1,0:T(8,128)(2,1)S(1)}, bf16[64,1024]{1,0:T(8,128)(2,1)S(1)}, u32[]{:S(2)}, u32[]{:S(2)}) collective-permute-start(bf16[64,1024]{1,0:T(8,128)(2,1)S(1)} %get-tuple-element.117.refs_0_), channel_id=1, source_target_pairs={{0,4},{2,6},{4,0},{6,2},{1,5},{3,7},{5,1},{7,3},{8,12},{10,14},{12... | collective-permute-start | bytes 393224 | tf_op jit(solution)/shard_map/ppermute | solution.py:47
  99.9 13.6 %collective-permute-start.34 = (bf16[256,1024]{1,0:T(8,128)(2,1)S(1)}, bf16[256,1024]{1,0:T(8,128)(2,1)S(1)}, u32[]{:S(2)}, u32[]{:S(2)}) collective-permute-start(bf16[256,1024]{1,0:T(8,128)(2,1)S(1)} %get-tuple-element.104), channel_id=1, source_target_pairs={{0,1},{1,0},{2,3},{3,2},{4,5},{5,4},{6,7},{7,6},{8,9},{9,8},{10,11... | collective-permute-start | bytes 1572872 | tf_op jit(solution)/shard_map/ppermute | solution.py:47
  100.0 8.7 %collective-permute-start.43 = (bf16[64,1024]{1,0:T(8,128)(2,1)S(1)}, bf16[64,1024]{1,0:T(8,128)(2,1)S(1)}, u32[]{:S(2)}, u32[]{:S(2)}) collective-permute-start(bf16[64,1024]{1,0:T(8,128)(2,1)S(1)} %get-tuple-element.117.refs_0_), channel_id=1, source_target_pairs={{0,2},{2,0},{4,6},{6,4},{1,3},{3,1},{5,7},{7,5},{8,10},{10,8},{12,... | collective-permute-start | bytes 393224 | tf_op jit(solution)/shard_map/ppermute | solution.py:47
  100.0 8.7 %collective-permute-start.46 = (bf16[64,1024]{1,0:T(8,128)(2,1)S(1)}, bf16[64,1024]{1,0:T(8,128)(2,1)S(1)}, u32[]{:S(2)}, u32[]{:S(2)}) collective-permute-start(bf16[64,1024]{1,0:T(8,128)(2,1)S(1)} %get-tuple-element.117.refs_0_), channel_id=1, source_target_pairs={{0,1},{1,0},{2,3},{3,2},{4,5},{5,4},{6,7},{7,6},{8,9},{9,8},{10,11... | collective-permute-start | bytes 393224 | tf_op jit(solution)/shard_map/ppermute | solution.py:47
  106.9 31.6 %collective-permute-start.58 = (bf16[3,144,1024]{2,1,0:T(8,128)(2,1)S(1)}, bf16[3,144,1024]{2,1,0:T(8,128)(2,1)S(1)}, u32[]{:S(2)}, u32[]{:S(2)}) collective-permute-start(bf16[3,144,1024]{2,1,0:T(8,128)(2,1)S(1)} %get-tuple-element.143), channel_id=1, source_target_pairs={{0,8},{8,0},{16,24},{24,16},{1,9},{9,1},{17,25},{25,17},{2,10},{10... | collective-permute-start | bytes 2654216 | tf_op jit(solution)/shard_map/ppermute | solution.py:47
  110.0 44.8 %collective-permute-start.59 = (bf16[3,144,1024]{2,1,0:T(8,128)(2,1)S(1)}, bf16[3,144,1024]{2,1,0:T(8,128)(2,1)S(1)}, u32[]{:S(2)}, u32[]{:S(2)}) collective-permute-start(bf16[3,144,1024]{2,1,0:T(8,128)(2,1)S(1)} %get-tuple-element.144), channel_id=1, source_target_pairs={{0,16},{8,24},{16,0},{24,8},{1,17},{9,25},{17,1},{25,9},{2,18},{10... | collective-permute-start | bytes 2654216 | tf_op jit(solution)/shard_map/ppermute | solution.py:47
  113.1 22.1 %collective-permute-start.50 = (bf16[272,1024]{1,0:T(8,128)(2,1)S(1)}, bf16[272,1024]{1,0:T(8,128)(2,1)S(1)}, u32[]{:S(2)}, u32[]{:S(2)}) collective-permute-start(bf16[272,1024]{1,0:T(8,128)(2,1)S(1)} %get-tuple-element.124), channel_id=1, source_target_pairs={{0,1},{1,0},{2,3},{3,2},{4,5},{5,4},{6,7},{7,6},{8,9},{9,8},{10,11... | collective-permute-start | bytes 1671176 | tf_op jit(solution)/shard_map/ppermute | solution.py:47
  113.5 5.9 %collective-permute-start.35 = (bf16[64,1024]{1,0:T(8,128)(2,1)S(1)}, bf16[64,1024]{1,0:T(8,128)(2,1)S(1)}, u32[]{:S(2)}, u32[]{:S(2)}) collective-permute-start(bf16[64,1024]{1,0:T(8,128)(2,1)S(1)} %get-tuple-element.106), channel_id=1, source_target_pairs={{0,2},{2,0},{4,6},{6,4},{1,3},{3,1},{5,7},{7,5},{8,10},{10,8},{12,... | collective-permute-start | bytes 393224 | tf_op jit(solution)/shard_map/ppermute | solution.py:47
  115.3 39.6 %collective-permute-start.60 = (bf16[3,144,1024]{2,1,0:T(8,128)(2,1)S(1)}, bf16[3,144,1024]{2,1,0:T(8,128)(2,1)S(1)}, u32[]{:S(2)}, u32[]{:S(2)}) collective-permute-start(bf16[3,144,1024]{2,1,0:T(8,128)(2,1)S(1)} %get-tuple-element.145), channel_id=1, source_target_pairs={{0,24},{8,16},{16,8},{24,0},{1,25},{9,17},{17,9},{25,1},{2,26},{10... | collective-permute-start | bytes 2654216 | tf_op jit(solution)/shard_map/ppermute | solution.py:47
  119.5 8.7 %collective-permute-start.36 = (bf16[64,1024]{1,0:T(8,128)(2,1)S(1)}, bf16[64,1024]{1,0:T(8,128)(2,1)S(1)}, u32[]{:S(2)}, u32[]{:S(2)}) collective-permute-start(bf16[64,1024]{1,0:T(8,128)(2,1)S(1)} %get-tuple-element.107), channel_id=1, source_target_pairs={{0,4},{2,6},{4,0},{6,2},{1,5},{3,7},{5,1},{7,3},{8,12},{10,14},{12... | collective-permute-start | bytes 393224 | tf_op jit(solution)/shard_map/ppermute | solution.py:47
  128.2 6.9 %collective-permute-start.37 = (bf16[64,1024]{1,0:T(8,128)(2,1)S(1)}, bf16[64,1024]{1,0:T(8,128)(2,1)S(1)}, u32[]{:S(2)}, u32[]{:S(2)}) collective-permute-start(bf16[64,1024]{1,0:T(8,128)(2,1)S(1)} %get-tuple-element.108), channel_id=1, source_target_pairs={{0,6},{2,4},{4,2},{6,0},{1,7},{3,5},{5,3},{7,1},{8,14},{10,12},{12... | collective-permute-start | bytes 393224 | tf_op jit(solution)/shard_map/ppermute | solution.py:47
  135.3 9.3 %collective-permute-start.51 = (bf16[80,1024]{1,0:T(8,128)(2,1)S(1)}, bf16[80,1024]{1,0:T(8,128)(2,1)S(1)}, u32[]{:S(2)}, u32[]{:S(2)}) collective-permute-start(bf16[80,1024]{1,0:T(8,128)(2,1)S(1)} %get-tuple-element.126), channel_id=1, source_target_pairs={{0,2},{2,0},{4,6},{6,4},{1,3},{3,1},{5,7},{7,5},{8,10},{10,8},{12,... | collective-permute-start | bytes 491528 | tf_op jit(solution)/shard_map/ppermute | solution.py:47
  136.5 15.0 %collective-permute-start.52 = (bf16[80,1024]{1,0:T(8,128)(2,1)S(1)}, bf16[80,1024]{1,0:T(8,128)(2,1)S(1)}, u32[]{:S(2)}, u32[]{:S(2)}) collective-permute-start(bf16[80,1024]{1,0:T(8,128)(2,1)S(1)} %get-tuple-element.127), channel_id=1, source_target_pairs={{0,4},{2,6},{4,0},{6,2},{1,5},{3,7},{5,1},{7,3},{8,12},{10,14},{12... | collective-permute-start | bytes 491528 | tf_op jit(solution)/shard_map/ppermute | solution.py:47
  138.5 14.1 %collective-permute-start.53 = (bf16[80,1024]{1,0:T(8,128)(2,1)S(1)}, bf16[80,1024]{1,0:T(8,128)(2,1)S(1)}, u32[]{:S(2)}, u32[]{:S(2)}) collective-permute-start(bf16[80,1024]{1,0:T(8,128)(2,1)S(1)} %get-tuple-element.128), channel_id=1, source_target_pairs={{0,6},{2,4},{4,2},{6,0},{1,7},{3,5},{5,3},{7,1},{8,14},{10,12},{12... | collective-permute-start | bytes 491528 | tf_op jit(solution)/shard_map/ppermute | solution.py:47
  144.6 10.9 %collective-permute-start.55 = (bf16[4,32,1024]{2,1,0:T(8,128)(2,1)S(1)}, bf16[4,32,1024]{2,1,0:T(8,128)(2,1)S(1)}, u32[]{:S(2)}, u32[]{:S(2)}) collective-permute-start(bf16[4,32,1024]{2,1,0:T(8,128)(2,1)S(1)} %get-tuple-element.135), channel_id=1, source_target_pairs={{0,8},{8,0},{16,24},{24,16},{1,9},{9,1},{17,25},{25,17},{2,10},{10... | collective-permute-start | bytes 786440 | tf_op jit(solution)/shard_map/ppermute | solution.py:47
  151.6 12.7 %collective-permute-start.56 = (bf16[4,32,1024]{2,1,0:T(8,128)(2,1)S(1)}, bf16[4,32,1024]{2,1,0:T(8,128)(2,1)S(1)}, u32[]{:S(2)}, u32[]{:S(2)}) collective-permute-start(bf16[4,32,1024]{2,1,0:T(8,128)(2,1)S(1)} %get-tuple-element.136), channel_id=1, source_target_pairs={{0,16},{8,24},{16,0},{24,8},{1,17},{9,25},{17,1},{25,9},{2,18},{10... | collective-permute-start | bytes 786440 | tf_op jit(solution)/shard_map/ppermute | solution.py:47
  152.6 19.1 %collective-permute-start.57 = (bf16[4,32,1024]{2,1,0:T(8,128)(2,1)S(1)}, bf16[4,32,1024]{2,1,0:T(8,128)(2,1)S(1)}, u32[]{:S(2)}, u32[]{:S(2)}) collective-permute-start(bf16[4,32,1024]{2,1,0:T(8,128)(2,1)S(1)} %get-tuple-element.137), channel_id=1, source_target_pairs={{0,24},{8,16},{16,8},{24,0},{1,25},{9,17},{17,9},{25,1},{2,26},{10... | collective-permute-start | bytes 786440 | tf_op jit(solution)/shard_map/ppermute | solution.py:47
  154.8 20.0 %collective-permute-start.54 = (f32[64,1024]{1,0:T(8,128)S(1)}, f32[64,1024]{1,0:T(8,128)S(1)}, u32[]{:S(2)}, u32[]{:S(2)}) collective-permute-start(f32[64,1024]{1,0:T(8,128)S(1)} %get-tuple-element.130.mine_ref), channel_id=1, source_target_pairs={{0,1},{1,0},{2,3},{3,2},{4,5},{5,4},{6,7},{7,6},{8,9},{9,8},{10,11... | collective-permute-start | bytes 786440 | tf_op jit(solution)/shard_map/ppermute | solution.py:47
  154.9 19.2 %collective-permute-start.61 = (f32[8,1024]{1,0:T(8,128)S(1)}, f32[8,1024]{1,0:T(8,128)S(1)}, u32[]{:S(2)}, u32[]{:S(2)}) collective-permute-start(f32[8,1024]{1,0:T(8,128)S(1)} %get-tuple-element.147.refs_0_), channel_id=1, source_target_pairs={{0,8},{8,0},{16,24},{24,16},{1,9},{9,1},{17,25},{25,17},{2,10},{10... | collective-permute-start | bytes 98312 | tf_op jit(solution)/shard_map/ppermute | solution.py:47
  155.5 18.6 %collective-permute-start.62 = (f32[8,1024]{1,0:T(8,128)S(1)}, f32[8,1024]{1,0:T(8,128)S(1)}, u32[]{:S(2)}, u32[]{:S(2)}) collective-permute-start(f32[8,1024]{1,0:T(8,128)S(1)} %get-tuple-element.147.refs_0_), channel_id=1, source_target_pairs={{0,16},{8,24},{16,0},{24,8},{1,17},{9,25},{17,1},{25,9},{2,18},{10... | collective-permute-start | bytes 98312 | tf_op jit(solution)/shard_map/ppermute | solution.py:47
  164.2 9.9 %collective-permute-start.63 = (f32[8,1024]{1,0:T(8,128)S(1)}, f32[8,1024]{1,0:T(8,128)S(1)}, u32[]{:S(2)}, u32[]{:S(2)}) collective-permute-start(f32[8,1024]{1,0:T(8,128)S(1)} %get-tuple-element.147.refs_0_), channel_id=1, source_target_pairs={{0,24},{8,16},{16,8},{24,0},{1,25},{9,17},{17,9},{25,1},{2,26},{10... | collective-permute-start | bytes 98312 | tf_op jit(solution)/shard_map/ppermute | solution.py:47
  (33 other events, 196.1 us)

commit v2 on v1

--- a/solution.py
+++ b/solution.py
@@ -64,6 +64,28 @@
             [swap_with(pieces[k ^ via][j], "shard", via) for j, via in enumerate((low, high))]
         )
     return pieces
+
+
+def owners_terms(terms):
+    count = lax.axis_size("shard")
+    if count != 4:
+        return [[swap_with(terms[k - 1][j], "shard", k) for k in range(1, count)] for j in range(2)]
+    (near_a, near_b), (next_a, next_b), (far_a, far_b) = terms
+    passed_a = swap_with(far_a, "shard", 1)
+    passed_b = swap_with(far_b, "shard", 2)
+    came_near_a = swap_with(near_a, "shard", 1)
+    came_next_b = swap_with(next_b, "shard", 2)
+    shape = [(near_a.shape, bf16)]
+    joint_a, joint_b = in_vmem(add_pairs, shape * 2, next_a, passed_a, near_b, passed_b)
+    came_next_a = swap_with(joint_a, "shard", 2)
+    came_near_b = swap_with(joint_b, "shard", 1)
+    return [[came_near_a, came_next_a], [came_near_b, came_next_b]]
+
+
+def add_pairs(*refs):
+    for j, out_ref in enumerate(refs[2 * (len(refs) // 3) :]):
+        total = refs[2 * j][...].astype(f32) + refs[2 * j + 1][...].astype(f32)
+        out_ref[...] = total.astype(out_ref.dtype)
 
 
 def spread_rows(own):
@@ -281,25 +303,38 @@
         out_ref[...] = part.astype(out_ref.dtype)
 
 
-def ffn_weight_grads(groups, gate_ref, up_ref, act_ref, h_ref, g_ref, *outs):
-    block = outs[0].shape[1]
+def ffn_weight_grads(gate_ref, up_ref, act_ref, h_ref, g_ref, *outs):
+    own_ref, halves = outs[0], outs[1:]
+    block, columns = own_ref.shape[1], halves[0].shape[2]
     for k, (left, right) in enumerate(((gate_ref, h_ref), (up_ref, h_ref), (act_ref, g_ref))):
         term = down_rows(left[...], right[...])
-        for s in range(groups):
-            outs[s][k] = term[s * block : (s + 1) * block].astype(outs[s].dtype)
-
-
-def ffn_adam(groups, *refs):
-    own_ref, *parts = refs[:groups]
-    weight, first, second, grad_out, *outs = refs[groups:]
+        own_ref[k] = term[:block]
+        for j, out_ref in enumerate(halves):
+            at, side = (1 + j // 2) * block, (j % 2) * columns
+            out_ref[k] = term[at : at + block, side : side + columns].astype(bf16)
+
+
+def ffn_adam(half_parts, *refs):
+    own_ref, parts = refs[0], refs[1 : 1 + 2 * half_parts]
+    weight, first, second, grad_out, *outs = refs[1 + 2 * half_parts :]
+    columns = parts[0].shape[2]
     for k in range(3):
-        grad = own_ref[k]
-        for part in parts:
-            grad = grad + part[k].astype(f32)
-        grad_out[k] = grad
-        news = adam_update(weight[k], grad, first[k], second[k], matrix_rate, decay_rate)
-        for out, new in zip(outs, news):
-            out[k] = new
+        for j in range(2):
+            side = slice(j * columns, (j + 1) * columns)
+            grad = own_ref[k, :, side]
+            for part in parts[j * half_parts : (j + 1) * half_parts]:
+                grad = grad + part[k].astype(f32)
+            grad_out[k, :, side] = grad
+            news = adam_update(
+                weight[k, :, side],
+                grad,
+                first[k, :, side],
+                second[k, :, side],
+                matrix_rate,
+                decay_rate,
+            )
+            for out, new in zip(outs, news):
+                out[k, :, side] = new
 
 
 def mixer_adam(groups, *refs):
@@ -328,15 +363,12 @@
     rows = outs[0].shape[0] - small_rows
     count = len(outs)
     small = kept_ref[count * rows :, :] + whole_of(got_ref, count * rows)
-    coarse, fine = halves_of(small)
+    rounded = small.astype(bf16)
     for k, out_ref in enumerate(outs):
         at = slice(k * rows, (k + 1) * rows)
         pair = kept_ref[at, :] + got_ref[at, :].astype(f32)
         out_ref[:rows, :] = pair.astype(out_ref.dtype)
-        if k == 0:
-            out_ref[rows:, :] = coarse.astype(f32) + fine.astype(f32)
-        else:
-            out_ref[rows:, :] = jnp.concatenate([coarse, fine], axis=0)
+        out_ref[rows:, :] = rounded.astype(out_ref.dtype)
 
 
 def total_of(own_ref, got_refs, rows=None):
@@ -400,7 +432,7 @@
     out_ref[...] = grad_ref[...] + norm_backward(
         total_of(own_ref, got, rows) * gain_ref[0:1, :], x * scale, scale
     )
-    small_ref[...] = tree_sum([own_ref[rows:, :]] + [whole_of(ref, rows) for ref in got])
+    small_ref[...] = tree_sum([ref[rows:, :].astype(f32) for ref in (own_ref, *got)])
 
 
 def small_adam(groups, *refs):
@@ -419,15 +451,20 @@
     out_ref[...] = (resid_ref[...] + total_of(own_ref, got)).astype(out_ref.dtype)
 
 
-def collect_rows(kept, sent, small=False):
+def collect_rows(kept, sent, small=False, passed=False):
     count = lax.axis_size("ctx")
     width = kept.shape[1]
     rows = (kept.shape[0] - small_rows * small) // count
     outs = [((rows + small_rows * small, width), f32)]
-    outs += [((rows + 2 * small_rows * small, width), bf16)] * (count - 1)
+    outs += [((rows + small_rows * small, width), bf16)] * (count - 1)
     got = swap_with(sent, "tp", 1)
     pieces = in_vmem(pair_with_small if small else pair_kernel, outs, kept, got)
-    return [pieces[0]] + [swap_with(pieces[k], "ctx", k) for k in range(1, count)]
+    if not passed or count != 4:
+        return [pieces[0]] + [swap_with(pieces[k], "ctx", k) for k in range(1, count)]
+    came = swap_with(pieces[3], "ctx", 1)
+    near = swap_with(pieces[1], "ctx", 1)
+    joint = in_vmem(add_pairs, outs[2:3], pieces[2], came)
+    return [pieces[0], near, swap_with(joint[0], "ctx", 2)]
 
 
 def per_device(
@@ -533,10 +570,11 @@
         norm_gains,
     )
     kept, sent = in_vmem(ffn_down, parted, act, down_w, flops=2 * seq_len * hidden * width)
-    ffn_pieces = collect_rows(kept, sent)
+    ffn_pieces = collect_rows(kept, sent, passed=True)
     ffn_terms = in_vmem(
-        functools.partial(ffn_weight_grads, shard_count),
-        [((3, ffn_block, width), f32)] + [((3, ffn_block, width), bf16)] * (shard_count - 1),
+        ffn_weight_grads,
+        [((3, ffn_block, width), f32)]
+        + [((3, ffn_block, width // 2), bf16)] * (2 * (shard_count - 1)),
         grad_gate,
         grad_up,
         act,
@@ -544,7 +582,7 @@
         g_all,
         flops=6 * seq_len * hidden * width,
     )
-    ffn_got = [swap_with(ffn_terms[k], "shard", k) for k in range(1, shard_count)]
+    ffn_got = owners_terms(list(zip(ffn_terms[1::2], ffn_terms[2::2])))
 
     grad_mix_all, grad_triple, kept, sent = in_vmem(
         functools.partial(mixer_backward, ctx_count, shard_count),
@@ -576,10 +614,11 @@
     )
     mixer_got = [swap_with(mixer_terms[k], "shard", k) for k in range(1, shard_count)]
     ffn_news = in_vmem(
-        functools.partial(ffn_adam, shard_count),
+        functools.partial(ffn_adam, len(ffn_got[0])),
         [((3, ffn_block, width), f32)] * 4,
         ffn_terms[0],
-        *ffn_got,
+        *ffn_got[0],
+        *ffn_got[1],
         *(value.transpose(1, 0, 2) for value in (ffn_weight, ffn_first, ffn_second)),
     )
     ffn_grad, ffn_new, ffn_first_new, ffn_second_new = (

time: 176 us -> 176 us (level)
    pallas_call x24 -> x26, Pallas kernels: 24.8 us -> 24.9 us  [in_vmem(): pl.pallas_call(body, out_shape=shapes, in_specs=[pl.BlockSpec(memory_spac...]
    ppermute x64 -> x67, waiting for transfers between devices: 85.9 us -> 85.8 us  [swap_with(): lax.ppermute(value, axis, [(i, partner_of(i, step, count)) for i in range...]
    ppermute x64 -> x67, starting transfers between devices: 60.3 us -> 60.3 us  [swap_with(): lax.ppermute(value, axis, [(i, partner_of(i, step, count)) for i in range...]
  transfers between devices with their start and end apart: 64 -> 67, of which waited for: 25 -> 24; matrix products, arithmetic and copies ran while one was open for 0% -> 0% of each run, Pallas kernels for 9% -> 9%
where the time goes in v2:
time: 176 us
  waiting for transfers between devices  85.8 us (49%)
  starting transfers between devices  60.3 us (34%)
  Pallas kernels  24.9 us (14%)
  local copies, waits for them, and re-layouts  3.59 us (2%)
    ppermute x67, waiting for transfers between devices, swap_with(): lax.ppermute(value, axis, [(i, partner_of(i, step, count)) for i in range...  85.8 us
    ppermute x67, starting transfers between devices, swap_with(): lax.ppermute(value, axis, [(i, partner_of(i, step, count)) for i in range...  60.3 us
    pallas_call x26, Pallas kernels, in_vmem(): pl.pallas_call(body, out_shape=shapes, in_specs=[pl.BlockSpec(memory_spac...  24.9 us
    unnamed x34, local copies, waits for them, and re-layouts  3.59 us
  transfers between devices with their start and end apart: 67, of which 24 were waited for; matrix products, arithmetic and copies ran while one was open for 0% of the time, Pallas kernels for 9%

profile of v2, /device:TPU:0, one launch (start us, length us, event | category | flops | bytes accessed | tf_op | source)
XLA Modules:
  0.0 175.7 jit_solution(11810122729741213759)
XLA Ops:
  0.7 1.1 copy-done.9
  1.8 4.1 %collective-permute-start.1 = (bf16[64,1024]{1,0:T(8,128)(2,1)S(1)}, bf16[64,1024]{1,0:T(8,128)(2,1)S(1)}, u32[]{:S(2)}, u32[]{:S(2)}) collective-permute-start(bf16[64,1024]{1,0:T(8,128)(2,1)S(1)} %shard_map.277.refs_0_.refs_4_), channel_id=1, source_target_pairs={{0,4},{2,6},{4,0},{6,2},{1,5},{3,7},{5,1},{7,3},{8,12},{10,14},{12... | collective-permute-start | bytes 393224 | tf_op jit(solution)/shard_map/ppermute | solution.py:47
  5.9 1.6 collective-permute-start
  9.0 1.6 collective-permute-start.7
  10.6 1.5 collective-permute-start.8
  12.9 2.4 %collective-permute-start.9 = (bf16[4,32,1024]{2,1,0:T(8,128)(2,1)S(1)}, bf16[4,32,1024]{2,1,0:T(8,128)(2,1)S(1)}, u32[]{:S(2)}, u32[]{:S(2)}) collective-permute-start(bf16[4,32,1024]{2,1,0:T(8,128)(2,1)S(1)} %shard_map.278.refs_8_), channel_id=1, source_target_pairs={{0,24},{8,16},{16,8},{24,0},{1,25},{9,17},{17,9},{25,1},{2,26},{10... | collective-permute-start | bytes 786440 | tf_op jit(solution)/shard_map/ppermute | solution.py:47
  15.4 2.1 %collective-permute-done.2.refs_3_ = bf16[64,1024]{1,0:T(8,128)(2,1)S(1)} collective-permute-done((bf16[64,1024]{1,0:T(8,128)(2,1)S(1)}, bf16[64,1024]{1,0:T(8,128)(2,1)S(1)}, u32[]{:S(2)}, u32[]{:S(2)}) %collective-permute-start.2) | collective-permute-done | bytes 131104 | tf_op jit(solution)/shard_map/ppermute | solution.py:47
  18.8 5.8 %collective-permute-done.8.refs_10_ = bf16[4,32,1024]{2,1,0:T(8,128)(2,1)S(1)} collective-permute-done((bf16[4,32,1024]{2,1,0:T(8,128)(2,1)S(1)}, bf16[4,32,1024]{2,1,0:T(8,128)(2,1)S(1)}, u32[]{:S(2)}, u32[]{:S(2)}) %collective-permute-start.8) | collective-permute-done | bytes 262176 | tf_op jit(solution)/shard_map/ppermute | solution.py:47
  26.1 2.3 %shard_map.279 = (bf16[512,1024]{1,0:T(8,128)(2,1)S(1)}, bf16[512,1024]{1,0:T(8,128)(2,1)S(1)}, f32[512,384]{1,0:T(8,128)S(1)}, bf16[512,128]{1,0:T(8,128)(2,1)S...) custom-call(bf16[64,1024]{1,0:T(8,128)(2,1)S(1)} %shard_map.277.refs_0_.refs_4_, ...), custom_call_target="tpu_custom_call" | custom-call | flops 536870912 | bytes 6706688 | tf_op jit(solution)/shard_map/pallas_call | solution.py:105
  29.1 1.3 collective-permute-start.29
  31.2 1.3 collective-permute-start.22
  32.5 1.9 %collective-permute-done.21.refs_1_ = bf16[64,1024]{1,0:T(8,128)(2,1)S(1)} collective-permute-done((bf16[64,1024]{1,0:T(8,128)(2,1)S(1)}, bf16[64,1024]{1,0:T(8,128)(2,1)S(1)}, u32[]{:S(2)}, u32[]{:S(2)}) %collective-permute-start.21) | collective-permute-done | bytes 131104 | tf_op jit(solution)/shard_map/ppermute | solution.py:47
  34.5 5.5 %collective-permute-done.22.refs_2_ = bf16[64,1024]{1,0:T(8,128)(2,1)S(1)} collective-permute-done((bf16[64,1024]{1,0:T(8,128)(2,1)S(1)}, bf16[64,1024]{1,0:T(8,128)(2,1)S(1)}, u32[]{:S(2)}, u32[]{:S(2)}) %collective-permute-start.22) | collective-permute-done | bytes 131104 | tf_op jit(solution)/shard_map/ppermute | solution.py:47
  40.7 4.3 %collective-permute-done.23.refs_3_ = bf16[64,1024]{1,0:T(8,128)(2,1)S(1)} collective-permute-done((bf16[64,1024]{1,0:T(8,128)(2,1)S(1)}, bf16[64,1024]{1,0:T(8,128)(2,1)S(1)}, u32[]{:S(2)}, u32[]{:S(2)}) %collective-permute-start.23) | collective-permute-done | bytes 131104 | tf_op jit(solution)/shard_map/ppermute | solution.py:47
  45.0 1.5 collective-permute-start.28
  46.5 2.1 %collective-permute-start.12 = (bf16[64,1024]{1,0:T(8,128)(2,1)S(1)}, bf16[64,1024]{1,0:T(8,128)(2,1)S(1)}, u32[]{:S(2)}, u32[]{:S(2)}) collective-permute-start(bf16[64,1024]{1,0:T(8,128)(2,1)S(1)} %get-tuple-element.99), channel_id=1, source_target_pairs={{0,4},{2,6},{4,0},{6,2},{1,5},{3,7},{5,1},{7,3},{8,12},{10,14},{12... | collective-permute-start | bytes 393224 | tf_op jit(solution)/shard_map/ppermute | solution.py:47
  49.0 2.4 %collective-permute-start.13 = (bf16[64,1024]{1,0:T(8,128)(2,1)S(1)}, bf16[64,1024]{1,0:T(8,128)(2,1)S(1)}, u32[]{:S(2)}, u32[]{:S(2)}) collective-permute-start(bf16[64,1024]{1,0:T(8,128)(2,1)S(1)} %get-tuple-element.100), channel_id=1, source_target_pairs={{0,6},{2,4},{4,2},{6,0},{1,7},{3,5},{5,3},{7,1},{8,14},{10,12},{12... | collective-permute-start | bytes 393224 | tf_op jit(solution)/shard_map/ppermute | solution.py:47
  51.4 1.7 collective-permute-start.32
  53.1 4.9 %collective-permute-done.12.refs_2_ = bf16[64,1024]{1,0:T(8,128)(2,1)S(1)} collective-permute-done((bf16[64,1024]{1,0:T(8,128)(2,1)S(1)}, bf16[64,1024]{1,0:T(8,128)(2,1)S(1)}, u32[]{:S(2)}, u32[]{:S(2)}) %collective-permute-start.12) | collective-permute-done | bytes 131104 | tf_op jit(solution)/shard_map/ppermute | solution.py:47
  59.3 2.1 %collective-permute-start.15 = (bf16[64,1024]{1,0:T(8,128)(2,1)S(1)}, bf16[64,1024]{1,0:T(8,128)(2,1)S(1)}, u32[]{:S(2)}, u32[]{:S(2)}) collective-permute-start(bf16[64,1024]{1,0:T(8,128)(2,1)S(1)} %get-tuple-element.101.refs_0_), channel_id=1, source_target_pairs={{0,4},{2,6},{4,0},{6,2},{1,5},{3,7},{5,1},{7,3},{8,12},{10,14},{12... | collective-permute-start | bytes 393224 | tf_op jit(solution)/shard_map/ppermute | solution.py:47
  62.2 6.2 %collective-permute-done.15.refs_2_ = bf16[64,1024]{1,0:T(8,128)(2,1)S(1)} collective-permute-done((bf16[64,1024]{1,0:T(8,128)(2,1)S(1)}, bf16[64,1024]{1,0:T(8,128)(2,1)S(1)}, u32[]{:S(2)}, u32[]{:S(2)}) %collective-permute-start.15) | collective-permute-done | bytes 131104 | tf_op jit(solution)/shard_map/ppermute | solution.py:47
  69.0 4.8 %collective-permute-done.16.refs_3_ = bf16[64,1024]{1,0:T(8,128)(2,1)S(1)} collective-permute-done((bf16[64,1024]{1,0:T(8,128)(2,1)S(1)}, bf16[64,1024]{1,0:T(8,128)(2,1)S(1)}, u32[]{:S(2)}, u32[]{:S(2)}) %collective-permute-start.16) | collective-permute-done | bytes 131104 | tf_op jit(solution)/shard_map/ppermute | solution.py:47
  75.1 5.2 %shard_map.285 = (bf16[512,1024]{1,0:T(8,128)(2,1)S(1)}, bf16[512,576]{1,0:T(8,128)(2,1)S(1)}, bf16[512,576]{1,0:T(8,128)(2,1)S(1)}, bf16[512,576]{1,0:T(8,128)(...) custom-call(bf16[64,1024]{1,0:T(8,128)(2,1)S(1)} %get-tuple-element.101.refs_0_, ...), custom_call_target="tpu_custom_call" | custom-call | flops 3019898880 | bytes 10027008 | tf_op jit(solution)/shard_map/pallas_call | solution.py:105
  80.5 1.8 %collective-permute-done.39.got_ref = bf16[256,1024]{1,0:T(8,128)(2,1)S(1)} collective-permute-done((bf16[256,1024]{1,0:T(8,128)(2,1)S(1)}, bf16[256,1024]{1,0:T(8,128)(2,1)S(1)}, u32[]{:S(2)}, u32[]{:S(2)}) %collective-permute-start.39) | collective-permute-done | bytes 524320 | tf_op jit(solution)/shard_map/ppermute | solution.py:47
  82.7 2.4 %collective-permute-start.41 = (bf16[64,1024]{1,0:T(8,128)(2,1)S(1)}, bf16[64,1024]{1,0:T(8,128)(2,1)S(1)}, u32[]{:S(2)}, u32[]{:S(2)}) collective-permute-start(bf16[64,1024]{1,0:T(8,128)(2,1)S(1)} %get-tuple-element.119), channel_id=1, source_target_pairs={{0,4},{2,6},{4,0},{6,2},{1,5},{3,7},{5,1},{7,3},{8,12},{10,14},{12... | collective-permute-start | bytes 393224 | tf_op jit(solution)/shard_map/ppermute | solution.py:47
  85.1 1.7 collective-permute-start.42
  86.8 3.2 %collective-permute-done.40.refs_1_ = bf16[64,1024]{1,0:T(8,128)(2,1)S(1)} collective-permute-done((bf16[64,1024]{1,0:T(8,128)(2,1)S(1)}, bf16[64,1024]{1,0:T(8,128)(2,1)S(1)}, u32[]{:S(2)}, u32[]{:S(2)}) %collective-permute-start.40) | collective-permute-done | bytes 131104 | tf_op jit(solution)/shard_map/ppermute | solution.py:47
  90.0 5.6 %collective-permute-done.41.refs_2_ = bf16[64,1024]{1,0:T(8,128)(2,1)S(1)} collective-permute-done((bf16[64,1024]{1,0:T(8,128)(2,1)S(1)}, bf16[64,1024]{1,0:T(8,128)(2,1)S(1)}, u32[]{:S(2)}, u32[]{:S(2)}) %collective-permute-start.41) | collective-permute-done | bytes 131104 | tf_op jit(solution)/shard_map/ppermute | solution.py:47
  95.8 3.1 %collective-permute-start.44 = (bf16[64,1024]{1,0:T(8,128)(2,1)S(1)}, bf16[64,1024]{1,0:T(8,128)(2,1)S(1)}, u32[]{:S(2)}, u32[]{:S(2)}) collective-permute-start(bf16[64,1024]{1,0:T(8,128)(2,1)S(1)} %get-tuple-element.122.refs_0_), channel_id=1, source_target_pairs={{0,4},{2,6},{4,0},{6,2},{1,5},{3,7},{5,1},{7,3},{8,12},{10,14},{12... | collective-permute-start | bytes 393224 | tf_op jit(solution)/shard_map/ppermute | solution.py:47
  98.9 5.2 %collective-permute-done.44.refs_2_ = bf16[64,1024]{1,0:T(8,128)(2,1)S(1)} collective-permute-done((bf16[64,1024]{1,0:T(8,128)(2,1)S(1)}, bf16[64,1024]{1,0:T(8,128)(2,1)S(1)}, u32[]{:S(2)}, u32[]{:S(2)}) %collective-permute-start.44) | collective-permute-done | bytes 131104 | tf_op jit(solution)/shard_map/ppermute | solution.py:47
  107.2 1.9 %collective-permute-done.45.refs_3_ = bf16[64,1024]{1,0:T(8,128)(2,1)S(1)} collective-permute-done((bf16[64,1024]{1,0:T(8,128)(2,1)S(1)}, bf16[64,1024]{1,0:T(8,128)(2,1)S(1)}, u32[]{:S(2)}, u32[]{:S(2)}) %collective-permute-start.45) | collective-permute-done | bytes 131104 | tf_op jit(solution)/shard_map/ppermute | solution.py:47
  109.1 2.2 %shard_map.299 = (f32[3,144,1024]{2,1,0:T(8,128)S(1)}, bf16[3,144,512]{2,1,0:T(8,128)(2,1)S(1)}, bf16[3,144,512]{2,1,0:T(8,128)(2,1)S(1)}, bf16[3,144,512]{2,1,0...) custom-call(bf16[512,576]{1,0:T(8,128)(2,1)S(1)} %get-tuple-element., ...), custom_call_target="tpu_custom_call" | custom-call | flops 1811939328 | bytes 8290304 | tf_op jit(solution)/shard_map/pallas_call | solution.py:105
  111.3 2.2 %collective-permute-start.59 = (bf16[3,144,512]{2,1,0:T(8,128)(2,1)S(1)}, bf16[3,144,512]{2,1,0:T(8,128)(2,1)S(1)}, u32[]{:S(2)}, u32[]{:S(2)}) collective-permute-start(bf16[3,144,512]{2,1,0:T(8,128)(2,1)S(1)} %get-tuple-element.150), channel_id=1, source_target_pairs={{0,8},{8,0},{16,24},{24,16},{1,9},{9,1},{17,25},{25,17},{2,10},{10... | collective-permute-start | bytes 1327112 | tf_op jit(solution)/shard_map/ppermute | solution.py:47
  114.5 2.1 %shard_map.293 = (bf16[512,1024]{1,0:T(8,128)(2,1)S(1)}, bf16[512,384]{1,0:T(8,128)(2,1)S(1)}, f32[264,1024]{1,0:T(8,128)S(1)}, bf16[272,1024]{1,0:T(8,128)(2,1)S(1)}) custom-call(bf16[64,1024]{1,0:T(8,128)(2,1)S(1)} %get-tuple-element.122.refs_0_, bf16[64,1024]{1,0:T(8,128)(2,1)S(1)} %collective-permute-done.43.refs_1_, ...), custom_call_target="tpu_custom_call" | custom-call | flops 536870912 | bytes 7026176 | tf_op jit(solution)/shard_map/pallas_call | solution.py:105
  118.2 6.4 %collective-permute-done.59.refs_1_ = bf16[3,144,512]{2,1,0:T(8,128)(2,1)S(1)} collective-permute-done((bf16[3,144,512]{2,1,0:T(8,128)(2,1)S(1)}, bf16[3,144,512]{2,1,0:T(8,128)(2,1)S(1)}, u32[]{:S(2)}, u32[]{:S(2)}) %collective-permute-start.59) | collective-permute-done | bytes 442400 | tf_op jit(solution)/shard_map/ppermute | solution.py:47
  125.4 1.2 collective-permute-done.60.refs_3_
  127.8 6.1 %collective-permute-done.58.refs_1_ = bf16[3,144,512]{2,1,0:T(8,128)(2,1)S(1)} collective-permute-done((bf16[3,144,512]{2,1,0:T(8,128)(2,1)S(1)}, bf16[3,144,512]{2,1,0:T(8,128)(2,1)S(1)}, u32[]{:S(2)}, u32[]{:S(2)}) %collective-permute-start.58) | collective-permute-done | bytes 442400 | tf_op jit(solution)/shard_map/ppermute | solution.py:47
  133.9 1.7 collective-permute-start.62
  136.1 1.9 %collective-permute-start.37 = (bf16[64,1024]{1,0:T(8,128)(2,1)S(1)}, bf16[64,1024]{1,0:T(8,128)(2,1)S(1)}, u32[]{:S(2)}, u32[]{:S(2)}) collective-permute-start(bf16[64,1024]{1,0:T(8,128)(2,1)S(1)} %shard_map.288), channel_id=1, source_target_pairs={{0,4},{2,6},{4,0},{6,2},{1,5},{3,7},{5,1},{7,3},{8,12},{10,14},{12... | collective-permute-start | bytes 393224 | tf_op jit(solution)/shard_map/ppermute | solution.py:47
  138.1 1.1 collective-permute-start.51
  139.2 5.6 %collective-permute-done.35.refs_1_ = bf16[64,1024]{1,0:T(8,128)(2,1)S(1)} collective-permute-done((bf16[64,1024]{1,0:T(8,128)(2,1)S(1)}, bf16[64,1024]{1,0:T(8,128)(2,1)S(1)}, u32[]{:S(2)}, u32[]{:S(2)}) %collective-permute-start.35) | collective-permute-done | bytes 131104 | tf_op jit(solution)/shard_map/ppermute | solution.py:47
  144.8 3.0 %collective-permute-start.53 = (bf16[72,1024]{1,0:T(8,128)(2,1)S(1)}, bf16[72,1024]{1,0:T(8,128)(2,1)S(1)}, u32[]{:S(2)}, u32[]{:S(2)}) collective-permute-start(bf16[72,1024]{1,0:T(8,128)(2,1)S(1)} %get-tuple-element.133), channel_id=1, source_target_pairs={{0,6},{2,4},{4,2},{6,0},{1,7},{3,5},{5,3},{7,1},{8,14},{10,12},{12... | collective-permute-start | bytes 442376 | tf_op jit(solution)/shard_map/ppermute | solution.py:47
  149.1 6.8 %collective-permute-done.52.refs_2_ = bf16[72,1024]{1,0:T(8,128)(2,1)S(1)} collective-permute-done((bf16[72,1024]{1,0:T(8,128)(2,1)S(1)}, bf16[72,1024]{1,0:T(8,128)(2,1)S(1)}, u32[]{:S(2)}, u32[]{:S(2)}) %collective-permute-start.52) | collective-permute-done | bytes 147488 | tf_op jit(solution)/shard_map/ppermute | solution.py:47
  159.9 1.5 collective-permute-start.64
  162.4 3.0 %collective-permute-done.56.refs_2_ = bf16[4,32,1024]{2,1,0:T(8,128)(2,1)S(1)} collective-permute-done((bf16[4,32,1024]{2,1,0:T(8,128)(2,1)S(1)}, bf16[4,32,1024]{2,1,0:T(8,128)(2,1)S(1)}, u32[]{:S(2)}, u32[]{:S(2)}) %collective-permute-start.56) | collective-permute-done | bytes 262176 | tf_op jit(solution)/shard_map/ppermute | solution.py:47
  165.4 1.1 collective-permute-start.66
  166.5 4.5 %shard_map.301 = (f32[3,144,1024]{2,1,0:T(8,128)}, f32[3,144,1024]{2,1,0:T(8,128)}, f32[3,144,1024]{2,1,0:T(8,128)}, f32[3,144,1024]{2,1,0:T(8,128)}) custom-call(f32[3,144,1024]{2,1,0:T(8,128)S(1)} %get-tuple-element.147.refs_0_, bf16[3,144,512]{2,1,0:T(8,128)(2,1)S(1)} %collective-permute-done.58.refs_1_, ...), custom_call_target="tpu_custom_call" | custom-call | bytes 15925248 | tf_op jit(solution)/shard_map/pallas_call | solution.py:105
  171.8 2.3 %shard_map.298 = (f32[32,4,1024]{2,1,0:T(4,128)}, f32[32,4,1024]{2,1,0:T(4,128)}, f32[32,4,1024]{2,1,0:T(4,128)}, f32[32,4,1024]{2,1,0:T(4,128)}) custom-call(f32[4,32,1024]{2,1,0:T(8,128)S(1)} %get-tuple-element.139.refs_0_, bf16[4,32,1024]{2,1,0:T(8,128)(2,1)S(1)} %collective-permute-done.55.refs_1_, ...), custom_call_target="tpu_custom_call" | custom-call | bytes 4980736 | tf_op jit(solution)/shard_map/pallas_call | solution.py:105
  (146 shorter events, 29.4 us)
Async XLA Ops:
  1.8 10.5 %collective-permute-start.1 = (bf16[64,1024]{1,0:T(8,128)(2,1)S(1)}, bf16[64,1024]{1,0:T(8,128)(2,1)S(1)}, u32[]{:S(2)}, u32[]{:S(2)}) collective-permute-start(bf16[64,1024]{1,0:T(8,128)(2,1)S(1)} %shard_map.277.refs_0_.refs_4_), channel_id=1, source_target_pairs={{0,4},{2,6},{4,0},{6,2},{1,5},{3,7},{5,1},{7,3},{8,12},{10,14},{12... | collective-permute-start | bytes 393224 | tf_op jit(solution)/shard_map/ppermute | solution.py:47
  5.9 7.0 %collective-permute-start = (bf16[64,1024]{1,0:T(8,128)(2,1)S(1)}, bf16[64,1024]{1,0:T(8,128)(2,1)S(1)}, u32[]{:S(2)}, u32[]{:S(2)}) collective-permute-start(bf16[64,1024]{1,0:T(8,128)(2,1)S(1)} %shard_map.277.refs_0_.refs_4_), channel_id=1, source_target_pairs={{0,2},{2,0},{4,6},{6,4},{1,3},{3,1},{5,7},{7,5},{8,10},{10,8},{12,... | collective-permute-start | bytes 393224 | tf_op jit(solution)/shard_map/ppermute | solution.py:47
  7.5 7.9 %collective-permute-start.3 = (bf16[64,1024]{1,0:T(8,128)(2,1)S(1)}, bf16[64,1024]{1,0:T(8,128)(2,1)S(1)}, u32[]{:S(2)}, u32[]{:S(2)}) collective-permute-start(bf16[64,1024]{1,0:T(8,128)(2,1)S(1)} %shard_map.277.refs_0_.refs_4_), channel_id=1, source_target_pairs={{0,1},{1,0},{2,3},{3,2},{4,5},{5,4},{6,7},{7,6},{8,9},{9,8},{10,11... | collective-permute-start | bytes 393224 | tf_op jit(solution)/shard_map/ppermute | solution.py:47
  9.0 9.8 %collective-permute-start.7 = (bf16[4,32,1024]{2,1,0:T(8,128)(2,1)S(1)}, bf16[4,32,1024]{2,1,0:T(8,128)(2,1)S(1)}, u32[]{:S(2)}, u32[]{:S(2)}) collective-permute-start(bf16[4,32,1024]{2,1,0:T(8,128)(2,1)S(1)} %shard_map.278.refs_8_), channel_id=1, source_target_pairs={{0,8},{8,0},{16,24},{24,16},{1,9},{9,1},{17,25},{25,17},{2,10},{10... | collective-permute-start | bytes 786440 | tf_op jit(solution)/shard_map/ppermute | solution.py:47
  10.6 14.1 %collective-permute-start.8 = (bf16[4,32,1024]{2,1,0:T(8,128)(2,1)S(1)}, bf16[4,32,1024]{2,1,0:T(8,128)(2,1)S(1)}, u32[]{:S(2)}, u32[]{:S(2)}) collective-permute-start(bf16[4,32,1024]{2,1,0:T(8,128)(2,1)S(1)} %shard_map.278.refs_8_), channel_id=1, source_target_pairs={{0,16},{8,24},{16,0},{24,8},{1,17},{9,25},{17,1},{25,9},{2,18},{10... | collective-permute-start | bytes 786440 | tf_op jit(solution)/shard_map/ppermute | solution.py:47
  12.9 11.7 %collective-permute-start.9 = (bf16[4,32,1024]{2,1,0:T(8,128)(2,1)S(1)}, bf16[4,32,1024]{2,1,0:T(8,128)(2,1)S(1)}, u32[]{:S(2)}, u32[]{:S(2)}) collective-permute-start(bf16[4,32,1024]{2,1,0:T(8,128)(2,1)S(1)} %shard_map.278.refs_8_), channel_id=1, source_target_pairs={{0,24},{8,16},{16,8},{24,0},{1,25},{9,17},{17,9},{25,1},{2,26},{10... | collective-permute-start | bytes 786440 | tf_op jit(solution)/shard_map/ppermute | solution.py:47
  17.5 7.2 %collective-permute-start.6 = (bf16[64,1024]{1,0:T(8,128)(2,1)S(1)}, bf16[64,1024]{1,0:T(8,128)(2,1)S(1)}, u32[]{:S(2)}, u32[]{:S(2)}) collective-permute-start(bf16[64,1024]{1,0:T(8,128)(2,1)S(1)} %collective-permute-done.2.refs_3_), channel_id=1, source_target_pairs={{0,1},{1,0},{2,3},{3,2},{4,5},{5,4},{6,7},{7,6},{8,9},{9,8},{10,11... | collective-permute-start | bytes 393224 | tf_op jit(solution)/shard_map/ppermute | solution.py:47
  28.4 11.7 %collective-permute-start.10 = (bf16[256,1024]{1,0:T(8,128)(2,1)S(1)}, bf16[256,1024]{1,0:T(8,128)(2,1)S(1)}, u32[]{:S(2)}, u32[]{:S(2)}) collective-permute-start(bf16[256,1024]{1,0:T(8,128)(2,1)S(1)} %get-tuple-element.96), channel_id=1, source_target_pairs={{0,1},{1,0},{2,3},{3,2},{4,5},{5,4},{6,7},{7,6},{8,9},{9,8},{10,11... | collective-permute-start | bytes 1572872 | tf_op jit(solution)/shard_map/ppermute | solution.py:47
  29.1 19.4 %collective-permute-start.29 = (bf16[3,144,512]{2,1,0:T(8,128)(2,1)S(1)}, bf16[3,144,512]{2,1,0:T(8,128)(2,1)S(1)}, u32[]{:S(2)}, u32[]{:S(2)}) collective-permute-start(bf16[3,144,512]{2,1,0:T(8,128)(2,1)S(1)} %get-tuple-element.103.refs_9_), channel_id=1, source_target_pairs={{0,8},{8,0},{16,24},{24,16},{1,9},{9,1},{17,25},{25,17},{2,10},{10... | collective-permute-start | bytes 1327112 | tf_op jit(solution)/shard_map/ppermute | solution.py:47
  30.4 18.6 %collective-permute-start.30 = (bf16[3,144,512]{2,1,0:T(8,128)(2,1)S(1)}, bf16[3,144,512]{2,1,0:T(8,128)(2,1)S(1)}, u32[]{:S(2)}, u32[]{:S(2)}) collective-permute-start(bf16[3,144,512]{2,1,0:T(8,128)(2,1)S(1)} %get-tuple-element.102.refs_8_), channel_id=1, source_target_pairs={{0,16},{8,24},{16,0},{24,8},{1,17},{9,25},{17,1},{25,9},{2,18},{10... | collective-permute-start | bytes 1327112 | tf_op jit(solution)/shard_map/ppermute | solution.py:47
  31.2 8.8 %collective-permute-start.22 = (bf16[64,1024]{1,0:T(8,128)(2,1)S(1)}, bf16[64,1024]{1,0:T(8,128)(2,1)S(1)}, u32[]{:S(2)}, u32[]{:S(2)}) collective-permute-start(bf16[64,1024]{1,0:T(8,128)(2,1)S(1)} %shard_map.282.refs_0_.refs_6_), channel_id=1, source_target_pairs={{0,4},{2,6},{4,0},{6,2},{1,5},{3,7},{5,1},{7,3},{8,12},{10,14},{12... | collective-permute-start | bytes 393224 | tf_op jit(solution)/shard_map/ppermute | solution.py:47
  45.0 6.4 %collective-permute-start.11 = (bf16[64,1024]{1,0:T(8,128)(2,1)S(1)}, bf16[64,1024]{1,0:T(8,128)(2,1)S(1)}, u32[]{:S(2)}, u32[]{:S(2)}) collective-permute-start(bf16[64,1024]{1,0:T(8,128)(2,1)S(1)} %get-tuple-element.98), channel_id=1, source_target_pairs={{0,2},{2,0},{4,6},{6,4},{1,3},{3,1},{5,7},{7,5},{8,10},{10,8},{12,... | collective-permute-start | bytes 393224 | tf_op jit(solution)/shard_map/ppermute | solution.py:47
  45.0 16.4 %collective-permute-start.28 = (bf16[3,144,512]{2,1,0:T(8,128)(2,1)S(1)}, bf16[3,144,512]{2,1,0:T(8,128)(2,1)S(1)}, u32[]{:S(2)}, u32[]{:S(2)}) collective-permute-start(bf16[3,144,512]{2,1,0:T(8,128)(2,1)S(1)} %get-tuple-element.102.refs_8_), channel_id=1, source_target_pairs={{0,8},{8,0},{16,24},{24,16},{1,9},{9,1},{17,25},{25,17},{2,10},{10... | collective-permute-start | bytes 1327112 | tf_op jit(solution)/shard_map/ppermute | solution.py:47
  46.5 11.5 %collective-permute-start.12 = (bf16[64,1024]{1,0:T(8,128)(2,1)S(1)}, bf16[64,1024]{1,0:T(8,128)(2,1)S(1)}, u32[]{:S(2)}, u32[]{:S(2)}) collective-permute-start(bf16[64,1024]{1,0:T(8,128)(2,1)S(1)} %get-tuple-element.99), channel_id=1, source_target_pairs={{0,4},{2,6},{4,0},{6,2},{1,5},{3,7},{5,1},{7,3},{8,12},{10,14},{12... | collective-permute-start | bytes 393224 | tf_op jit(solution)/shard_map/ppermute | solution.py:47
  48.5 19.8 %collective-permute-start.31 = (bf16[3,144,512]{2,1,0:T(8,128)(2,1)S(1)}, bf16[3,144,512]{2,1,0:T(8,128)(2,1)S(1)}, u32[]{:S(2)}, u32[]{:S(2)}) collective-permute-start(bf16[3,144,512]{2,1,0:T(8,128)(2,1)S(1)} %get-tuple-element.103.refs_9_), channel_id=1, source_target_pairs={{0,16},{8,24},{16,0},{24,8},{1,17},{9,25},{17,1},{25,9},{2,18},{10... | collective-permute-start | bytes 1327112 | tf_op jit(solution)/shard_map/ppermute | solution.py:47
  49.0 8.9 %collective-permute-start.13 = (bf16[64,1024]{1,0:T(8,128)(2,1)S(1)}, bf16[64,1024]{1,0:T(8,128)(2,1)S(1)}, u32[]{:S(2)}, u32[]{:S(2)}) collective-permute-start(bf16[64,1024]{1,0:T(8,128)(2,1)S(1)} %get-tuple-element.100), channel_id=1, source_target_pairs={{0,6},{2,4},{4,2},{6,0},{1,7},{3,5},{5,3},{7,1},{8,14},{10,12},{12... | collective-permute-start | bytes 393224 | tf_op jit(solution)/shard_map/ppermute | solution.py:47
  51.4 17.0 %collective-permute-start.32 = (bf16[3,144,512]{2,1,0:T(8,128)(2,1)S(1)}, bf16[3,144,512]{2,1,0:T(8,128)(2,1)S(1)}, u32[]{:S(2)}, u32[]{:S(2)}) collective-permute-start(bf16[3,144,512]{2,1,0:T(8,128)(2,1)S(1)} %collective-permute-done.30.refs_12_), channel_id=1, source_target_pairs={{0,8},{8,0},{16,24},{24,16},{1,9},{9,1},{17,25},{25,17},{2,10},{10... | collective-permute-start | bytes 1327112 | tf_op jit(solution)/shard_map/ppermute | solution.py:47
  58.0 15.8 %collective-permute-start.33 = (bf16[3,144,512]{2,1,0:T(8,128)(2,1)S(1)}, bf16[3,144,512]{2,1,0:T(8,128)(2,1)S(1)}, u32[]{:S(2)}, u32[]{:S(2)}) collective-permute-start(bf16[3,144,512]{2,1,0:T(8,128)(2,1)S(1)} %collective-permute-done.29.refs_11_), channel_id=1, source_target_pairs={{0,16},{8,24},{16,0},{24,8},{1,17},{9,25},{17,1},{25,9},{2,18},{10... | collective-permute-start | bytes 1327112 | tf_op jit(solution)/shard_map/ppermute | solution.py:47
  59.3 9.0 %collective-permute-start.15 = (bf16[64,1024]{1,0:T(8,128)(2,1)S(1)}, bf16[64,1024]{1,0:T(8,128)(2,1)S(1)}, u32[]{:S(2)}, u32[]{:S(2)}) collective-permute-start(bf16[64,1024]{1,0:T(8,128)(2,1)S(1)} %get-tuple-element.101.refs_0_), channel_id=1, source_target_pairs={{0,4},{2,6},{4,0},{6,2},{1,5},{3,7},{5,1},{7,3},{8,12},{10,14},{12... | collective-permute-start | bytes 393224 | tf_op jit(solution)/shard_map/ppermute | solution.py:47
  61.4 7.5 %collective-permute-start.14 = (bf16[64,1024]{1,0:T(8,128)(2,1)S(1)}, bf16[64,1024]{1,0:T(8,128)(2,1)S(1)}, u32[]{:S(2)}, u32[]{:S(2)}) collective-permute-start(bf16[64,1024]{1,0:T(8,128)(2,1)S(1)} %get-tuple-element.101.refs_0_), channel_id=1, source_target_pairs={{0,2},{2,0},{4,6},{6,4},{1,3},{3,1},{5,7},{7,5},{8,10},{10,8},{12,... | collective-permute-start | bytes 393224 | tf_op jit(solution)/shard_map/ppermute | solution.py:47
  82.4 7.6 %collective-permute-start.40 = (bf16[64,1024]{1,0:T(8,128)(2,1)S(1)}, bf16[64,1024]{1,0:T(8,128)(2,1)S(1)}, u32[]{:S(2)}, u32[]{:S(2)}) collective-permute-start(bf16[64,1024]{1,0:T(8,128)(2,1)S(1)} %get-tuple-element.118), channel_id=1, source_target_pairs={{0,2},{2,0},{4,6},{6,4},{1,3},{3,1},{5,7},{7,5},{8,10},{10,8},{12,... | collective-permute-start | bytes 393224 | tf_op jit(solution)/shard_map/ppermute | solution.py:47
  82.7 12.9 %collective-permute-start.41 = (bf16[64,1024]{1,0:T(8,128)(2,1)S(1)}, bf16[64,1024]{1,0:T(8,128)(2,1)S(1)}, u32[]{:S(2)}, u32[]{:S(2)}) collective-permute-start(bf16[64,1024]{1,0:T(8,128)(2,1)S(1)} %get-tuple-element.119), channel_id=1, source_target_pairs={{0,4},{2,6},{4,0},{6,2},{1,5},{3,7},{5,1},{7,3},{8,12},{10,14},{12... | collective-permute-start | bytes 393224 | tf_op jit(solution)/shard_map/ppermute | solution.py:47
  85.1 10.5 %collective-permute-start.42 = (bf16[64,1024]{1,0:T(8,128)(2,1)S(1)}, bf16[64,1024]{1,0:T(8,128)(2,1)S(1)}, u32[]{:S(2)}, u32[]{:S(2)}) collective-permute-start(bf16[64,1024]{1,0:T(8,128)(2,1)S(1)} %get-tuple-element.120), channel_id=1, source_target_pairs={{0,6},{2,4},{4,2},{6,0},{1,7},{3,5},{5,3},{7,1},{8,14},{10,12},{12... | collective-permute-start | bytes 393224 | tf_op jit(solution)/shard_map/ppermute | solution.py:47
  95.8 8.3 %collective-permute-start.44 = (bf16[64,1024]{1,0:T(8,128)(2,1)S(1)}, bf16[64,1024]{1,0:T(8,128)(2,1)S(1)}, u32[]{:S(2)}, u32[]{:S(2)}) collective-permute-start(bf16[64,1024]{1,0:T(8,128)(2,1)S(1)} %get-tuple-element.122.refs_0_), channel_id=1, source_target_pairs={{0,4},{2,6},{4,0},{6,2},{1,5},{3,7},{5,1},{7,3},{8,12},{10,14},{12... | collective-permute-start | bytes 393224 | tf_op jit(solution)/shard_map/ppermute | solution.py:47
  98.9 7.8 %collective-permute-start.43 = (bf16[64,1024]{1,0:T(8,128)(2,1)S(1)}, bf16[64,1024]{1,0:T(8,128)(2,1)S(1)}, u32[]{:S(2)}, u32[]{:S(2)}) collective-permute-start(bf16[64,1024]{1,0:T(8,128)(2,1)S(1)} %get-tuple-element.122.refs_0_), channel_id=1, source_target_pairs={{0,2},{2,0},{4,6},{6,4},{1,3},{3,1},{5,7},{7,5},{8,10},{10,8},{12,... | collective-permute-start | bytes 393224 | tf_op jit(solution)/shard_map/ppermute | solution.py:47
  106.1 11.3 %collective-permute-start.34 = (bf16[256,1024]{1,0:T(8,128)(2,1)S(1)}, bf16[256,1024]{1,0:T(8,128)(2,1)S(1)}, u32[]{:S(2)}, u32[]{:S(2)}) collective-permute-start(bf16[256,1024]{1,0:T(8,128)(2,1)S(1)} %get-tuple-element.109), channel_id=1, source_target_pairs={{0,1},{1,0},{2,3},{3,2},{4,5},{5,4},{6,7},{7,6},{8,9},{9,8},{10,11... | collective-permute-start | bytes 1572872 | tf_op jit(solution)/shard_map/ppermute | solution.py:47
  106.7 7.8 %collective-permute-start.48 = (bf16[64,1024]{1,0:T(8,128)(2,1)S(1)}, bf16[64,1024]{1,0:T(8,128)(2,1)S(1)}, u32[]{:S(2)}, u32[]{:S(2)}) collective-permute-start(bf16[64,1024]{1,0:T(8,128)(2,1)S(1)} %collective-permute-done.44.refs_2_), channel_id=1, source_target_pairs={{0,1},{1,0},{2,3},{3,2},{4,5},{5,4},{6,7},{7,6},{8,9},{9,8},{10,11... | collective-permute-start | bytes 393224 | tf_op jit(solution)/shard_map/ppermute | solution.py:47
  106.7 6.8 %collective-permute-start.47 = (bf16[64,1024]{1,0:T(8,128)(2,1)S(1)}, bf16[64,1024]{1,0:T(8,128)(2,1)S(1)}, u32[]{:S(2)}, u32[]{:S(2)}) collective-permute-start(bf16[64,1024]{1,0:T(8,128)(2,1)S(1)} %collective-permute-done.43.refs_1_), channel_id=1, source_target_pairs={{0,1},{1,0},{2,3},{3,2},{4,5},{5,4},{6,7},{7,6},{8,9},{9,8},{10,11... | collective-permute-start | bytes 393224 | tf_op jit(solution)/shard_map/ppermute | solution.py:47
  111.3 13.3 %collective-permute-start.59 = (bf16[3,144,512]{2,1,0:T(8,128)(2,1)S(1)}, bf16[3,144,512]{2,1,0:T(8,128)(2,1)S(1)}, u32[]{:S(2)}, u32[]{:S(2)}) collective-permute-start(bf16[3,144,512]{2,1,0:T(8,128)(2,1)S(1)} %get-tuple-element.150), channel_id=1, source_target_pairs={{0,8},{8,0},{16,24},{24,16},{1,9},{9,1},{17,25},{25,17},{2,10},{10... | collective-permute-start | bytes 1327112 | tf_op jit(solution)/shard_map/ppermute | solution.py:47
  113.6 13.0 %collective-permute-start.60 = (bf16[3,144,512]{2,1,0:T(8,128)(2,1)S(1)}, bf16[3,144,512]{2,1,0:T(8,128)(2,1)S(1)}, u32[]{:S(2)}, u32[]{:S(2)}) collective-permute-start(bf16[3,144,512]{2,1,0:T(8,128)(2,1)S(1)} %get-tuple-element.152), channel_id=1, source_target_pairs={{0,16},{8,24},{16,0},{24,8},{1,17},{9,25},{17,1},{25,9},{2,18},{10... | collective-permute-start | bytes 1327112 | tf_op jit(solution)/shard_map/ppermute | solution.py:47
  116.6 19.5 %collective-permute-start.50 = (bf16[272,1024]{1,0:T(8,128)(2,1)S(1)}, bf16[272,1024]{1,0:T(8,128)(2,1)S(1)}, u32[]{:S(2)}, u32[]{:S(2)}) collective-permute-start(bf16[272,1024]{1,0:T(8,128)(2,1)S(1)} %get-tuple-element.129), channel_id=1, source_target_pairs={{0,1},{1,0},{2,3},{3,2},{4,5},{5,4},{6,7},{7,6},{8,9},{9,8},{10,11... | collective-permute-start | bytes 1671176 | tf_op jit(solution)/shard_map/ppermute | solution.py:47
  116.7 17.2 %collective-permute-start.58 = (bf16[3,144,512]{2,1,0:T(8,128)(2,1)S(1)}, bf16[3,144,512]{2,1,0:T(8,128)(2,1)S(1)}, u32[]{:S(2)}, u32[]{:S(2)}) collective-permute-start(bf16[3,144,512]{2,1,0:T(8,128)(2,1)S(1)} %get-tuple-element.148), channel_id=1, source_target_pairs={{0,8},{8,0},{16,24},{24,16},{1,9},{9,1},{17,25},{25,17},{2,10},{10... | collective-permute-start | bytes 1327112 | tf_op jit(solution)/shard_map/ppermute | solution.py:47
  117.4 20.7 %collective-permute-start.63 = (bf16[3,144,512]{2,1,0:T(8,128)(2,1)S(1)}, bf16[3,144,512]{2,1,0:T(8,128)(2,1)S(1)}, u32[]{:S(2)}, u32[]{:S(2)}) collective-permute-start(bf16[3,144,512]{2,1,0:T(8,128)(2,1)S(1)} %get-tuple-element.155), channel_id=1, source_target_pairs={{0,16},{8,24},{16,0},{24,8},{1,17},{9,25},{17,1},{25,9},{2,18},{10... | collective-permute-start | bytes 1327112 | tf_op jit(solution)/shard_map/ppermute | solution.py:47
  124.6 11.0 %collective-permute-start.36 = (bf16[64,1024]{1,0:T(8,128)(2,1)S(1)}, bf16[64,1024]{1,0:T(8,128)(2,1)S(1)}, u32[]{:S(2)}, u32[]{:S(2)}) collective-permute-start(bf16[64,1024]{1,0:T(8,128)(2,1)S(1)} %get-tuple-element.113), channel_id=1, source_target_pairs={{0,2},{2,0},{4,6},{6,4},{1,3},{3,1},{5,7},{7,5},{8,10},{10,8},{12,... | collective-permute-start | bytes 393224 | tf_op jit(solution)/shard_map/ppermute | solution.py:47
  126.8 31.3 %collective-permute-start.61 = (bf16[3,144,512]{2,1,0:T(8,128)(2,1)S(1)}, bf16[3,144,512]{2,1,0:T(8,128)(2,1)S(1)}, u32[]{:S(2)}, u32[]{:S(2)}) collective-permute-start(bf16[3,144,512]{2,1,0:T(8,128)(2,1)S(1)} %get-tuple-element.153), channel_id=1, source_target_pairs={{0,16},{8,24},{16,0},{24,8},{1,17},{9,25},{17,1},{25,9},{2,18},{10... | collective-permute-start | bytes 1327112 | tf_op jit(solution)/shard_map/ppermute | solution.py:47
  133.9 24.4 %collective-permute-start.62 = (bf16[3,144,512]{2,1,0:T(8,128)(2,1)S(1)}, bf16[3,144,512]{2,1,0:T(8,128)(2,1)S(1)}, u32[]{:S(2)}, u32[]{:S(2)}) collective-permute-start(bf16[3,144,512]{2,1,0:T(8,128)(2,1)S(1)} %get-tuple-element.154), channel_id=1, source_target_pairs={{0,8},{8,0},{16,24},{24,16},{1,9},{9,1},{17,25},{25,17},{2,10},{10... | collective-permute-start | bytes 1327112 | tf_op jit(solution)/shard_map/ppermute | solution.py:47
  135.6 9.1 %collective-permute-start.35 = (bf16[64,1024]{1,0:T(8,128)(2,1)S(1)}, bf16[64,1024]{1,0:T(8,128)(2,1)S(1)}, u32[]{:S(2)}, u32[]{:S(2)}) collective-permute-start(bf16[64,1024]{1,0:T(8,128)(2,1)S(1)} %get-tuple-element.111), channel_id=1, source_target_pairs={{0,2},{2,0},{4,6},{6,4},{1,3},{3,1},{5,7},{7,5},{8,10},{10,8},{12,... | collective-permute-start | bytes 393224 | tf_op jit(solution)/shard_map/ppermute | solution.py:47
  136.1 8.7 %collective-permute-start.37 = (bf16[64,1024]{1,0:T(8,128)(2,1)S(1)}, bf16[64,1024]{1,0:T(8,128)(2,1)S(1)}, u32[]{:S(2)}, u32[]{:S(2)}) collective-permute-start(bf16[64,1024]{1,0:T(8,128)(2,1)S(1)} %shard_map.288), channel_id=1, source_target_pairs={{0,4},{2,6},{4,0},{6,2},{1,5},{3,7},{5,1},{7,3},{8,12},{10,14},{12... | collective-permute-start | bytes 393224 | tf_op jit(solution)/shard_map/ppermute | solution.py:47
  138.1 10.5 %collective-permute-start.51 = (bf16[72,1024]{1,0:T(8,128)(2,1)S(1)}, bf16[72,1024]{1,0:T(8,128)(2,1)S(1)}, u32[]{:S(2)}, u32[]{:S(2)}) collective-permute-start(bf16[72,1024]{1,0:T(8,128)(2,1)S(1)} %get-tuple-element.131), channel_id=1, source_target_pairs={{0,2},{2,0},{4,6},{6,4},{1,3},{3,1},{5,7},{7,5},{8,10},{10,8},{12,... | collective-permute-start | bytes 442376 | tf_op jit(solution)/shard_map/ppermute | solution.py:47
  144.8 11.1 %collective-permute-start.52 = (bf16[72,1024]{1,0:T(8,128)(2,1)S(1)}, bf16[72,1024]{1,0:T(8,128)(2,1)S(1)}, u32[]{:S(2)}, u32[]{:S(2)}) collective-permute-start(bf16[72,1024]{1,0:T(8,128)(2,1)S(1)} %get-tuple-element.132), channel_id=1, source_target_pairs={{0,4},{2,6},{4,0},{6,2},{1,5},{3,7},{5,1},{7,3},{8,12},{10,14},{12... | collective-permute-start | bytes 442376 | tf_op jit(solution)/shard_map/ppermute | solution.py:47
  144.8 12.1 %collective-permute-start.53 = (bf16[72,1024]{1,0:T(8,128)(2,1)S(1)}, bf16[72,1024]{1,0:T(8,128)(2,1)S(1)}, u32[]{:S(2)}, u32[]{:S(2)}) collective-permute-start(bf16[72,1024]{1,0:T(8,128)(2,1)S(1)} %get-tuple-element.133), channel_id=1, source_target_pairs={{0,6},{2,4},{4,2},{6,0},{1,7},{3,5},{5,3},{7,1},{8,14},{10,12},{12... | collective-permute-start | bytes 442376 | tf_op jit(solution)/shard_map/ppermute | solution.py:47
  148.6 12.8 %collective-permute-start.55 = (bf16[4,32,1024]{2,1,0:T(8,128)(2,1)S(1)}, bf16[4,32,1024]{2,1,0:T(8,128)(2,1)S(1)}, u32[]{:S(2)}, u32[]{:S(2)}) collective-permute-start(bf16[4,32,1024]{2,1,0:T(8,128)(2,1)S(1)} %get-tuple-element.140), channel_id=1, source_target_pairs={{0,8},{8,0},{16,24},{24,16},{1,9},{9,1},{17,25},{25,17},{2,10},{10... | collective-permute-start | bytes 786440 | tf_op jit(solution)/shard_map/ppermute | solution.py:47
  155.9 9.5 %collective-permute-start.56 = (bf16[4,32,1024]{2,1,0:T(8,128)(2,1)S(1)}, bf16[4,32,1024]{2,1,0:T(8,128)(2,1)S(1)}, u32[]{:S(2)}, u32[]{:S(2)}) collective-permute-start(bf16[4,32,1024]{2,1,0:T(8,128)(2,1)S(1)} %get-tuple-element.141), channel_id=1, source_target_pairs={{0,16},{8,24},{16,0},{24,8},{1,17},{9,25},{17,1},{25,9},{2,18},{10... | collective-permute-start | bytes 786440 | tf_op jit(solution)/shard_map/ppermute | solution.py:47
  156.9 14.9 %collective-permute-start.57 = (bf16[4,32,1024]{2,1,0:T(8,128)(2,1)S(1)}, bf16[4,32,1024]{2,1,0:T(8,128)(2,1)S(1)}, u32[]{:S(2)}, u32[]{:S(2)}) collective-permute-start(bf16[4,32,1024]{2,1,0:T(8,128)(2,1)S(1)} %get-tuple-element.142), channel_id=1, source_target_pairs={{0,24},{8,16},{16,8},{24,0},{1,25},{9,17},{17,9},{25,1},{2,26},{10... | collective-permute-start | bytes 786440 | tf_op jit(solution)/shard_map/ppermute | solution.py:47
  158.1 16.8 %collective-permute-start.54 = (f32[64,1024]{1,0:T(8,128)S(1)}, f32[64,1024]{1,0:T(8,128)S(1)}, u32[]{:S(2)}, u32[]{:S(2)}) collective-permute-start(f32[64,1024]{1,0:T(8,128)S(1)} %get-tuple-element.135.mine_ref), channel_id=1, source_target_pairs={{0,1},{1,0},{2,3},{3,2},{4,5},{5,4},{6,7},{7,6},{8,9},{9,8},{10,11... | collective-permute-start | bytes 786440 | tf_op jit(solution)/shard_map/ppermute | solution.py:47
  159.9 14.2 %collective-permute-start.64 = (f32[8,1024]{1,0:T(8,128)S(1)}, f32[8,1024]{1,0:T(8,128)S(1)}, u32[]{:S(2)}, u32[]{:S(2)}) collective-permute-start(f32[8,1024]{1,0:T(8,128)S(1)} %get-tuple-element.157.refs_0_), channel_id=1, source_target_pairs={{0,8},{8,0},{16,24},{24,16},{1,9},{9,1},{17,25},{25,17},{2,10},{10... | collective-permute-start | bytes 98312 | tf_op jit(solution)/shard_map/ppermute | solution.py:47
  161.4 12.7 %collective-permute-start.65 = (f32[8,1024]{1,0:T(8,128)S(1)}, f32[8,1024]{1,0:T(8,128)S(1)}, u32[]{:S(2)}, u32[]{:S(2)}) collective-permute-start(f32[8,1024]{1,0:T(8,128)S(1)} %get-tuple-element.157.refs_0_), channel_id=1, source_target_pairs={{0,16},{8,24},{16,0},{24,8},{1,17},{9,25},{17,1},{25,9},{2,18},{10... | collective-permute-start | bytes 98312 | tf_op jit(solution)/shard_map/ppermute | solution.py:47
  165.4 8.7 %collective-permute-start.66 = (f32[8,1024]{1,0:T(8,128)S(1)}, f32[8,1024]{1,0:T(8,128)S(1)}, u32[]{:S(2)}, u32[]{:S(2)}) collective-permute-start(f32[8,1024]{1,0:T(8,128)S(1)} %get-tuple-element.157.refs_0_), channel_id=1, source_target_pairs={{0,24},{8,16},{16,8},{24,0},{1,25},{9,17},{17,9},{25,1},{2,26},{10... | collective-permute-start | bytes 98312 | tf_op jit(solution)/shard_map/ppermute | solution.py:47
  (36 other events, 213.8 us)

commit v3 on v2

--- a/solution.py
+++ b/solution.py
@@ -272,46 +272,43 @@
         down_ref[at : at + block, side] = part[2]
 
 
-def ffn_rows(count, *refs):
-    pieces = refs[: 2 * count]
-    g_ref, w_ref, down_ref, h_ref, act_ref, gate_ref, up_ref, keep_ref, send_ref = refs[2 * count :]
+def ffn_rows(count, first, *refs):
+    pieces = refs[:count]
+    g_ref, w_ref, down_ref, h_ref, act_ref, gate_ref, up_ref, part_ref = refs[count:]
     rows, hidden = pieces[0].shape[0], down_ref.shape[0]
-    for j in range(2 * count):
+    for j in range(count):
         h_ref[j * rows : (j + 1) * rows, :] = pieces[j][...]
-    side_rows = count * rows
-    for at, out_ref in ((side_rows, send_ref), (0, keep_ref)):
-        these = slice(at, at + side_rows)
-        gate = by_rows(h_ref[these, :], w_ref[:hidden, :])
-        up = by_rows(h_ref[these, :], w_ref[hidden:, :])
-        sigmoid = jax.nn.sigmoid(gate)
-        gate_act = gate * sigmoid
-        act_ref[these, :] = (gate_act * up).astype(bf16)
-        grad_act = by_rows(g_ref[these, :], down_ref[...])
-        up_ref[these, :] = (grad_act * gate_act).astype(bf16)
-        gate_ref[these, :] = (
-            grad_act * up * sigmoid * (1.0 + gate * (1.0 - sigmoid))
-        ).astype(bf16)
-        part = jnp.dot(gate_ref[these, :], w_ref[:hidden, :], preferred_element_type=f32)
-        part = part + jnp.dot(up_ref[these, :], w_ref[hidden:, :], preferred_element_type=f32)
+    gate = by_rows(h_ref[...], w_ref[:hidden, :])
+    up = by_rows(h_ref[...], w_ref[hidden:, :])
+    sigmoid = jax.nn.sigmoid(gate)
+    gate_act = gate * sigmoid
+    act_ref[...] = (gate_act * up).astype(bf16)
+    grad_act = by_rows(g_ref[first : first + count * rows, :], down_ref[...])
+    up_ref[...] = (grad_act * gate_act).astype(bf16)
+    gate_ref[...] = (grad_act * up * sigmoid * (1.0 + gate * (1.0 - sigmoid))).astype(bf16)
+    part = jnp.dot(gate_ref[...], w_ref[:hidden, :], preferred_element_type=f32)
+    part = part + jnp.dot(up_ref[...], w_ref[hidden:, :], preferred_element_type=f32)
+    part_ref[...] = part.astype(part_ref.dtype)
+
+
+def ffn_down(mine_ref, other_ref, down_ref, keep_ref, send_ref):
+    for act_ref, out_ref in ((other_ref, send_ref), (mine_ref, keep_ref)):
+        part = jnp.dot(act_ref[...], down_ref[...], preferred_element_type=f32)
         out_ref[...] = part.astype(out_ref.dtype)
 
 
-def ffn_down(act_ref, down_ref, keep_ref, send_ref):
-    half = keep_ref.shape[0]
-    for at, out_ref in ((half, send_ref), (0, keep_ref)):
-        part = jnp.dot(act_ref[at : at + half, :], down_ref[...], preferred_element_type=f32)
-        out_ref[...] = part.astype(out_ref.dtype)
-
-
-def ffn_weight_grads(gate_ref, up_ref, act_ref, h_ref, g_ref, *outs):
-    own_ref, halves = outs[0], outs[1:]
+def ffn_weight_grads(*refs):
+    mine, other = refs[:4], refs[4:8]
+    g_ref, own_ref, *halves = refs[8:]
     block, columns = own_ref.shape[1], halves[0].shape[2]
-    for k, (left, right) in enumerate(((gate_ref, h_ref), (up_ref, h_ref), (act_ref, g_ref))):
-        term = down_rows(left[...], right[...])
+    count = mine[0].shape[0]
+    for k, at in enumerate((2, 3, 1)):
+        rights = (g_ref[:count, :], g_ref[count:, :]) if at == 1 else (mine[0][...], other[0][...])
+        term = down_rows(mine[at][...], rights[0]) + down_rows(other[at][...], rights[1])
         own_ref[k] = term[:block]
         for j, out_ref in enumerate(halves):
-            at, side = (1 + j // 2) * block, (j % 2) * columns
-            out_ref[k] = term[at : at + block, side : side + columns].astype(bf16)
+            row, side = (1 + j // 2) * block, (j % 2) * columns
+            out_ref[k] = term[row : row + block, side : side + columns].astype(bf16)
 
 
 def ffn_adam(half_parts, *refs):
@@ -540,7 +537,7 @@
         norm_gains,
     )
 
-    hidden_rows = ((seq_len, hidden), bf16)
+    hidden_rows = ((mine_count, hidden), bf16)
     g_all, gate_up_w, down_w = in_vmem(
         functools.partial(ffn_gather, ctx_count),
         [
@@ -551,15 +548,21 @@
         *g_pieces,
         *ffn_parts,
     )
-    h_two, act, grad_gate, grad_up, kept, sent = in_vmem(
-        functools.partial(ffn_rows, ctx_count),
-        [((seq_len, width), bf16), hidden_rows, hidden_rows, hidden_rows] + parted,
-        *spread_rows(h_two_own),
-        g_all,
-        gate_up_w,
-        down_w,
-        flops=10 * seq_len * hidden * width,
-    )
+    h_pieces = spread_rows(h_two_own)
+    sides = []
+    for j in range(2):
+        sides.append(
+            in_vmem(
+                functools.partial(ffn_rows, ctx_count, j * mine_count),
+                [((mine_count, width), bf16), hidden_rows, hidden_rows, hidden_rows, parted[j]],
+                *h_pieces[j * ctx_count : (j + 1) * ctx_count],
+                g_all,
+                gate_up_w,
+                down_w,
+                flops=5 * seq_len * hidden * width,
+            )
+        )
+    (*mine, kept), (*other, sent) = sides
     grad_resid, grad_mix_own, gain_two_part = in_vmem(
         second_norm_backward,
         [half_shape, half_sent, ((1, width), f32)],
@@ -569,16 +572,16 @@
         g_half,
         norm_gains,
     )
-    kept, sent = in_vmem(ffn_down, parted, act, down_w, flops=2 * seq_len * hidden * width)
+    kept, sent = in_vmem(
+        ffn_down, parted, mine[1], other[1], down_w, flops=2 * seq_len * hidden * width
+    )
     ffn_pieces = collect_rows(kept, sent, passed=True)
     ffn_terms = in_vmem(
         ffn_weight_grads,
         [((3, ffn_block, width), f32)]
         + [((3, ffn_block, width // 2), bf16)] * (2 * (shard_count - 1)),
-        grad_gate,
-        grad_up,
-        act,
-        h_two,
+        *mine,
+        *other,
         g_all,
         flops=6 * seq_len * hidden * width,
     )

time: 176 us -> 175 us (level)
    pallas_call x26 -> x27, Pallas kernels: 24.9 us -> 25.6 us  [in_vmem(): pl.pallas_call(body, out_shape=shapes, in_specs=[pl.BlockSpec(memory_spac...]
  transfers between devices with their start and end apart: 67 -> 67, of which waited for: 24 -> 23; matrix products, arithmetic and copies ran while one was open for 0% -> 0% of each run, Pallas kernels for 9% -> 11%
where the time goes in v3:
time: 175 us
  waiting for transfers between devices  84.2 us (48%)
  starting transfers between devices  60.5 us (35%)
  Pallas kernels  25.6 us (15%)
  local copies, waits for them, and re-layouts  3.59 us (2%)
    ppermute x67, waiting for transfers between devices, swap_with(): lax.ppermute(value, axis, [(i, partner_of(i, step, count)) for i in range...  84.2 us
    ppermute x67, starting transfers between devices, swap_with(): lax.ppermute(value, axis, [(i, partner_of(i, step, count)) for i in range...  60.5 us
    pallas_call x27, Pallas kernels, in_vmem(): pl.pallas_call(body, out_shape=shapes, in_specs=[pl.BlockSpec(memory_spac...  25.6 us
    unnamed x34, local copies, waits for them, and re-layouts  3.59 us
  transfers between devices with their start and end apart: 67, of which 23 were waited for; matrix products, arithmetic and copies ran while one was open for 0% of the time, Pallas kernels for 11%

profile of v3, /device:TPU:0, one launch (start us, length us, event | category | flops | bytes accessed | tf_op | source)
XLA Modules:
  0.0 175.0 jit_solution(11155167311372762851)
XLA Ops:
  0.7 1.1 copy-done.9
  1.8 4.1 %collective-permute-start.1 = (bf16[64,1024]{1,0:T(8,128)(2,1)S(1)}, bf16[64,1024]{1,0:T(8,128)(2,1)S(1)}, u32[]{:S(2)}, u32[]{:S(2)}) collective-permute-start(bf16[64,1024]{1,0:T(8,128)(2,1)S(1)} %shard_map.277.refs_0_.refs_4_), channel_id=1, source_target_pairs={{0,4},{2,6},{4,0},{6,2},{1,5},{3,7},{5,1},{7,3},{8,12},{10,14},{12... | collective-permute-start | bytes 393224 | tf_op jit(solution)/shard_map/ppermute | solution.py:47
  5.9 1.6 collective-permute-start
  9.0 1.6 collective-permute-start.7
  10.6 1.5 collective-permute-start.8
  12.9 2.4 %collective-permute-start.9 = (bf16[4,32,1024]{2,1,0:T(8,128)(2,1)S(1)}, bf16[4,32,1024]{2,1,0:T(8,128)(2,1)S(1)}, u32[]{:S(2)}, u32[]{:S(2)}) collective-permute-start(bf16[4,32,1024]{2,1,0:T(8,128)(2,1)S(1)} %shard_map.278.refs_8_), channel_id=1, source_target_pairs={{0,24},{8,16},{16,8},{24,0},{1,25},{9,17},{17,9},{25,1},{2,26},{10... | collective-permute-start | bytes 786440 | tf_op jit(solution)/shard_map/ppermute | solution.py:47
  15.4 2.1 %collective-permute-done.2.refs_3_ = bf16[64,1024]{1,0:T(8,128)(2,1)S(1)} collective-permute-done((bf16[64,1024]{1,0:T(8,128)(2,1)S(1)}, bf16[64,1024]{1,0:T(8,128)(2,1)S(1)}, u32[]{:S(2)}, u32[]{:S(2)}) %collective-permute-start.2) | collective-permute-done | bytes 131104 | tf_op jit(solution)/shard_map/ppermute | solution.py:47
  18.8 5.8 %collective-permute-done.8.refs_10_ = bf16[4,32,1024]{2,1,0:T(8,128)(2,1)S(1)} collective-permute-done((bf16[4,32,1024]{2,1,0:T(8,128)(2,1)S(1)}, bf16[4,32,1024]{2,1,0:T(8,128)(2,1)S(1)}, u32[]{:S(2)}, u32[]{:S(2)}) %collective-permute-start.8) | collective-permute-done | bytes 262176 | tf_op jit(solution)/shard_map/ppermute | solution.py:47
  26.1 2.3 %shard_map.279 = (bf16[512,1024]{1,0:T(8,128)(2,1)S(1)}, bf16[512,1024]{1,0:T(8,128)(2,1)S(1)}, f32[512,384]{1,0:T(8,128)S(1)}, bf16[512,128]{1,0:T(8,128)(2,1)S...) custom-call(bf16[64,1024]{1,0:T(8,128)(2,1)S(1)} %shard_map.277.refs_0_.refs_4_, ...), custom_call_target="tpu_custom_call" | custom-call | flops 536870912 | bytes 6706688 | tf_op jit(solution)/shard_map/pallas_call | solution.py:105
  29.1 1.3 collective-permute-start.25
  31.2 1.3 collective-permute-start.18
  32.5 1.9 %collective-permute-done.17.refs_1_ = bf16[64,1024]{1,0:T(8,128)(2,1)S(1)} collective-permute-done((bf16[64,1024]{1,0:T(8,128)(2,1)S(1)}, bf16[64,1024]{1,0:T(8,128)(2,1)S(1)}, u32[]{:S(2)}, u32[]{:S(2)}) %collective-permute-start.17) | collective-permute-done | bytes 131104 | tf_op jit(solution)/shard_map/ppermute | solution.py:47
  34.5 5.5 %collective-permute-done.18.refs_2_ = bf16[64,1024]{1,0:T(8,128)(2,1)S(1)} collective-permute-done((bf16[64,1024]{1,0:T(8,128)(2,1)S(1)}, bf16[64,1024]{1,0:T(8,128)(2,1)S(1)}, u32[]{:S(2)}, u32[]{:S(2)}) %collective-permute-start.18) | collective-permute-done | bytes 131104 | tf_op jit(solution)/shard_map/ppermute | solution.py:47
  40.7 4.3 %collective-permute-done.19.refs_3_ = bf16[64,1024]{1,0:T(8,128)(2,1)S(1)} collective-permute-done((bf16[64,1024]{1,0:T(8,128)(2,1)S(1)}, bf16[64,1024]{1,0:T(8,128)(2,1)S(1)}, u32[]{:S(2)}, u32[]{:S(2)}) %collective-permute-start.19) | collective-permute-done | bytes 131104 | tf_op jit(solution)/shard_map/ppermute | solution.py:47
  45.0 1.5 collective-permute-start.24
  46.5 2.1 %collective-permute-start.12 = (bf16[64,1024]{1,0:T(8,128)(2,1)S(1)}, bf16[64,1024]{1,0:T(8,128)(2,1)S(1)}, u32[]{:S(2)}, u32[]{:S(2)}) collective-permute-start(bf16[64,1024]{1,0:T(8,128)(2,1)S(1)} %get-tuple-element.103), channel_id=1, source_target_pairs={{0,4},{2,6},{4,0},{6,2},{1,5},{3,7},{5,1},{7,3},{8,12},{10,14},{12... | collective-permute-start | bytes 393224 | tf_op jit(solution)/shard_map/ppermute | solution.py:47
  49.1 2.4 %collective-permute-start.13 = (bf16[64,1024]{1,0:T(8,128)(2,1)S(1)}, bf16[64,1024]{1,0:T(8,128)(2,1)S(1)}, u32[]{:S(2)}, u32[]{:S(2)}) collective-permute-start(bf16[64,1024]{1,0:T(8,128)(2,1)S(1)} %get-tuple-element.104), channel_id=1, source_target_pairs={{0,6},{2,4},{4,2},{6,0},{1,7},{3,5},{5,3},{7,1},{8,14},{10,12},{12... | collective-permute-start | bytes 393224 | tf_op jit(solution)/shard_map/ppermute | solution.py:47
  51.4 1.7 collective-permute-start.28
  53.1 4.9 %collective-permute-done.12.refs_2_ = bf16[64,1024]{1,0:T(8,128)(2,1)S(1)} collective-permute-done((bf16[64,1024]{1,0:T(8,128)(2,1)S(1)}, bf16[64,1024]{1,0:T(8,128)(2,1)S(1)}, u32[]{:S(2)}, u32[]{:S(2)}) %collective-permute-start.12) | collective-permute-done | bytes 131104 | tf_op jit(solution)/shard_map/ppermute | solution.py:47
  59.3 2.1 %collective-permute-start.15 = (bf16[64,1024]{1,0:T(8,128)(2,1)S(1)}, bf16[64,1024]{1,0:T(8,128)(2,1)S(1)}, u32[]{:S(2)}, u32[]{:S(2)}) collective-permute-start(bf16[64,1024]{1,0:T(8,128)(2,1)S(1)} %get-tuple-element.105.refs_0_), channel_id=1, source_target_pairs={{0,4},{2,6},{4,0},{6,2},{1,5},{3,7},{5,1},{7,3},{8,12},{10,14},{12... | collective-permute-start | bytes 393224 | tf_op jit(solution)/shard_map/ppermute | solution.py:47
  62.2 6.2 %collective-permute-done.15.refs_2_ = bf16[64,1024]{1,0:T(8,128)(2,1)S(1)} collective-permute-done((bf16[64,1024]{1,0:T(8,128)(2,1)S(1)}, bf16[64,1024]{1,0:T(8,128)(2,1)S(1)}, u32[]{:S(2)}, u32[]{:S(2)}) %collective-permute-start.15) | collective-permute-done | bytes 131104 | tf_op jit(solution)/shard_map/ppermute | solution.py:47
  69.0 4.8 %collective-permute-done.16.refs_3_ = bf16[64,1024]{1,0:T(8,128)(2,1)S(1)} collective-permute-done((bf16[64,1024]{1,0:T(8,128)(2,1)S(1)}, bf16[64,1024]{1,0:T(8,128)(2,1)S(1)}, u32[]{:S(2)}, u32[]{:S(2)}) %collective-permute-start.16) | collective-permute-done | bytes 131104 | tf_op jit(solution)/shard_map/ppermute | solution.py:47
  75.1 3.1 %shard_map.286 = (bf16[256,1024]{1,0:T(8,128)(2,1)S(1)}, bf16[256,576]{1,0:T(8,128)(2,1)S(1)}, bf16[256,576]{1,0:T(8,128)(2,1)S(1)}, bf16[256,576]{1,0:T(8,128)(2,1)S(1)}, bf16[256,1024]{1,0:T(8,128)(2,1)S(1)}) custom-call(bf16[64,1024]{1,0:T(8,128)(2,1)S(1)} %collective-permute-done.30.refs_0_, bf16[64,1024]{1,0:T(8,128)(2,1)S(1)} %collective-permute-done.31.refs_1_, ...), custom_call_target="tpu_custom_call" | custom-call | flops 1509949440 | bytes 7045120 | tf_op jit(solution)/shard_map/pallas_call | solution.py:105
  78.4 3.1 %shard_map.285 = (bf16[256,1024]{1,0:T(8,128)(2,1)S(1)}, bf16[256,576]{1,0:T(8,128)(2,1)S(1)}, bf16[256,576]{1,0:T(8,128)(2,1)S(1)}, bf16[256,576]{1,0:T(8,128)(2,1)S(1)}, f32[256,1024]{1,0:T(8,128)S(1)}) custom-call(bf16[64,1024]{1,0:T(8,128)(2,1)S(1)} %get-tuple-element.105.refs_0_, bf16[64,1024]{1,0:T(8,128)(2,1)S(1)} %collective-permute-done.14.refs_1_, ...), custom_call_target="tpu_custom_call" | custom-call | flops 1509949440 | bytes 7569408 | tf_op jit(solution)/shard_map/pallas_call | solution.py:105
  81.9 2.4 %collective-permute-start.41 = (bf16[64,1024]{1,0:T(8,128)(2,1)S(1)}, bf16[64,1024]{1,0:T(8,128)(2,1)S(1)}, u32[]{:S(2)}, u32[]{:S(2)}) collective-permute-start(bf16[64,1024]{1,0:T(8,128)(2,1)S(1)} %get-tuple-element.124), channel_id=1, source_target_pairs={{0,4},{2,6},{4,0},{6,2},{1,5},{3,7},{5,1},{7,3},{8,12},{10,14},{12... | collective-permute-start | bytes 393224 | tf_op jit(solution)/shard_map/ppermute | solution.py:47
  84.3 1.7 collective-permute-start.42
  86.0 3.5 %collective-permute-done.40.refs_1_ = bf16[64,1024]{1,0:T(8,128)(2,1)S(1)} collective-permute-done((bf16[64,1024]{1,0:T(8,128)(2,1)S(1)}, bf16[64,1024]{1,0:T(8,128)(2,1)S(1)}, u32[]{:S(2)}, u32[]{:S(2)}) %collective-permute-start.40) | collective-permute-done | bytes 131104 | tf_op jit(solution)/shard_map/ppermute | solution.py:47
  89.5 5.3 %collective-permute-done.41.refs_2_ = bf16[64,1024]{1,0:T(8,128)(2,1)S(1)} collective-permute-done((bf16[64,1024]{1,0:T(8,128)(2,1)S(1)}, bf16[64,1024]{1,0:T(8,128)(2,1)S(1)}, u32[]{:S(2)}, u32[]{:S(2)}) %collective-permute-start.41) | collective-permute-done | bytes 131104 | tf_op jit(solution)/shard_map/ppermute | solution.py:47
  95.0 3.2 %collective-permute-start.44 = (bf16[64,1024]{1,0:T(8,128)(2,1)S(1)}, bf16[64,1024]{1,0:T(8,128)(2,1)S(1)}, u32[]{:S(2)}, u32[]{:S(2)}) collective-permute-start(bf16[64,1024]{1,0:T(8,128)(2,1)S(1)} %get-tuple-element.127.refs_0_), channel_id=1, source_target_pairs={{0,4},{2,6},{4,0},{6,2},{1,5},{3,7},{5,1},{7,3},{8,12},{10,14},{12... | collective-permute-start | bytes 393224 | tf_op jit(solution)/shard_map/ppermute | solution.py:47
  98.3 5.5 %collective-permute-done.44.refs_2_ = bf16[64,1024]{1,0:T(8,128)(2,1)S(1)} collective-permute-done((bf16[64,1024]{1,0:T(8,128)(2,1)S(1)}, bf16[64,1024]{1,0:T(8,128)(2,1)S(1)}, u32[]{:S(2)}, u32[]{:S(2)}) %collective-permute-start.44) | collective-permute-done | bytes 131104 | tf_op jit(solution)/shard_map/ppermute | solution.py:47
  106.8 1.9 %collective-permute-done.45.refs_3_ = bf16[64,1024]{1,0:T(8,128)(2,1)S(1)} collective-permute-done((bf16[64,1024]{1,0:T(8,128)(2,1)S(1)}, bf16[64,1024]{1,0:T(8,128)(2,1)S(1)}, u32[]{:S(2)}, u32[]{:S(2)}) %collective-permute-start.45) | collective-permute-done | bytes 131104 | tf_op jit(solution)/shard_map/ppermute | solution.py:47
  108.7 2.0 %shard_map.300 = (f32[3,144,1024]{2,1,0:T(8,128)S(1)}, bf16[3,144,512]{2,1,0:T(8,128)(2,1)S(1)}, bf16[3,144,512]{2,1,0:T(8,128)(2,1)S(1)}, bf16[3,144,512]{2,1,0...) custom-call(bf16[256,1024]{1,0:T(8,128)(2,1)S(1)} %get-tuple-element, ...), custom_call_target="tpu_custom_call" | custom-call | flops 1811939328 | bytes 8290304 | tf_op jit(solution)/shard_map/pallas_call | solution.py:105
  110.8 2.1 %collective-permute-start.59 = (bf16[3,144,512]{2,1,0:T(8,128)(2,1)S(1)}, bf16[3,144,512]{2,1,0:T(8,128)(2,1)S(1)}, u32[]{:S(2)}, u32[]{:S(2)}) collective-permute-start(bf16[3,144,512]{2,1,0:T(8,128)(2,1)S(1)} %get-tuple-element.158), channel_id=1, source_target_pairs={{0,8},{8,0},{16,24},{24,16},{1,9},{9,1},{17,25},{25,17},{2,10},{10... | collective-permute-start | bytes 1327112 | tf_op jit(solution)/shard_map/ppermute | solution.py:47
  113.8 2.1 %shard_map.294 = (bf16[512,1024]{1,0:T(8,128)(2,1)S(1)}, bf16[512,384]{1,0:T(8,128)(2,1)S(1)}, f32[264,1024]{1,0:T(8,128)S(1)}, bf16[272,1024]{1,0:T(8,128)(2,1)S(1)}) custom-call(bf16[64,1024]{1,0:T(8,128)(2,1)S(1)} %get-tuple-element.127.refs_0_, bf16[64,1024]{1,0:T(8,128)(2,1)S(1)} %collective-permute-done.43.refs_1_, ...), custom_call_target="tpu_custom_call" | custom-call | flops 536870912 | bytes 7026176 | tf_op jit(solution)/shard_map/pallas_call | solution.py:105
  117.5 6.4 %collective-permute-done.59.refs_1_ = bf16[3,144,512]{2,1,0:T(8,128)(2,1)S(1)} collective-permute-done((bf16[3,144,512]{2,1,0:T(8,128)(2,1)S(1)}, bf16[3,144,512]{2,1,0:T(8,128)(2,1)S(1)}, u32[]{:S(2)}, u32[]{:S(2)}) %collective-permute-start.59) | collective-permute-done | bytes 442400 | tf_op jit(solution)/shard_map/ppermute | solution.py:47
  124.8 1.1 collective-permute-done.60.refs_3_
  127.1 6.1 %collective-permute-done.58.refs_1_ = bf16[3,144,512]{2,1,0:T(8,128)(2,1)S(1)} collective-permute-done((bf16[3,144,512]{2,1,0:T(8,128)(2,1)S(1)}, bf16[3,144,512]{2,1,0:T(8,128)(2,1)S(1)}, u32[]{:S(2)}, u32[]{:S(2)}) %collective-permute-start.58) | collective-permute-done | bytes 442400 | tf_op jit(solution)/shard_map/ppermute | solution.py:47
  133.2 1.7 collective-permute-start.62
  135.4 1.4 collective-permute-start.37
  137.0 1.7 collective-permute-start.51
  138.6 5.7 %collective-permute-done.35.refs_1_ = bf16[64,1024]{1,0:T(8,128)(2,1)S(1)} collective-permute-done((bf16[64,1024]{1,0:T(8,128)(2,1)S(1)}, bf16[64,1024]{1,0:T(8,128)(2,1)S(1)}, u32[]{:S(2)}, u32[]{:S(2)}) %collective-permute-start.35) | collective-permute-done | bytes 131104 | tf_op jit(solution)/shard_map/ppermute | solution.py:47
  144.3 3.3 %collective-permute-start.53 = (bf16[72,1024]{1,0:T(8,128)(2,1)S(1)}, bf16[72,1024]{1,0:T(8,128)(2,1)S(1)}, u32[]{:S(2)}, u32[]{:S(2)}) collective-permute-start(bf16[72,1024]{1,0:T(8,128)(2,1)S(1)} %get-tuple-element.138), channel_id=1, source_target_pairs={{0,6},{2,4},{4,2},{6,0},{1,7},{3,5},{5,3},{7,1},{8,14},{10,12},{12... | collective-permute-start | bytes 442376 | tf_op jit(solution)/shard_map/ppermute | solution.py:47
  148.7 6.5 %collective-permute-done.52.refs_2_ = bf16[72,1024]{1,0:T(8,128)(2,1)S(1)} collective-permute-done((bf16[72,1024]{1,0:T(8,128)(2,1)S(1)}, bf16[72,1024]{1,0:T(8,128)(2,1)S(1)}, u32[]{:S(2)}, u32[]{:S(2)}) %collective-permute-start.52) | collective-permute-done | bytes 147488 | tf_op jit(solution)/shard_map/ppermute | solution.py:47
  158.2 1.1 collective-permute-done.38.other_ref
  159.3 1.4 collective-permute-start.64
  161.7 3.0 %collective-permute-done.56.refs_2_ = bf16[4,32,1024]{2,1,0:T(8,128)(2,1)S(1)} collective-permute-done((bf16[4,32,1024]{2,1,0:T(8,128)(2,1)S(1)}, bf16[4,32,1024]{2,1,0:T(8,128)(2,1)S(1)}, u32[]{:S(2)}, u32[]{:S(2)}) %collective-permute-start.56) | collective-permute-done | bytes 262176 | tf_op jit(solution)/shard_map/ppermute | solution.py:47
  165.8 4.5 %shard_map.302 = (f32[3,144,1024]{2,1,0:T(8,128)}, f32[3,144,1024]{2,1,0:T(8,128)}, f32[3,144,1024]{2,1,0:T(8,128)}, f32[3,144,1024]{2,1,0:T(8,128)}) custom-call(f32[3,144,1024]{2,1,0:T(8,128)S(1)} %get-tuple-element.155.refs_0_, bf16[3,144,512]{2,1,0:T(8,128)(2,1)S(1)} %collective-permute-done.58.refs_1_, ...), custom_call_target="tpu_custom_call" | custom-call | bytes 15925248 | tf_op jit(solution)/shard_map/pallas_call | solution.py:105
  171.1 2.3 %shard_map.299 = (f32[32,4,1024]{2,1,0:T(4,128)}, f32[32,4,1024]{2,1,0:T(4,128)}, f32[32,4,1024]{2,1,0:T(4,128)}, f32[32,4,1024]{2,1,0:T(4,128)}) custom-call(f32[4,32,1024]{2,1,0:T(8,128)S(1)} %get-tuple-element.144.refs_0_, bf16[4,32,1024]{2,1,0:T(8,128)(2,1)S(1)} %collective-permute-done.55.refs_1_, ...), custom_call_target="tpu_custom_call" | custom-call | bytes 4980736 | tf_op jit(solution)/shard_map/pallas_call | solution.py:105
  (147 shorter events, 29.3 us)
Async XLA Ops:
  1.8 10.5 %collective-permute-start.1 = (bf16[64,1024]{1,0:T(8,128)(2,1)S(1)}, bf16[64,1024]{1,0:T(8,128)(2,1)S(1)}, u32[]{:S(2)}, u32[]{:S(2)}) collective-permute-start(bf16[64,1024]{1,0:T(8,128)(2,1)S(1)} %shard_map.277.refs_0_.refs_4_), channel_id=1, source_target_pairs={{0,4},{2,6},{4,0},{6,2},{1,5},{3,7},{5,1},{7,3},{8,12},{10,14},{12... | collective-permute-start | bytes 393224 | tf_op jit(solution)/shard_map/ppermute | solution.py:47
  5.9 7.0 %collective-permute-start = (bf16[64,1024]{1,0:T(8,128)(2,1)S(1)}, bf16[64,1024]{1,0:T(8,128)(2,1)S(1)}, u32[]{:S(2)}, u32[]{:S(2)}) collective-permute-start(bf16[64,1024]{1,0:T(8,128)(2,1)S(1)} %shard_map.277.refs_0_.refs_4_), channel_id=1, source_target_pairs={{0,2},{2,0},{4,6},{6,4},{1,3},{3,1},{5,7},{7,5},{8,10},{10,8},{12,... | collective-permute-start | bytes 393224 | tf_op jit(solution)/shard_map/ppermute | solution.py:47
  7.5 7.9 %collective-permute-start.3 = (bf16[64,1024]{1,0:T(8,128)(2,1)S(1)}, bf16[64,1024]{1,0:T(8,128)(2,1)S(1)}, u32[]{:S(2)}, u32[]{:S(2)}) collective-permute-start(bf16[64,1024]{1,0:T(8,128)(2,1)S(1)} %shard_map.277.refs_0_.refs_4_), channel_id=1, source_target_pairs={{0,1},{1,0},{2,3},{3,2},{4,5},{5,4},{6,7},{7,6},{8,9},{9,8},{10,11... | collective-permute-start | bytes 393224 | tf_op jit(solution)/shard_map/ppermute | solution.py:47
  9.0 9.8 %collective-permute-start.7 = (bf16[4,32,1024]{2,1,0:T(8,128)(2,1)S(1)}, bf16[4,32,1024]{2,1,0:T(8,128)(2,1)S(1)}, u32[]{:S(2)}, u32[]{:S(2)}) collective-permute-start(bf16[4,32,1024]{2,1,0:T(8,128)(2,1)S(1)} %shard_map.278.refs_8_), channel_id=1, source_target_pairs={{0,8},{8,0},{16,24},{24,16},{1,9},{9,1},{17,25},{25,17},{2,10},{10... | collective-permute-start | bytes 786440 | tf_op jit(solution)/shard_map/ppermute | solution.py:47
  10.6 14.1 %collective-permute-start.8 = (bf16[4,32,1024]{2,1,0:T(8,128)(2,1)S(1)}, bf16[4,32,1024]{2,1,0:T(8,128)(2,1)S(1)}, u32[]{:S(2)}, u32[]{:S(2)}) collective-permute-start(bf16[4,32,1024]{2,1,0:T(8,128)(2,1)S(1)} %shard_map.278.refs_8_), channel_id=1, source_target_pairs={{0,16},{8,24},{16,0},{24,8},{1,17},{9,25},{17,1},{25,9},{2,18},{10... | collective-permute-start | bytes 786440 | tf_op jit(solution)/shard_map/ppermute | solution.py:47
  12.9 11.7 %collective-permute-start.9 = (bf16[4,32,1024]{2,1,0:T(8,128)(2,1)S(1)}, bf16[4,32,1024]{2,1,0:T(8,128)(2,1)S(1)}, u32[]{:S(2)}, u32[]{:S(2)}) collective-permute-start(bf16[4,32,1024]{2,1,0:T(8,128)(2,1)S(1)} %shard_map.278.refs_8_), channel_id=1, source_target_pairs={{0,24},{8,16},{16,8},{24,0},{1,25},{9,17},{17,9},{25,1},{2,26},{10... | collective-permute-start | bytes 786440 | tf_op jit(solution)/shard_map/ppermute | solution.py:47
  17.5 7.2 %collective-permute-start.6 = (bf16[64,1024]{1,0:T(8,128)(2,1)S(1)}, bf16[64,1024]{1,0:T(8,128)(2,1)S(1)}, u32[]{:S(2)}, u32[]{:S(2)}) collective-permute-start(bf16[64,1024]{1,0:T(8,128)(2,1)S(1)} %collective-permute-done.2.refs_3_), channel_id=1, source_target_pairs={{0,1},{1,0},{2,3},{3,2},{4,5},{5,4},{6,7},{7,6},{8,9},{9,8},{10,11... | collective-permute-start | bytes 393224 | tf_op jit(solution)/shard_map/ppermute | solution.py:47
  28.4 11.7 %collective-permute-start.10 = (bf16[256,1024]{1,0:T(8,128)(2,1)S(1)}, bf16[256,1024]{1,0:T(8,128)(2,1)S(1)}, u32[]{:S(2)}, u32[]{:S(2)}) collective-permute-start(bf16[256,1024]{1,0:T(8,128)(2,1)S(1)} %get-tuple-element.100), channel_id=1, source_target_pairs={{0,1},{1,0},{2,3},{3,2},{4,5},{5,4},{6,7},{7,6},{8,9},{9,8},{10,11... | collective-permute-start | bytes 1572872 | tf_op jit(solution)/shard_map/ppermute | solution.py:47
  29.1 19.4 %collective-permute-start.25 = (bf16[3,144,512]{2,1,0:T(8,128)(2,1)S(1)}, bf16[3,144,512]{2,1,0:T(8,128)(2,1)S(1)}, u32[]{:S(2)}, u32[]{:S(2)}) collective-permute-start(bf16[3,144,512]{2,1,0:T(8,128)(2,1)S(1)} %get-tuple-element.107.refs_9_), channel_id=1, source_target_pairs={{0,8},{8,0},{16,24},{24,16},{1,9},{9,1},{17,25},{25,17},{2,10},{10... | collective-permute-start | bytes 1327112 | tf_op jit(solution)/shard_map/ppermute | solution.py:47
  30.4 18.6 %collective-permute-start.26 = (bf16[3,144,512]{2,1,0:T(8,128)(2,1)S(1)}, bf16[3,144,512]{2,1,0:T(8,128)(2,1)S(1)}, u32[]{:S(2)}, u32[]{:S(2)}) collective-permute-start(bf16[3,144,512]{2,1,0:T(8,128)(2,1)S(1)} %get-tuple-element.106.refs_8_), channel_id=1, source_target_pairs={{0,16},{8,24},{16,0},{24,8},{1,17},{9,25},{17,1},{25,9},{2,18},{10... | collective-permute-start | bytes 1327112 | tf_op jit(solution)/shard_map/ppermute | solution.py:47
  31.2 8.8 %collective-permute-start.18 = (bf16[64,1024]{1,0:T(8,128)(2,1)S(1)}, bf16[64,1024]{1,0:T(8,128)(2,1)S(1)}, u32[]{:S(2)}, u32[]{:S(2)}) collective-permute-start(bf16[64,1024]{1,0:T(8,128)(2,1)S(1)} %shard_map.282.refs_0_.refs_6_), channel_id=1, source_target_pairs={{0,4},{2,6},{4,0},{6,2},{1,5},{3,7},{5,1},{7,3},{8,12},{10,14},{12... | collective-permute-start | bytes 393224 | tf_op jit(solution)/shard_map/ppermute | solution.py:47
  45.0 6.4 %collective-permute-start.11 = (bf16[64,1024]{1,0:T(8,128)(2,1)S(1)}, bf16[64,1024]{1,0:T(8,128)(2,1)S(1)}, u32[]{:S(2)}, u32[]{:S(2)}) collective-permute-start(bf16[64,1024]{1,0:T(8,128)(2,1)S(1)} %get-tuple-element.102), channel_id=1, source_target_pairs={{0,2},{2,0},{4,6},{6,4},{1,3},{3,1},{5,7},{7,5},{8,10},{10,8},{12,... | collective-permute-start | bytes 393224 | tf_op jit(solution)/shard_map/ppermute | solution.py:47
  45.0 16.4 %collective-permute-start.24 = (bf16[3,144,512]{2,1,0:T(8,128)(2,1)S(1)}, bf16[3,144,512]{2,1,0:T(8,128)(2,1)S(1)}, u32[]{:S(2)}, u32[]{:S(2)}) collective-permute-start(bf16[3,144,512]{2,1,0:T(8,128)(2,1)S(1)} %get-tuple-element.106.refs_8_), channel_id=1, source_target_pairs={{0,8},{8,0},{16,24},{24,16},{1,9},{9,1},{17,25},{25,17},{2,10},{10... | collective-permute-start | bytes 1327112 | tf_op jit(solution)/shard_map/ppermute | solution.py:47
  46.5 11.5 %collective-permute-start.12 = (bf16[64,1024]{1,0:T(8,128)(2,1)S(1)}, bf16[64,1024]{1,0:T(8,128)(2,1)S(1)}, u32[]{:S(2)}, u32[]{:S(2)}) collective-permute-start(bf16[64,1024]{1,0:T(8,128)(2,1)S(1)} %get-tuple-element.103), channel_id=1, source_target_pairs={{0,4},{2,6},{4,0},{6,2},{1,5},{3,7},{5,1},{7,3},{8,12},{10,14},{12... | collective-permute-start | bytes 393224 | tf_op jit(solution)/shard_map/ppermute | solution.py:47
  48.5 19.8 %collective-permute-start.27 = (bf16[3,144,512]{2,1,0:T(8,128)(2,1)S(1)}, bf16[3,144,512]{2,1,0:T(8,128)(2,1)S(1)}, u32[]{:S(2)}, u32[]{:S(2)}) collective-permute-start(bf16[3,144,512]{2,1,0:T(8,128)(2,1)S(1)} %get-tuple-element.107.refs_9_), channel_id=1, source_target_pairs={{0,16},{8,24},{16,0},{24,8},{1,17},{9,25},{17,1},{25,9},{2,18},{10... | collective-permute-start | bytes 1327112 | tf_op jit(solution)/shard_map/ppermute | solution.py:47
  49.1 8.9 %collective-permute-start.13 = (bf16[64,1024]{1,0:T(8,128)(2,1)S(1)}, bf16[64,1024]{1,0:T(8,128)(2,1)S(1)}, u32[]{:S(2)}, u32[]{:S(2)}) collective-permute-start(bf16[64,1024]{1,0:T(8,128)(2,1)S(1)} %get-tuple-element.104), channel_id=1, source_target_pairs={{0,6},{2,4},{4,2},{6,0},{1,7},{3,5},{5,3},{7,1},{8,14},{10,12},{12... | collective-permute-start | bytes 393224 | tf_op jit(solution)/shard_map/ppermute | solution.py:47
  51.4 17.0 %collective-permute-start.28 = (bf16[3,144,512]{2,1,0:T(8,128)(2,1)S(1)}, bf16[3,144,512]{2,1,0:T(8,128)(2,1)S(1)}, u32[]{:S(2)}, u32[]{:S(2)}) collective-permute-start(bf16[3,144,512]{2,1,0:T(8,128)(2,1)S(1)} %collective-permute-done.26.refs_12_), channel_id=1, source_target_pairs={{0,8},{8,0},{16,24},{24,16},{1,9},{9,1},{17,25},{25,17},{2,10},{10... | collective-permute-start | bytes 1327112 | tf_op jit(solution)/shard_map/ppermute | solution.py:47
  58.0 15.8 %collective-permute-start.29 = (bf16[3,144,512]{2,1,0:T(8,128)(2,1)S(1)}, bf16[3,144,512]{2,1,0:T(8,128)(2,1)S(1)}, u32[]{:S(2)}, u32[]{:S(2)}) collective-permute-start(bf16[3,144,512]{2,1,0:T(8,128)(2,1)S(1)} %collective-permute-done.25.refs_11_), channel_id=1, source_target_pairs={{0,16},{8,24},{16,0},{24,8},{1,17},{9,25},{17,1},{25,9},{2,18},{10... | collective-permute-start | bytes 1327112 | tf_op jit(solution)/shard_map/ppermute | solution.py:47
  59.3 9.0 %collective-permute-start.15 = (bf16[64,1024]{1,0:T(8,128)(2,1)S(1)}, bf16[64,1024]{1,0:T(8,128)(2,1)S(1)}, u32[]{:S(2)}, u32[]{:S(2)}) collective-permute-start(bf16[64,1024]{1,0:T(8,128)(2,1)S(1)} %get-tuple-element.105.refs_0_), channel_id=1, source_target_pairs={{0,4},{2,6},{4,0},{6,2},{1,5},{3,7},{5,1},{7,3},{8,12},{10,14},{12... | collective-permute-start | bytes 393224 | tf_op jit(solution)/shard_map/ppermute | solution.py:47
  61.4 7.5 %collective-permute-start.14 = (bf16[64,1024]{1,0:T(8,128)(2,1)S(1)}, bf16[64,1024]{1,0:T(8,128)(2,1)S(1)}, u32[]{:S(2)}, u32[]{:S(2)}) collective-permute-start(bf16[64,1024]{1,0:T(8,128)(2,1)S(1)} %get-tuple-element.105.refs_0_), channel_id=1, source_target_pairs={{0,2},{2,0},{4,6},{6,4},{1,3},{3,1},{5,7},{7,5},{8,10},{10,8},{12,... | collective-permute-start | bytes 393224 | tf_op jit(solution)/shard_map/ppermute | solution.py:47
  81.5 7.9 %collective-permute-start.40 = (bf16[64,1024]{1,0:T(8,128)(2,1)S(1)}, bf16[64,1024]{1,0:T(8,128)(2,1)S(1)}, u32[]{:S(2)}, u32[]{:S(2)}) collective-permute-start(bf16[64,1024]{1,0:T(8,128)(2,1)S(1)} %get-tuple-element.123), channel_id=1, source_target_pairs={{0,2},{2,0},{4,6},{6,4},{1,3},{3,1},{5,7},{7,5},{8,10},{10,8},{12,... | collective-permute-start | bytes 393224 | tf_op jit(solution)/shard_map/ppermute | solution.py:47
  81.9 12.9 %collective-permute-start.41 = (bf16[64,1024]{1,0:T(8,128)(2,1)S(1)}, bf16[64,1024]{1,0:T(8,128)(2,1)S(1)}, u32[]{:S(2)}, u32[]{:S(2)}) collective-permute-start(bf16[64,1024]{1,0:T(8,128)(2,1)S(1)} %get-tuple-element.124), channel_id=1, source_target_pairs={{0,4},{2,6},{4,0},{6,2},{1,5},{3,7},{5,1},{7,3},{8,12},{10,14},{12... | collective-permute-start | bytes 393224 | tf_op jit(solution)/shard_map/ppermute | solution.py:47
  84.3 10.6 %collective-permute-start.42 = (bf16[64,1024]{1,0:T(8,128)(2,1)S(1)}, bf16[64,1024]{1,0:T(8,128)(2,1)S(1)}, u32[]{:S(2)}, u32[]{:S(2)}) collective-permute-start(bf16[64,1024]{1,0:T(8,128)(2,1)S(1)} %get-tuple-element.125), channel_id=1, source_target_pairs={{0,6},{2,4},{4,2},{6,0},{1,7},{3,5},{5,3},{7,1},{8,14},{10,12},{12... | collective-permute-start | bytes 393224 | tf_op jit(solution)/shard_map/ppermute | solution.py:47
  95.0 8.7 %collective-permute-start.44 = (bf16[64,1024]{1,0:T(8,128)(2,1)S(1)}, bf16[64,1024]{1,0:T(8,128)(2,1)S(1)}, u32[]{:S(2)}, u32[]{:S(2)}) collective-permute-start(bf16[64,1024]{1,0:T(8,128)(2,1)S(1)} %get-tuple-element.127.refs_0_), channel_id=1, source_target_pairs={{0,4},{2,6},{4,0},{6,2},{1,5},{3,7},{5,1},{7,3},{8,12},{10,14},{12... | collective-permute-start | bytes 393224 | tf_op jit(solution)/shard_map/ppermute | solution.py:47
  98.3 8.1 %collective-permute-start.43 = (bf16[64,1024]{1,0:T(8,128)(2,1)S(1)}, bf16[64,1024]{1,0:T(8,128)(2,1)S(1)}, u32[]{:S(2)}, u32[]{:S(2)}) collective-permute-start(bf16[64,1024]{1,0:T(8,128)(2,1)S(1)} %get-tuple-element.127.refs_0_), channel_id=1, source_target_pairs={{0,2},{2,0},{4,6},{6,4},{1,3},{3,1},{5,7},{7,5},{8,10},{10,8},{12,... | collective-permute-start | bytes 393224 | tf_op jit(solution)/shard_map/ppermute | solution.py:47
  105.7 11.0 %collective-permute-start.34 = (bf16[256,1024]{1,0:T(8,128)(2,1)S(1)}, bf16[256,1024]{1,0:T(8,128)(2,1)S(1)}, u32[]{:S(2)}, u32[]{:S(2)}) collective-permute-start(bf16[256,1024]{1,0:T(8,128)(2,1)S(1)} %get-tuple-element.114), channel_id=1, source_target_pairs={{0,1},{1,0},{2,3},{3,2},{4,5},{5,4},{6,7},{7,6},{8,9},{9,8},{10,11... | collective-permute-start | bytes 1572872 | tf_op jit(solution)/shard_map/ppermute | solution.py:47
  106.3 7.6 %collective-permute-start.48 = (bf16[64,1024]{1,0:T(8,128)(2,1)S(1)}, bf16[64,1024]{1,0:T(8,128)(2,1)S(1)}, u32[]{:S(2)}, u32[]{:S(2)}) collective-permute-start(bf16[64,1024]{1,0:T(8,128)(2,1)S(1)} %collective-permute-done.44.refs_2_), channel_id=1, source_target_pairs={{0,1},{1,0},{2,3},{3,2},{4,5},{5,4},{6,7},{7,6},{8,9},{9,8},{10,11... | collective-permute-start | bytes 393224 | tf_op jit(solution)/shard_map/ppermute | solution.py:47
  106.3 6.6 %collective-permute-start.47 = (bf16[64,1024]{1,0:T(8,128)(2,1)S(1)}, bf16[64,1024]{1,0:T(8,128)(2,1)S(1)}, u32[]{:S(2)}, u32[]{:S(2)}) collective-permute-start(bf16[64,1024]{1,0:T(8,128)(2,1)S(1)} %collective-permute-done.43.refs_1_), channel_id=1, source_target_pairs={{0,1},{1,0},{2,3},{3,2},{4,5},{5,4},{6,7},{7,6},{8,9},{9,8},{10,11... | collective-permute-start | bytes 393224 | tf_op jit(solution)/shard_map/ppermute | solution.py:47
  110.8 13.2 %collective-permute-start.59 = (bf16[3,144,512]{2,1,0:T(8,128)(2,1)S(1)}, bf16[3,144,512]{2,1,0:T(8,128)(2,1)S(1)}, u32[]{:S(2)}, u32[]{:S(2)}) collective-permute-start(bf16[3,144,512]{2,1,0:T(8,128)(2,1)S(1)} %get-tuple-element.158), channel_id=1, source_target_pairs={{0,8},{8,0},{16,24},{24,16},{1,9},{9,1},{17,25},{25,17},{2,10},{10... | collective-permute-start | bytes 1327112 | tf_op jit(solution)/shard_map/ppermute | solution.py:47
  112.9 13.0 %collective-permute-start.60 = (bf16[3,144,512]{2,1,0:T(8,128)(2,1)S(1)}, bf16[3,144,512]{2,1,0:T(8,128)(2,1)S(1)}, u32[]{:S(2)}, u32[]{:S(2)}) collective-permute-start(bf16[3,144,512]{2,1,0:T(8,128)(2,1)S(1)} %get-tuple-element.160), channel_id=1, source_target_pairs={{0,16},{8,24},{16,0},{24,8},{1,17},{9,25},{17,1},{25,9},{2,18},{10... | collective-permute-start | bytes 1327112 | tf_op jit(solution)/shard_map/ppermute | solution.py:47
  115.9 19.5 %collective-permute-start.50 = (bf16[272,1024]{1,0:T(8,128)(2,1)S(1)}, bf16[272,1024]{1,0:T(8,128)(2,1)S(1)}, u32[]{:S(2)}, u32[]{:S(2)}) collective-permute-start(bf16[272,1024]{1,0:T(8,128)(2,1)S(1)} %get-tuple-element.134), channel_id=1, source_target_pairs={{0,1},{1,0},{2,3},{3,2},{4,5},{5,4},{6,7},{7,6},{8,9},{9,8},{10,11... | collective-permute-start | bytes 1671176 | tf_op jit(solution)/shard_map/ppermute | solution.py:47
  116.0 17.2 %collective-permute-start.58 = (bf16[3,144,512]{2,1,0:T(8,128)(2,1)S(1)}, bf16[3,144,512]{2,1,0:T(8,128)(2,1)S(1)}, u32[]{:S(2)}, u32[]{:S(2)}) collective-permute-start(bf16[3,144,512]{2,1,0:T(8,128)(2,1)S(1)} %get-tuple-element.156), channel_id=1, source_target_pairs={{0,8},{8,0},{16,24},{24,16},{1,9},{9,1},{17,25},{25,17},{2,10},{10... | collective-permute-start | bytes 1327112 | tf_op jit(solution)/shard_map/ppermute | solution.py:47
  116.7 20.3 %collective-permute-start.63 = (bf16[3,144,512]{2,1,0:T(8,128)(2,1)S(1)}, bf16[3,144,512]{2,1,0:T(8,128)(2,1)S(1)}, u32[]{:S(2)}, u32[]{:S(2)}) collective-permute-start(bf16[3,144,512]{2,1,0:T(8,128)(2,1)S(1)} %get-tuple-element.163), channel_id=1, source_target_pairs={{0,16},{8,24},{16,0},{24,8},{1,17},{9,25},{17,1},{25,9},{2,18},{10... | collective-permute-start | bytes 1327112 | tf_op jit(solution)/shard_map/ppermute | solution.py:47
  123.9 11.0 %collective-permute-start.36 = (bf16[64,1024]{1,0:T(8,128)(2,1)S(1)}, bf16[64,1024]{1,0:T(8,128)(2,1)S(1)}, u32[]{:S(2)}, u32[]{:S(2)}) collective-permute-start(bf16[64,1024]{1,0:T(8,128)(2,1)S(1)} %get-tuple-element.118), channel_id=1, source_target_pairs={{0,2},{2,0},{4,6},{6,4},{1,3},{3,1},{5,7},{7,5},{8,10},{10,8},{12,... | collective-permute-start | bytes 393224 | tf_op jit(solution)/shard_map/ppermute | solution.py:47
  126.2 31.3 %collective-permute-start.61 = (bf16[3,144,512]{2,1,0:T(8,128)(2,1)S(1)}, bf16[3,144,512]{2,1,0:T(8,128)(2,1)S(1)}, u32[]{:S(2)}, u32[]{:S(2)}) collective-permute-start(bf16[3,144,512]{2,1,0:T(8,128)(2,1)S(1)} %get-tuple-element.161), channel_id=1, source_target_pairs={{0,16},{8,24},{16,0},{24,8},{1,17},{9,25},{17,1},{25,9},{2,18},{10... | collective-permute-start | bytes 1327112 | tf_op jit(solution)/shard_map/ppermute | solution.py:47
  133.2 24.4 %collective-permute-start.62 = (bf16[3,144,512]{2,1,0:T(8,128)(2,1)S(1)}, bf16[3,144,512]{2,1,0:T(8,128)(2,1)S(1)}, u32[]{:S(2)}, u32[]{:S(2)}) collective-permute-start(bf16[3,144,512]{2,1,0:T(8,128)(2,1)S(1)} %get-tuple-element.162), channel_id=1, source_target_pairs={{0,8},{8,0},{16,24},{24,16},{1,9},{9,1},{17,25},{25,17},{2,10},{10... | collective-permute-start | bytes 1327112 | tf_op jit(solution)/shard_map/ppermute | solution.py:47
  135.0 9.3 %collective-permute-start.35 = (bf16[64,1024]{1,0:T(8,128)(2,1)S(1)}, bf16[64,1024]{1,0:T(8,128)(2,1)S(1)}, u32[]{:S(2)}, u32[]{:S(2)}) collective-permute-start(bf16[64,1024]{1,0:T(8,128)(2,1)S(1)} %get-tuple-element.116), channel_id=1, source_target_pairs={{0,2},{2,0},{4,6},{6,4},{1,3},{3,1},{5,7},{7,5},{8,10},{10,8},{12,... | collective-permute-start | bytes 393224 | tf_op jit(solution)/shard_map/ppermute | solution.py:47
  135.4 8.9 %collective-permute-start.37 = (bf16[64,1024]{1,0:T(8,128)(2,1)S(1)}, bf16[64,1024]{1,0:T(8,128)(2,1)S(1)}, u32[]{:S(2)}, u32[]{:S(2)}) collective-permute-start(bf16[64,1024]{1,0:T(8,128)(2,1)S(1)} %shard_map.289), channel_id=1, source_target_pairs={{0,4},{2,6},{4,0},{6,2},{1,5},{3,7},{5,1},{7,3},{8,12},{10,14},{12... | collective-permute-start | bytes 393224 | tf_op jit(solution)/shard_map/ppermute | solution.py:47
  137.0 11.4 %collective-permute-start.51 = (bf16[72,1024]{1,0:T(8,128)(2,1)S(1)}, bf16[72,1024]{1,0:T(8,128)(2,1)S(1)}, u32[]{:S(2)}, u32[]{:S(2)}) collective-permute-start(bf16[72,1024]{1,0:T(8,128)(2,1)S(1)} %get-tuple-element.136), channel_id=1, source_target_pairs={{0,2},{2,0},{4,6},{6,4},{1,3},{3,1},{5,7},{7,5},{8,10},{10,8},{12,... | collective-permute-start | bytes 442376 | tf_op jit(solution)/shard_map/ppermute | solution.py:47
  144.3 10.9 %collective-permute-start.52 = (bf16[72,1024]{1,0:T(8,128)(2,1)S(1)}, bf16[72,1024]{1,0:T(8,128)(2,1)S(1)}, u32[]{:S(2)}, u32[]{:S(2)}) collective-permute-start(bf16[72,1024]{1,0:T(8,128)(2,1)S(1)} %get-tuple-element.137), channel_id=1, source_target_pairs={{0,4},{2,6},{4,0},{6,2},{1,5},{3,7},{5,1},{7,3},{8,12},{10,14},{12... | collective-permute-start | bytes 442376 | tf_op jit(solution)/shard_map/ppermute | solution.py:47
  144.3 11.9 %collective-permute-start.53 = (bf16[72,1024]{1,0:T(8,128)(2,1)S(1)}, bf16[72,1024]{1,0:T(8,128)(2,1)S(1)}, u32[]{:S(2)}, u32[]{:S(2)}) collective-permute-start(bf16[72,1024]{1,0:T(8,128)(2,1)S(1)} %get-tuple-element.138), channel_id=1, source_target_pairs={{0,6},{2,4},{4,2},{6,0},{1,7},{3,5},{5,3},{7,1},{8,14},{10,12},{12... | collective-permute-start | bytes 442376 | tf_op jit(solution)/shard_map/ppermute | solution.py:47
  148.4 12.3 %collective-permute-start.55 = (bf16[4,32,1024]{2,1,0:T(8,128)(2,1)S(1)}, bf16[4,32,1024]{2,1,0:T(8,128)(2,1)S(1)}, u32[]{:S(2)}, u32[]{:S(2)}) collective-permute-start(bf16[4,32,1024]{2,1,0:T(8,128)(2,1)S(1)} %get-tuple-element.145), channel_id=1, source_target_pairs={{0,8},{8,0},{16,24},{24,16},{1,9},{9,1},{17,25},{25,17},{2,10},{10... | collective-permute-start | bytes 786440 | tf_op jit(solution)/shard_map/ppermute | solution.py:47
  155.2 9.5 %collective-permute-start.56 = (bf16[4,32,1024]{2,1,0:T(8,128)(2,1)S(1)}, bf16[4,32,1024]{2,1,0:T(8,128)(2,1)S(1)}, u32[]{:S(2)}, u32[]{:S(2)}) collective-permute-start(bf16[4,32,1024]{2,1,0:T(8,128)(2,1)S(1)} %get-tuple-element.146), channel_id=1, source_target_pairs={{0,16},{8,24},{16,0},{24,8},{1,17},{9,25},{17,1},{25,9},{2,18},{10... | collective-permute-start | bytes 786440 | tf_op jit(solution)/shard_map/ppermute | solution.py:47
  156.2 14.9 %collective-permute-start.57 = (bf16[4,32,1024]{2,1,0:T(8,128)(2,1)S(1)}, bf16[4,32,1024]{2,1,0:T(8,128)(2,1)S(1)}, u32[]{:S(2)}, u32[]{:S(2)}) collective-permute-start(bf16[4,32,1024]{2,1,0:T(8,128)(2,1)S(1)} %get-tuple-element.147), channel_id=1, source_target_pairs={{0,24},{8,16},{16,8},{24,0},{1,25},{9,17},{17,9},{25,1},{2,26},{10... | collective-permute-start | bytes 786440 | tf_op jit(solution)/shard_map/ppermute | solution.py:47
  157.5 16.7 %collective-permute-start.54 = (f32[64,1024]{1,0:T(8,128)S(1)}, f32[64,1024]{1,0:T(8,128)S(1)}, u32[]{:S(2)}, u32[]{:S(2)}) collective-permute-start(f32[64,1024]{1,0:T(8,128)S(1)} %get-tuple-element.140.mine_ref), channel_id=1, source_target_pairs={{0,1},{1,0},{2,3},{3,2},{4,5},{5,4},{6,7},{7,6},{8,9},{9,8},{10,11... | collective-permute-start | bytes 786440 | tf_op jit(solution)/shard_map/ppermute | solution.py:47
  159.3 14.2 %collective-permute-start.64 = (f32[8,1024]{1,0:T(8,128)S(1)}, f32[8,1024]{1,0:T(8,128)S(1)}, u32[]{:S(2)}, u32[]{:S(2)}) collective-permute-start(f32[8,1024]{1,0:T(8,128)S(1)} %get-tuple-element.165.refs_0_), channel_id=1, source_target_pairs={{0,8},{8,0},{16,24},{24,16},{1,9},{9,1},{17,25},{25,17},{2,10},{10... | collective-permute-start | bytes 98312 | tf_op jit(solution)/shard_map/ppermute | solution.py:47
  160.7 12.7 %collective-permute-start.65 = (f32[8,1024]{1,0:T(8,128)S(1)}, f32[8,1024]{1,0:T(8,128)S(1)}, u32[]{:S(2)}, u32[]{:S(2)}) collective-permute-start(f32[8,1024]{1,0:T(8,128)S(1)} %get-tuple-element.165.refs_0_), channel_id=1, source_target_pairs={{0,16},{8,24},{16,0},{24,8},{1,17},{9,25},{17,1},{25,9},{2,18},{10... | collective-permute-start | bytes 98312 | tf_op jit(solution)/shard_map/ppermute | solution.py:47
  164.7 8.7 %collective-permute-start.66 = (f32[8,1024]{1,0:T(8,128)S(1)}, f32[8,1024]{1,0:T(8,128)S(1)}, u32[]{:S(2)}, u32[]{:S(2)}) collective-permute-start(f32[8,1024]{1,0:T(8,128)S(1)} %get-tuple-element.165.refs_0_), channel_id=1, source_target_pairs={{0,24},{8,16},{16,8},{24,0},{1,25},{9,17},{17,9},{25,1},{2,26},{10... | collective-permute-start | bytes 98312 | tf_op jit(solution)/shard_map/ppermute | solution.py:47
  (36 other events, 213.6 us)
